TPU v7x, 128 devices: a whole 4x4x4 slice. The times are simulated.
128 devices in a mesh: cell: 4 (over z), wide: 32 (over y, x, core).
Axes of the slice: x: 4, y: 4, z: 4, core: 2. Of those that a mesh axis runs over, the one named last changes fastest.
Arguments:
- positions: float32 [3, 4, 256, 128], P(None, 'cell', 'wide'), may hold values from 0 to 1
- rhs: float32 [3, 4, 256, 128], P(None, 'cell', 'wide'), may hold values from -6 to 6
- blob_owner: int32 [4, 256, 128, 1], P('cell', 'wide'), may hold values from 0 to 127; in each aligned block of 1024 rows (0 to 1023, 1024 to 2047, ..., all dimensions but the last counted through in order) at most 32 rows name the same one
- blob_row: int32 [4, 256, 128], P('cell', 'wide'), may hold values from 0 to 31
- blob_arm: float32 [3, 4, 256, 128], P(None, 'cell', 'wide'), may hold values from -1 to 1
- body_inverse: float32 [6, 6, 4096], P(None, None, ('cell', 'wide'))
Outputs:
- blob_forces: float32 [3, 4, 256, 128], P(None, 'cell', 'wide')
- body_motion: float32 [6, 4096], P(None, ('cell', 'wide'))
Inputs may be any that keep to these rules, and one draw needn't show every extreme that they name: `blob_owner`: at most 32 of the blobs of one device have bodies of one owner, and that many in some device.
All inputs are finite; a program needn't handle non-finite values.
Results may differ from a plain program's by a relative error of at most 0.0003.
Values sent between devices are 32-bit elements; how exact they have to be, the bound alone decides.
No kernel may reach another device: no remote copies, remote signals or barrier semaphores. Data moves between devices by JAX's collectives and lax.ppermute only.
A program may use at most 64 MiB of HBM per device.

v0:
```python
import functools
import math

import jax
import jax.numpy as jnp
from jax import lax
from jax.sharding import Mesh
from jax.sharding import PartitionSpec as P

ITERS = 3
WIDE = ("wide_0", "wide_1", "wide_2")
CELL_WIDE = ("cell", "wide_0", "wide_1", "wide_2")


EPS2 = 0.04
KAPPA = 0.3


def with_halo(array, sides, width):
    for axis, dim in sides:
        count, length = (lax.axis_size(axis), array.shape[dim])
        up = [(i, (i + 1) % count) for i in range(count)]
        down = [(j, i) for i, j in up]
        last = lax.slice_in_dim(array, length - width, length, axis=dim)
        first = lax.slice_in_dim(array, 0, width, axis=dim)
        before = lax.ppermute(last, axis, up)
        after = lax.ppermute(first, axis, down)
        array = jnp.concatenate([before, array, after], axis=dim)
    return array


def over_axes(array, axes):
    return functools.reduce(lax.psum, axes, array)


def pair_sum(target, source, forces):
    sep = target[..., :, None] - source[..., None, :]
    dist2 = jnp.sum(sep * sep, axis=0)
    soft = dist2 + EPS2
    inverse = 1.0 / (soft * jnp.sqrt(soft))
    near = (dist2 + 2.0 * EPS2) * inverse
    along = jnp.sum(sep * forces[..., None, :], axis=0)
    return jnp.sum(near[None] * forces[..., None, :] + (inverse * along)[None] * sep, axis=-1)


def local(positions, rhs, blob_owner, blob_row, blob_arm, body_inverse):
    tiles = positions.shape[2]
    tile = positions.shape[3]
    count = 9
    nblob = tiles * tile
    body_dev = body_inverse.shape[2]
    ncell = lax.axis_size("cell")
    nwide = lax.axis_size(WIDE)
    ndev = ncell * nwide
    capacity = 4 * nblob // ndev
    factor = KAPPA / math.sqrt(count * tile)
    extended = with_halo(positions, (("cell", 1), (WIDE, 2)), 1)
    extended = extended.reshape(3, 3 * (tiles + 2), tile)
    target = positions[:, 0]
    column_ids = jnp.arange(tiles, dtype=jnp.int32)
    starts_of = []
    sources = []
    for code in range(count):
        step_x = code // 3 - 1
        step_y = code % 3 - 1
        picks = (1 + step_x) * (tiles + 2) + 1 + step_y + column_ids
        starts_of.append(picks)
        offset = jnp.array([step_x, step_y, 0], jnp.float32)[:, None, None]
        sources.append(jnp.take(extended, picks, axis=1) + offset)
    arms = blob_arm.reshape(3, nblob)
    owners = blob_owner.reshape(nblob)
    rows = blob_row.reshape(nblob)
    order = jnp.argsort(owners, stable=True)
    sorted_owner = owners[order]
    counts = jnp.sum(
        (owners[:, None] == jnp.arange(ndev, dtype=jnp.int32)[None, :]).astype(jnp.int32), axis=0
    )
    starts = jnp.cumsum(counts) - counts
    ranks = jnp.arange(nblob, dtype=jnp.int32) - starts[sorted_owner]
    slots = jnp.zeros((nblob,), jnp.int32).at[order].set(sorted_owner * capacity + ranks)
    id_buffer = jnp.full((ndev * capacity,), -1, jnp.int32).at[slots].set(rows)
    arrived = lax.all_to_all(id_buffer, CELL_WIDE, split_axis=0, concat_axis=0, tiled=True)
    onehot = (arrived[:, None] == jnp.arange(body_dev, dtype=jnp.int32)[None, :]).astype(
        jnp.float32
    )

    def send_out(buffer):
        return lax.all_to_all(buffer, CELL_WIDE, split_axis=1, concat_axis=1, tiled=True)

    def send_back(buffer):
        return lax.all_to_all(buffer, CELL_WIDE, split_axis=1, concat_axis=1, tiled=True)

    def body_motion_of(sums):
        return jnp.einsum("abn,bn->an", body_inverse, sums, precision=lax.Precision.HIGHEST)

    def precondition(field):
        values = field.reshape(3, nblob)
        sent = jnp.concatenate([values, jnp.cross(arms, values, axis=0)], 0)
        buffer = jnp.zeros((6, ndev * capacity), jnp.float32).at[:, slots].set(sent)
        received = send_out(buffer)
        sums = jnp.dot(received, onehot, precision=lax.Precision.HIGHEST)
        motion = body_motion_of(sums)
        per_row = jnp.dot(motion, onehot.T, precision=lax.Precision.HIGHEST)
        returned = send_back(per_row)
        mine = returned[:, slots]
        extra = mine[:3] + jnp.cross(mine[3:], arms, axis=0)
        return (field + extra.reshape(field.shape), motion)

    beta = jnp.sqrt(over_axes(jnp.sum(rhs * rhs), CELL_WIDE))
    basis = [rhs / beta]
    hessen = jnp.zeros((ITERS + 1, ITERS), jnp.float32)
    for column in range(ITERS):
        moved, unused = precondition(basis[column])
        outer = with_halo(moved, (("cell", 1), (WIDE, 2)), 1)
        outer = outer.reshape(3, 3 * (tiles + 2), tile)
        total = jnp.zeros((3, tiles, tile), jnp.float32)
        for mobility_code in range(count):
            total = total + pair_sum(
                target, sources[mobility_code], jnp.take(outer, starts_of[mobility_code], axis=1)
            )
        fresh = moved + factor * total[:, None]
        locals_now = jnp.stack([jnp.sum(basis[row] * fresh) for row in range(column + 1)])
        inners, whole = (
            over_axes(locals_now, CELL_WIDE),
            over_axes(jnp.sum(fresh * fresh), CELL_WIDE),
        )
        for row in range(column + 1):
            fresh = fresh - inners[row] * basis[row]
            hessen = hessen.at[row, column].set(inners[row])
        squared = whole - jnp.sum(inners * inners)
        length = jnp.sqrt(squared)
        hessen = hessen.at[column + 1, column].set(length)
        basis.append(fresh / length)
    normal_matrix = jnp.dot(hessen.T, hessen, precision=lax.Precision.HIGHEST)
    target_side = beta * hessen[0]
    lower = jnp.linalg.cholesky(normal_matrix)
    coeffs = jax.scipy.linalg.cho_solve((lower, True), target_side)
    combined = jnp.zeros_like(rhs)
    for column in range(ITERS):
        combined = combined + coeffs[column] * basis[column]
    blob_forces, body_motion = precondition(combined)
    return (blob_forces, body_motion)


def solution(mesh):
    split = Mesh(
        mesh.devices.reshape(mesh.shape["cell"], 4, 4, 2), ("cell", "wide_0", "wide_1", "wide_2")
    )
    in_specs = (
        P(None, "cell", WIDE, None),
        P(None, "cell", WIDE, None),
        P("cell", WIDE, None, None),
        P("cell", WIDE, None),
        P(None, "cell", WIDE, None),
        P(None, None, CELL_WIDE),
    )
    out_specs = (P(None, "cell", WIDE, None), P(None, CELL_WIDE))
    return jax.shard_map(local, mesh=split, in_specs=in_specs, out_specs=out_specs, check_vma=False)
```

profile of v0, /device:TPU:1, one launch (start us, length us, event | category | flops | bytes accessed | tf_op | source)
XLA Modules:
  0.0 501.5 jit_solution(5258189545581995606)
XLA Ops:
  6.3 5.1 %sort.17 = (s32[1024]{0:T(1024)}, s32[1024]{0:T(1024)S(1)}) sort(s32[1024]{0:T(1024)} %bitcast.303, s32[1024]{0:T(1024)S(1)} %iota.131), dimensions={0}, to_apply=%region_5.6 | sort | flops 10240 | bytes 16384 | tf_op jit(solution)/shard_map/jit(argsort)/sort | solution.py:73
  11.4 4.5 gather_fusion
  16.3 6.6 %gather_fusion.1 = s32[1024]{0:T(1024)S(1)} fusion(s32[128]{0:T(128)S(1)} %sub.95, s32[1024]{0:T(1024)S(1)} %broadcast_clamp_fusion.1), kind=kCustom, calls=%fused_computation.37 | custom fusion | bytes 12288 | tf_op jit(solution)/shard_map/gather | solution.py:79
  22.9 4.3 scatter_custom_fusion
  27.3 4.5 scatter_custom_fusion.2
  32.5 8.9 %all-to-all-start.1 = ((s32[128,32,1]{1,2,0:T(1,128)}), s32[128,32,1]{1,2,0:T(1,128)S(1)}, u32[]{:S(2)}, u32[]{:S(2)}) async-start(s32[128,32,1]{1,2,0:T(1,128)} %bitcast.22), calls=%async_computation.1 | async-start | bytes 131072 | tf_op jit(solution)/shard_map/all_to_all | solution.py:82
  42.1 10.2 %psum.196 = f32[]{:T(128)} all-reduce(f32[]{:T(128)} %multiply_reduce_fusion.13), channel_id=1, replica_groups=mesh['cell'=4,'wide_0'=4,'wide_1'=4,'wide_2'=2] {'cell'}, use_global_device_ids=true, to_apply=%region_1.2 | all-reduce | flops 1 | bytes 8 | tf_op jit(solution)/shard_map/psum | solution.py:33
  52.2 8.9 %psum.197 = f32[]{:T(128)} all-reduce(f32[]{:T(128)} %psum.196), channel_id=1, replica_groups=mesh['cell'=4,'wide_0'=4,'wide_1'=4,'wide_2'=2] {'wide_0'}, use_global_device_ids=true, to_apply=%region_2.3 | all-reduce | flops 1 | bytes 8 | tf_op jit(solution)/shard_map/psum | solution.py:33
  61.1 9.0 %psum.198 = f32[]{:T(128)} all-reduce(f32[]{:T(128)} %psum.197), channel_id=1, replica_groups=mesh['cell'=4,'wide_0'=4,'wide_1'=4,'wide_2'=2] {'wide_1'}, use_global_device_ids=true, to_apply=%region_3.4 | all-reduce | flops 1 | bytes 8 | tf_op jit(solution)/shard_map/psum | solution.py:33
  70.2 9.2 %psum.199 = f32[]{:T(128)} all-reduce(f32[]{:T(128)} %psum.198), channel_id=1, replica_groups=mesh['cell'=4,'wide_0'=4,'wide_1'=4,'wide_2'=2] {'wide_2'}, use_global_device_ids=true, to_apply=%region_4.5 | all-reduce | flops 1 | bytes 8 | tf_op jit(solution)/shard_map/psum | solution.py:33
  88.2 8.9 %all-to-all-start = ((f32[128,1,192]{2,1,0:T(1,128)}), f32[128,1,192]{2,1,0:T(1,128)S(1)}, u32[]{:S(2)}, u32[]{:S(2)}) async-start(f32[128,1,192]{2,1,0:T(1,128)} %reshape.1600), calls=%async_computation | async-start | bytes 262144 | tf_op jit(solution)/shard_map/all_to_all | solution.py:88
  102.5 4.8 all-to-all-done
  111.2 5.1 %all-to-all-start.2 = ((f32[128,1,192]{2,1,0:T(1,128)}), f32[128,1,192]{2,1,0:T(1,128)S(1)}, u32[]{:S(2)}, u32[]{:S(2)}) async-start(f32[128,1,192]{2,1,0:T(1,128)} %reshape.1602), calls=%async_computation.2 | async-start | bytes 262144 | tf_op jit(solution)/shard_map/all_to_all | solution.py:91
  117.0 9.4 %all-to-all-done.2 = f32[128,1,192]{2,1,0:T(1,128)S(1)} async-done(((f32[128,1,192]{2,1,0:T(1,128)}), f32[128,1,192]{2,1,0:T(1,128)S(1)}, u32[]{:S(2)}, u32[]{:S(2)}) %all-to-all-start.2) | async-done | bytes 98336 | tf_op jit(solution)/shard_map/all_to_all | solution.py:91
  164.1 6.6 %all-reduce.9 = (f32[]{:T(128)}, f32[1]{0:T(128)}) all-reduce(f32[]{:T(128)} %get-tuple-element.204, f32[1]{0:T(128)} %bitcast.50), channel_id=1, replica_groups=mesh['cell'=4,'wide_0'=4,'wide_1'=4,'wide_2'=2] {'cell'}, use_global_device_ids=true, to_apply=%region_44.47 | all-reduce | flops 2 | bytes 16 | tf_op jit(solution)/shard_map/psum | solution.py:33
  170.7 7.8 %all-reduce.6 = (f32[]{:T(128)}, f32[1]{0:T(128)}) all-reduce(f32[]{:T(128)} %get-tuple-element.242, f32[1]{0:T(128)} %get-tuple-element.243), channel_id=1, replica_groups=mesh['cell'=4,'wide_0'=4,'wide_1'=4,'wide_2'=2] {'wide_0'}, use_global_device_ids=true, to_apply=%region_45.48 | all-reduce | flops 2 | bytes 16 | tf_op jit(solution)/shard_map/psum | solution.py:33
  178.5 14.0 %all-reduce.3 = (f32[]{:T(128)}, f32[1]{0:T(128)}) all-reduce(f32[]{:T(128)} %get-tuple-element.236, f32[1]{0:T(128)} %get-tuple-element.237), channel_id=1, replica_groups=mesh['cell'=4,'wide_0'=4,'wide_1'=4,'wide_2'=2] {'wide_1'}, use_global_device_ids=true, to_apply=%region_46.49 | all-reduce | flops 2 | bytes 16 | tf_op jit(solution)/shard_map/psum | solution.py:33
  208.2 15.8 %all_to_all.105 = f32[128,1,192]{2,1,0:T(1,128)S(1)} all-to-all(f32[128,1,192]{2,1,0:T(1,128)S(1)} %reshape.1604), channel_id=1, replica_groups=mesh['cell'=4,'wide_0'=4,'wide_1'=4,'wide_2'=2] {'cell','wide_0','wide_1..., dimensions={0} | all-to-all | bytes 196608 | tf_op jit(solution)/shard_map/all_to_all | solution.py:88
  226.7 14.3 %all_to_all.106 = f32[128,1,192]{2,1,0:T(1,128)S(1)} all-to-all(f32[128,1,192]{2,1,0:T(1,128)S(1)} %reshape.1606), channel_id=1, replica_groups=mesh['cell'=4,'wide_0'=4,'wide_1'=4,'wide_2'=2] {'cell','wide_0','wide_1..., dimensions={0} | all-to-all | bytes 196608 | tf_op jit(solution)/shard_map/all_to_all | solution.py:91
  283.4 6.7 %all-reduce.8 = (f32[]{:T(128)}, f32[2]{0:T(128)S(1)}) all-reduce(f32[]{:T(128)} %get-tuple-element.183, f32[2]{0:T(128)S(1)} %pad_maximum_fusion.17), channel_id=1, replica_groups=mesh['cell'=4,'wide_0'=4,'wide_1'=4,'wide_2'=2] {'cell'}, use_global_device_ids=true, to_apply=%region_74.77 | all-reduce | flops 3 | bytes 24 | tf_op jit(solution)/shard_map/psum | solution.py:33
  290.1 7.9 %all-reduce.5 = (f32[]{:T(128)}, f32[2]{0:T(128)S(1)}) all-reduce(f32[]{:T(128)} %get-tuple-element.240, f32[2]{0:T(128)S(1)} %get-tuple-element.241), channel_id=1, replica_groups=mesh['cell'=4,'wide_0'=4,'wide_1'=4,'wide_2'=2] {'wide_0'}, use_global_device_ids=true, to_apply=%region_75.78 | all-reduce | flops 3 | bytes 24 | tf_op jit(solution)/shard_map/psum | solution.py:33
  298.0 13.9 %all-reduce.2 = (f32[]{:T(128)}, f32[2]{0:T(128)S(1)}) all-reduce(f32[]{:T(128)} %get-tuple-element.234, f32[2]{0:T(128)S(1)} %get-tuple-element.235), channel_id=1, replica_groups=mesh['cell'=4,'wide_0'=4,'wide_1'=4,'wide_2'=2] {'wide_1'}, use_global_device_ids=true, to_apply=%region_76.79 | all-reduce | flops 3 | bytes 24 | tf_op jit(solution)/shard_map/psum | solution.py:33
  329.1 6.1 %all-to-all-start.5 = ((f32[128,1,192]{2,1,0:T(1,128)}), f32[128,1,192]{2,1,0:T(1,128)S(1)}, u32[]{:S(2)}, u32[]{:S(2)}) async-start(f32[128,1,192]{2,1,0:T(1,128)} %reshape.1608), calls=%async_computation.5 | async-start | bytes 262144 | tf_op jit(solution)/shard_map/all_to_all | solution.py:88
  336.0 9.2 %all-to-all-done.5 = f32[128,1,192]{2,1,0:T(1,128)S(1)} async-done(((f32[128,1,192]{2,1,0:T(1,128)}), f32[128,1,192]{2,1,0:T(1,128)S(1)}, u32[]{:S(2)}, u32[]{:S(2)}) %all-to-all-start.5) | async-done | bytes 98336 | tf_op jit(solution)/shard_map/all_to_all | solution.py:88
  348.5 4.2 all-to-all-start.6
  353.4 9.4 %all-to-all-done.6 = f32[128,1,192]{2,1,0:T(1,128)S(1)} async-done(((f32[128,1,192]{2,1,0:T(1,128)}), f32[128,1,192]{2,1,0:T(1,128)S(1)}, u32[]{:S(2)}, u32[]{:S(2)}) %all-to-all-start.6) | async-done | bytes 98336 | tf_op jit(solution)/shard_map/all_to_all | solution.py:91
  409.5 6.6 %all-reduce.7 = (f32[3]{0:T(128)S(1)}, f32[]{:T(128)}) all-reduce(f32[3]{0:T(128)S(1)} %pad_maximum_fusion.18, f32[]{:T(128)} %get-tuple-element.160), channel_id=1, replica_groups=mesh['cell'=4,'wide_0'=4,'wide_1'=4,'wide_2'=2] {'cell'}, use_global_device_ids=true, to_apply=%region_102.105 | all-reduce | flops 4 | bytes 32 | tf_op jit(solution)/shard_map/psum | solution.py:33
  416.1 7.7 %all-reduce.4 = (f32[3]{0:T(128)S(1)}, f32[]{:T(128)}) all-reduce(f32[3]{0:T(128)S(1)} %get-tuple-element.238, f32[]{:T(128)} %get-tuple-element.239), channel_id=1, replica_groups=mesh['cell'=4,'wide_0'=4,'wide_1'=4,'wide_2'=2] {'wide_0'}, use_global_device_ids=true, to_apply=%region_103.106 | all-reduce | flops 4 | bytes 32 | tf_op jit(solution)/shard_map/psum | solution.py:33
  423.7 10.4 %all-reduce.1 = (f32[3]{0:T(128)S(1)}, f32[]{:T(128)}) all-reduce(f32[3]{0:T(128)S(1)} %get-tuple-element.232, f32[]{:T(128)} %get-tuple-element.233), channel_id=1, replica_groups=mesh['cell'=4,'wide_0'=4,'wide_1'=4,'wide_2'=2] {'wide_1'}, use_global_device_ids=true, to_apply=%region_104.107 | all-reduce | flops 4 | bytes 32 | tf_op jit(solution)/shard_map/psum | solution.py:33
  434.1 8.1 %all-reduce.10 = (f32[3]{0:T(128)S(1)}, f32[]{:T(128)}) all-reduce(f32[3]{0:T(128)S(1)} %get-tuple-element.226, f32[]{:T(128)} %get-tuple-element.227), channel_id=1, replica_groups=mesh['cell'=4,'wide_0'=4,'wide_1'=4,'wide_2'=2] {'wide_2'}, use_global_device_ids=true, to_apply=%region_105.108 | all-reduce | flops 4 | bytes 32 | tf_op jit(solution)/shard_map/psum | solution.py:33
  461.0 16.0 %all_to_all.107 = f32[128,1,192]{2,1,0:T(1,128)S(1)} all-to-all(f32[128,1,192]{2,1,0:T(1,128)S(1)} %reshape.1612), channel_id=1, replica_groups=mesh['cell'=4,'wide_0'=4,'wide_1'=4,'wide_2'=2] {'cell','wide_0','wide_1..., dimensions={0} | all-to-all | bytes 196608 | tf_op jit(solution)/shard_map/all_to_all | solution.py:88
  479.8 14.3 %all_to_all.108 = f32[128,1,192]{2,1,0:T(1,128)S(1)} all-to-all(f32[128,1,192]{2,1,0:T(1,128)S(1)} %reshape.1614), channel_id=1, replica_groups=mesh['cell'=4,'wide_0'=4,'wide_1'=4,'wide_2'=2] {'cell','wide_0','wide_1..., dimensions={0} | all-to-all | bytes 196608 | tf_op jit(solution)/shard_map/all_to_all | solution.py:91
  (519 shorter events, 213.4 us)
Async XLA Ops:
  0.6 81.3 %collective-permute-start = (f32[3,1,8,128]{3,2,1,0:T(8,128)}, f32[3,1,8,128]{3,2,1,0:T(8,128)S(1)}, u32[]{:S(2)}, u32[]{:S(2)}) collective-permute-start(f32[3,1,8,128]{3,2,1,0:T(8,128)} %param.37), channel_id=1, source_target_pairs={{0,32},{32,64},{64,96},{96,0},{1,33},{33,65},{65,97},{97,1},{2,34}... | collective-permute-start | bytes 36872 | tf_op jit(solution)/shard_map/ppermute | solution.py:26
  3.2 78.8 %collective-permute-start.1 = (f32[3,1,8,128]{3,2,1,0:T(8,128)}, f32[3,1,8,128]{3,2,1,0:T(8,128)S(1)}, u32[]{:S(2)}, u32[]{:S(2)}) collective-permute-start(f32[3,1,8,128]{3,2,1,0:T(8,128)} %param.37), channel_id=1, source_target_pairs={{32,0},{64,32},{96,64},{0,96},{33,1},{65,33},{97,65},{1,97},{34,2}... | collective-permute-start | bytes 36872 | tf_op jit(solution)/shard_map/ppermute | solution.py:27
  16.3 25.2 %copy-start.55 = (f32[3,1,8,128]{3,2,1,0:T(8,128)S(1)}, f32[3,1,8,128]{3,2,1,0:T(8,128)}, u32[]{:S(2)}) copy-start(f32[3,1,8,128]{3,2,1,0:T(8,128)} %param.38) | copy-start | bytes 36868
  16.3 64.1 %copy-start.58 = (f32[3,1,8,128]{3,2,1,0:T(8,128)S(1)}, f32[3,1,8,128]{3,2,1,0:T(8,128)}, u32[]{:S(2)}) copy-start(f32[3,1,8,128]{3,2,1,0:T(8,128)} %param.41) | copy-start | bytes 36868
  32.5 55.8 %all-to-all-start.1 = ((s32[128,32,1]{1,2,0:T(1,128)}), s32[128,32,1]{1,2,0:T(1,128)S(1)}, u32[]{:S(2)}, u32[]{:S(2)}) async-start(s32[128,32,1]{1,2,0:T(1,128)} %bitcast.22), calls=%async_computation.1 | async-start | bytes 131072 | tf_op jit(solution)/shard_map/all_to_all | solution.py:82
  82.0 16.6 %collective-permute-start.2 = (f32[3,3,1,128]{3,2,1,0:T(1,128)S(1)}, f32[3,3,1,128]{3,2,1,0:T(1,128)S(1)}, u32[]{:S(2)}, u32[]{:S(2)}) collective-permute-start(f32[3,3,1,128]{3,2,1,0:T(1,128)S(1)} %get-tuple-element.276), channel_id=1, source_target_pairs={{0,1},{1,2},{2,3},{3,4},{4,5},{5,6},{6,7},{7,8},{8,9},{9,10},{10,1... | collective-permute-start | bytes 13832 | tf_op jit(solution)/shard_map/ppermute | solution.py:26
  82.1 16.5 %collective-permute-start.3 = (f32[3,3,1,128]{3,2,1,0:T(1,128)S(1)}, f32[3,3,1,128]{3,2,1,0:T(1,128)S(1)}, u32[]{:S(2)}, u32[]{:S(2)}) collective-permute-start(f32[3,3,1,128]{3,2,1,0:T(1,128)S(1)} %get-tuple-element.277), channel_id=1, source_target_pairs={{1,0},{2,1},{3,2},{4,3},{5,4},{6,5},{7,6},{8,7},{9,8},{10,9},{11,1... | collective-permute-start | bytes 13832 | tf_op jit(solution)/shard_map/ppermute | solution.py:27
  86.4 15.1 %copy-start.66 = (f32[3]{0:T(128)S(1)}, f32[3]{0:T(128)}, u32[]{:S(2)}) copy-start(f32[3]{0:T(128)} %constant.364.clone) | copy-start | bytes 40
  86.4 15.2 %copy-start.65 = (f32[3]{0:T(128)S(1)}, f32[3]{0:T(128)}, u32[]{:S(2)}) copy-start(f32[3]{0:T(128)} %constant.363.clone) | copy-start | bytes 40
  86.5 15.3 %copy-start.64 = (f32[3]{0:T(128)S(1)}, f32[3]{0:T(128)}, u32[]{:S(2)}) copy-start(f32[3]{0:T(128)} %constant.362.clone) | copy-start | bytes 40
  86.5 15.3 %copy-start.63 = (f32[3]{0:T(128)S(1)}, f32[3]{0:T(128)}, u32[]{:S(2)}) copy-start(f32[3]{0:T(128)} %constant.361.clone) | copy-start | bytes 40
  86.5 15.4 %copy-start.62 = (f32[3]{0:T(128)S(1)}, f32[3]{0:T(128)}, u32[]{:S(2)}) copy-start(f32[3]{0:T(128)} %constant.359.clone) | copy-start | bytes 40
  88.2 19.1 %all-to-all-start = ((f32[128,1,192]{2,1,0:T(1,128)}), f32[128,1,192]{2,1,0:T(1,128)S(1)}, u32[]{:S(2)}, u32[]{:S(2)}) async-start(f32[128,1,192]{2,1,0:T(1,128)} %reshape.1600), calls=%async_computation | async-start | bytes 262144 | tf_op jit(solution)/shard_map/all_to_all | solution.py:88
  98.5 11.1 %copy-start.56 = (f32[6,6,32]{2,1,0:T(8,128)S(1)}, f32[6,6,32]{2,1,0:T(8,128)}, u32[]{:S(2)}) copy-start(f32[6,6,32]{2,1,0:T(8,128)} %param.42) | copy-start | bytes 13828
  111.2 15.2 %all-to-all-start.2 = ((f32[128,1,192]{2,1,0:T(1,128)}), f32[128,1,192]{2,1,0:T(1,128)S(1)}, u32[]{:S(2)}, u32[]{:S(2)}) async-start(f32[128,1,192]{2,1,0:T(1,128)} %reshape.1602), calls=%async_computation.2 | async-start | bytes 262144 | tf_op jit(solution)/shard_map/all_to_all | solution.py:91
  132.9 2.6 collective-permute-start.5
  133.4 3.8 collective-permute-start.4
  137.1 3.0 collective-permute-start.6
  139.2 3.2 collective-permute-start.7
  251.4 16.8 %copy-start.32 = (f32[8,128,128]{2,1,0:T(8,128)S(1)}, f32[8,128,128]{2,1,0:T(8,128)}, u32[]{:S(2)}) copy-start(f32[8,128,128]{2,1,0:T(8,128)} %copy-done.31) | copy-start | bytes 1572868
  251.6 2.6 collective-permute-start.9
  252.1 3.8 collective-permute-start.8
  255.8 3.0 collective-permute-start.10
  258.1 3.4 collective-permute-start.11
  329.1 16.1 %all-to-all-start.5 = ((f32[128,1,192]{2,1,0:T(1,128)}), f32[128,1,192]{2,1,0:T(1,128)S(1)}, u32[]{:S(2)}, u32[]{:S(2)}) async-start(f32[128,1,192]{2,1,0:T(1,128)} %reshape.1608), calls=%async_computation.5 | async-start | bytes 262144 | tf_op jit(solution)/shard_map/all_to_all | solution.py:88
  348.5 14.2 %all-to-all-start.6 = ((f32[128,1,192]{2,1,0:T(1,128)}), f32[128,1,192]{2,1,0:T(1,128)S(1)}, u32[]{:S(2)}, u32[]{:S(2)}) async-start(f32[128,1,192]{2,1,0:T(1,128)} %reshape.1610), calls=%async_computation.6 | async-start | bytes 262144 | tf_op jit(solution)/shard_map/all_to_all | solution.py:91
  373.3 19.7 %copy-start.27 = (f32[8,128,128]{2,1,0:T(8,128)S(1)}, f32[8,128,128]{2,1,0:T(8,128)}, u32[]{:S(2)}) copy-start(f32[8,128,128]{2,1,0:T(8,128)} %copy-done.25) | copy-start | bytes 1572868
  373.5 2.6 collective-permute-start.13
  373.9 3.8 collective-permute-start.12
  377.7 8.5 %collective-permute-start.14 = (f32[3,3,1,128]{3,2,0,1:T(1,128)S(1)}, f32[3,3,1,128]{3,2,0,1:T(1,128)S(1)}, u32[]{:S(2)}, u32[]{:S(2)}) collective-permute-start(f32[3,3,1,128]{3,2,0,1:T(1,128)S(1)} %get-tuple-element.270), channel_id=1, source_target_pairs={{0,1},{1,2},{2,3},{3,4},{4,5},{5,6},{6,7},{7,8},{8,9},{9,10},{10,1... | collective-permute-start | bytes 13832 | tf_op jit(solution)/shard_map/ppermute | solution.py:26
  379.7 6.5 %collective-permute-start.15 = (f32[3,3,1,128]{3,2,0,1:T(1,128)S(1)}, f32[3,3,1,128]{3,2,0,1:T(1,128)S(1)}, u32[]{:S(2)}, u32[]{:S(2)}) collective-permute-start(f32[3,3,1,128]{3,2,0,1:T(1,128)S(1)} %get-tuple-element.271), channel_id=1, source_target_pairs={{1,0},{2,1},{3,2},{4,3},{5,4},{6,5},{7,6},{8,7},{9,8},{10,9},{11,1... | collective-permute-start | bytes 13832 | tf_op jit(solution)/shard_map/ppermute | solution.py:27
  478.9 16.3 %copy-start.57 = (f32[32,6]{0,1:T(8,128)}, f32[32,6]{0,1:T(8,128)S(1)}, u32[]{:S(2)}) copy-start(f32[32,6]{0,1:T(8,128)S(1)} %multiply_reduce_fusion) | copy-start | bytes 2308
  (57 other events, 126.1 us)
where the time goes:
time: 511 us; the launch traced here: 502 us
  blocking collectives  193 us (38%)
  local copies, waits for them, and re-layouts  126 us (25%)
  other arithmetic  73.4 us (14%)
  starting transfers between devices  50.5 us (10%)
  waiting for transfers between devices  45.2 us (9%)
  between operations  9.96 us (2%)
    psum x16, blocking collectives, over_axes(): return functools.reduce(lax.psum, axes, array)  133 us
    all_to_all x2, blocking collectives, send_out(): lax.all_to_all(buffer, CELL_WIDE, split_axis=1, concat_axis=1, tiled=True)  31.8 us
    all_to_all x2, blocking collectives, send_back(): lax.all_to_all(buffer, CELL_WIDE, split_axis=1, concat_axis=1, tiled=True)  28.5 us
    unnamed x155, local copies, waits for them, and re-layouts  20.6 us
    all_to_all x2, waiting for transfers between devices, send_back(): lax.all_to_all(buffer, CELL_WIDE, split_axis=1, concat_axis=1, tiled=True)  18.7 us
    gather x27, local copies, waits for them, and re-layouts, local(): jnp.take(outer, starts_of[mobility_code], axis=1)  15.5 us
    scatter x4, local copies, waits for them, and re-layouts, precondition(): buffer = jnp.zeros((6, ndev * capacity), jnp.float32).at[:, slots].set(sent)  15.4 us
    all_to_all x2, starting transfers between devices, send_out(): lax.all_to_all(buffer, CELL_WIDE, split_axis=1, concat_axis=1, tiled=True)  15.1 us
  transfers between devices with their start and end apart: 21, of which 13 were waited for; matrix products, arithmetic and copies ran while one was open for 10% of the time, Pallas kernels for 0%

commit v1 on v0

v1 whole, which is shorter than its diff:
```python
import math

import jax
import jax.numpy as jnp
from jax import lax
from jax.experimental import pallas as pl
from jax.experimental.pallas import tpu as pltpu
from jax.sharding import Mesh
from jax.sharding import PartitionSpec as P

ITERS = 3
WIDE = ("wide_0", "wide_1", "wide_2")
CELL_WIDE = ("cell", "wide_0", "wide_1", "wide_2")
EPS2 = 0.04
KAPPA = 0.3
FACTOR = KAPPA / math.sqrt(9 * 128)
F32 = jnp.float32
BF16 = jnp.bfloat16

TY = 8
TILE = 128
NDEV = 128
NWIDE = 32
ROWS = 32
HALO_AT = 64
DOT_AT = 88
BLOCKS = 6
EDGE_OF = {-1: 3, 0: 4, 1: 5}
ROW_OF = {-1: 1, 0: 0, 1: 2}


def iota(shape, axis):
    return lax.broadcasted_iota(jnp.int32, shape, axis)


def split2(x):
    hi = x.astype(BF16).astype(F32)
    return hi, x - hi


def cross(a, b):
    return (
        a[1] * b[2] - a[2] * b[1],
        a[2] * b[0] - a[0] * b[2],
        a[0] * b[1] - a[1] * b[0],
    )


def rows_of(message_ref, part, parts):
    return message_ref[pl.ds(part, NDEV, stride=parts), :]


def body_sums(field, arms, owner, row, onehot_ref, high_ref, low_ref):
    sent = list(field) + list(cross(arms, field))
    pieces = [split2(x) for x in sent]
    owner_ids = iota((NDEV, TILE), 0)
    row_ids = iota((ROWS, TILE), 0)
    for tile in range(TY):
        lanes = pl.ds(tile * TILE, TILE)
        pick = slice(tile, tile + 1)
        onehot_ref[:, lanes] = jnp.where(owner_ids == owner[pick], 1.0, 0.0).astype(BF16)
        mine = row_ids == row[pick]
        for part in range(6):
            place = slice(part * ROWS, (part + 1) * ROWS)
            high, low = pieces[part]
            high_ref[place, lanes] = jnp.where(mine, high[pick], 0.0).astype(BF16)
            low_ref[place, lanes] = jnp.where(mine, low[pick], 0.0).astype(BF16)
    contract = (((1,), (1,)), ((), ()))
    onehot = onehot_ref[...]
    return lax.dot_general(
        onehot, high_ref[...], contract, preferred_element_type=F32
    ) + lax.dot_general(onehot, low_ref[...], contract, preferred_element_type=F32)


def total(x):
    return jnp.sum(jnp.sum(x, axis=1, keepdims=True), axis=0, keepdims=True)


def forward_message(field, sums, dots, out_ref, parts):
    lane = iota((NDEV, TILE), 1)
    stacked = jnp.concatenate(
        [jnp.zeros((HALO_AT, TILE), F32)]
        + list(field)
        + [jnp.zeros((TILE - DOT_AT, TILE), F32)],
        axis=0,
    )
    second = jnp.concatenate([sums[:, TILE:], jnp.zeros((NDEV, 64), F32)], axis=1)
    second = second + stacked.T
    for at, dot in enumerate(dots):
        second = jnp.where(lane == DOT_AT + at, dot, second)
    out_ref[pl.ds(0, NDEV, stride=parts), :] = sums[:, :TILE]
    out_ref[pl.ds(1, NDEV, stride=parts), :] = second


def start_kernel(pos_ref, rhs_ref, owner_ref, row_ref, arm_ref, out_ref, onehot, high, low):
    field = [rhs_ref[8 * c : 8 * c + 8, :] for c in range(3)]
    arms = [arm_ref[8 * c : 8 * c + 8, :] for c in range(3)]
    owner, row = owner_ref[...], row_ref[...]
    sums = body_sums(field, arms, owner, row, onehot, high, low)
    square = total(field[0] * field[0] + field[1] * field[1] + field[2] * field[2])
    forward_message(field, sums, [square], out_ref, 3)
    fixed = jnp.concatenate(
        [
            pos_ref[...],
            arm_ref[...],
            owner.astype(F32),
            row.astype(F32),
            jnp.zeros((64, TILE), F32),
        ],
        axis=0,
    )
    out_ref[pl.ds(2, NDEV, stride=3), :] = fixed.T


def turned(x, by):
    by = (by % 4) * NWIDE
    return x if by == 0 else jnp.concatenate([x[by:], x[:by]], axis=0)


def beside(x, by):
    groups = [x[z * NWIDE : (z + 1) * NWIDE] for z in range(4)]
    return jnp.concatenate([pltpu.roll(g, (-by) % NWIDE, 0) for g in groups], axis=0)


def routed(x, first, width):
    lane = iota((NDEV, TILE), 1)
    x = jnp.where((lane >= first) & (lane < first + width), x, 0.0)
    place = (lane - first) & 7
    edge = jnp.where(place == 7, beside(x, -1), jnp.where(place == 0, beside(x, 1), 0.0))
    return [turned(x, -1), turned(x, 1), turned(edge, -1), edge, turned(edge, 1)]


def shifted(x, by):
    by = by % TILE
    return x if by == 0 else pltpu.roll(x, by, 1)


def spread(row, lane):
    return jnp.broadcast_to(row[:, lane : lane + 1], (1, TILE))


def owner_kernel(step, parts, inverse_ref, message_ref, *refs):
    states = refs[:step]
    out_ref, state_ref = refs[step:]
    first = rows_of(message_ref, 0, parts)
    second = rows_of(message_ref, 1, parts)
    sums = [jnp.sum(first, axis=0, keepdims=True), jnp.sum(second, axis=0, keepdims=True)]
    inners = [spread(sums[1], DOT_AT + 1 + i) for i in range(step)]
    square = spread(sums[1], DOT_AT)
    for inner in inners:
        square = square - inner * inner
    length = jnp.sqrt(square)
    scale = 1.0 / length
    for i in range(step):
        for half in range(2):
            sums[half] = sums[half] - inners[i] * states[i][half : half + 1, :]
    sums = [s * scale for s in sums]
    sub, lane = iota((8, TILE), 0), iota((8, TILE), 1)
    tiled = jnp.where(sub < 4, sums[0], sums[1])
    tiled = jnp.where((lane // ROWS == sub % 4) & (sub < 6), tiled, 0.0)
    tiled = tiled + pltpu.roll(tiled, 32, 1)
    tiled = tiled + pltpu.roll(tiled, 64, 1)
    motion = [
        jnp.sum(inverse_ref[8 * half : 8 * half + 8, :] * tiled, axis=0, keepdims=True)
        for half in range(2)
    ]
    zero = jnp.zeros((1, TILE), F32)
    state_ref[...] = jnp.concatenate(
        sums + motion + [length, scale] + inners + [zero] * (2 - step), axis=0
    )
    back = 6 if parts == 3 else 3
    for half in range(2):
        out_ref[pl.ds(half, NDEV, stride=back), :] = jnp.broadcast_to(motion[half], (NDEV, TILE))
    blocks = routed(second, HALO_AT, 24)
    rim = shifted(blocks[0], -HALO_AT)
    for k in range(1, 5):
        rim = rim + shifted(blocks[k], 24 * k - HALO_AT)
    out_ref[pl.ds(2, NDEV, stride=back), :] = rim
    if parts == 3:
        blocks = routed(rows_of(message_ref, 2, parts), 0, 64)
        out_ref[pl.ds(3, NDEV, stride=back), :] = blocks[0] + shifted(blocks[1], 64)
        out_ref[pl.ds(4, NDEV, stride=back), :] = blocks[2] + shifted(blocks[3], 64)
        out_ref[pl.ds(5, NDEV, stride=back), :] = blocks[4]


def picked_motion(first, second, owner_ref, row_ref):
    table = jnp.concatenate([first.T, second.T[:64]], axis=0)
    high, low = split2(table)
    table = jnp.concatenate([high.astype(BF16), low.astype(BF16)], axis=1)
    owner_ids = iota((NDEV, TILE), 0)
    row_ids = iota((ROWS, TILE), 0)
    sub = iota((8, TILE), 0)
    results = []
    for block in range(BLOCKS):
        owner = owner_ref[8 * block : 8 * block + 8, :]
        row = row_ref[8 * block : 8 * block + 8, :]
        values = [jnp.zeros((8, TILE), F32) for _ in range(6)]
        for tile in range(TY) if block < 3 else (0, 7):
            pick = slice(tile, tile + 1)
            onehot = jnp.where(owner_ids == owner[pick], 1.0, 0.0).astype(BF16)
            onehot = jnp.concatenate([onehot, onehot], axis=0)
            found = jnp.dot(table, onehot, preferred_element_type=F32)
            mine = row_ids == row[pick]
            for part in range(6):
                chosen = jnp.where(mine, found[part * ROWS : (part + 1) * ROWS], 0.0)
                value = jnp.sum(chosen, axis=0, keepdims=True)
                values[part] = jnp.where(sub == tile, value, values[part])
        results.append(values)
    return results


def mobility(pos_ref, moved, source_ref):
    sub = iota((8, TILE), 0)

    def block(get, number, part):
        return get(number, part)

    def at(number, part):
        return pos_ref[24 * number + 8 * part : 24 * number + 8 * part + 8, :]

    def moved_at(number, part):
        return moved[number][part]

    for code in range(9):
        dx, dy = code // 3 - 1, code % 3 - 1
        for kind, get in enumerate((at, moved_at)):
            for part in range(3):
                x = get(ROW_OF[dx], part)
                if dy == -1:
                    x = jnp.where(sub == 7, get(EDGE_OF[dx], part), x)
                    x = pltpu.roll(x, 1, 0)
                elif dy == 1:
                    x = jnp.where(sub == 0, get(EDGE_OF[dx], part), x)
                    x = pltpu.roll(x, 7, 0)
                if kind == 0 and part < 2:
                    x = x + float((dx, dy)[part])
                place = 24 * kind + 8 * part
                source_ref[code, place : place + 8, :] = x
    target = [at(0, part) for part in range(3)]
    unroll = 8

    def of_code(code, sums):
        source = [source_ref[code, 8 * k : 8 * k + 8, :] for k in range(6)]

        def of_turn(turn, sums):
            for k in range(unroll):
                there = [pltpu.roll(s, turn * unroll + k, 1) for s in source]
                sep = [target[a] - there[a] for a in range(3)]
                soft = sep[0] * sep[0] + sep[1] * sep[1] + (sep[2] * sep[2] + EPS2)
                root = lax.rsqrt(soft)
                inverse = root * root * root
                near = root + EPS2 * inverse
                along = sep[0] * there[3] + sep[1] * there[4] + sep[2] * there[5]
                along = along * inverse
                sums = tuple(
                    sums[a] + (near * there[3 + a] + along * sep[a]) for a in range(3)
                )
            return sums

        return lax.fori_loop(0, TILE // unroll, of_turn, sums)

    zero = jnp.zeros((8, TILE), F32)
    return lax.fori_loop(0, 9, of_code, (zero, zero, zero))


def local_kernel(step, *refs):
    refs = list(refs)
    take = lambda n: [refs.pop(0) for _ in range(n)]
    message_ref, state_ref, field_ref = take(3)
    back = 6 if step == 0 else 3
    if step == 0:
        own_pos, own_arm, own_owner, own_row = take(4)
    else:
        pos_ref, arm_ref, owner_ref, row_ref = take(4)
    bases = take(step)
    if step == 0:
        pos_ref, arm_ref, owner_ref, row_ref = take(4)
    basis_ref, moved_ref, fresh_ref, out_ref = take(4)
    source_ref, onehot, high, low = take(4)
    if step == 0:
        near = rows_of(message_ref, 3, back).T
        edge = rows_of(message_ref, 4, back).T
        last = rows_of(message_ref, 5, back).T
        fixed = [near[:64], near[64:], edge[:64], edge[64:], last[:64]]
        pos_ref[0:24, :] = own_pos[...]
        arm_ref[0:24, :] = own_arm[...]
        owner_ref[0:8, :] = own_owner[...]
        row_ref[0:8, :] = own_row[...]
        for k in range(5):
            pos_ref[24 * (k + 1) : 24 * (k + 2), :] = fixed[k][0:24]
            arm_ref[24 * (k + 1) : 24 * (k + 2), :] = fixed[k][24:48]
            owner_ref[8 * (k + 1) : 8 * (k + 2), :] = fixed[k][48:56].astype(jnp.int32)
            row_ref[8 * (k + 1) : 8 * (k + 2), :] = fixed[k][56:64].astype(jnp.int32)
    rim = rows_of(message_ref, 2, back).T
    basis = jnp.concatenate([field_ref[...], rim[:120]], axis=0)
    for i in range(step):
        basis = basis - state_ref[6 + i : 7 + i, :] * bases[i][...]
    basis = basis * state_ref[5:6, :]
    basis_ref[...] = basis
    motions = picked_motion(
        rows_of(message_ref, 0, back), rows_of(message_ref, 1, back), owner_ref, row_ref
    )
    moved = []
    for block in range(BLOCKS):
        arm = [arm_ref[24 * block + 8 * a : 24 * block + 8 * a + 8, :] for a in range(3)]
        turn = cross(motions[block][3:], arm)
        moved.append(
            [
                basis[24 * block + 8 * a : 24 * block + 8 * a + 8]
                + (motions[block][a] + turn[a])
                for a in range(3)
            ]
        )
    pairs = mobility(pos_ref, moved, source_ref)
    fresh = [moved[0][a] + FACTOR * pairs[a] for a in range(3)]
    for a in range(3):
        moved_ref[8 * a : 8 * a + 8, :] = moved[0][a]
        fresh_ref[8 * a : 8 * a + 8, :] = fresh[a]

    def dot(get):
        return total(fresh[0] * get(0) + fresh[1] * get(1) + fresh[2] * get(2))

    dots = [dot(lambda a: fresh[a])]
    for i in range(step):
        dots.append(dot(lambda a: bases[i][8 * a : 8 * a + 8, :]))
    dots.append(dot(lambda a: basis[8 * a : 8 * a + 8]))
    if step < ITERS - 1:
        arms = [arm_ref[8 * a : 8 * a + 8, :] for a in range(3)]
        sums = body_sums(
            fresh, arms, owner_ref[0:8, :], row_ref[0:8, :], onehot, high, low
        )
        forward_message(fresh, sums, dots, out_ref, 2)
    else:
        lane = iota((NDEV, TILE), 1)
        message = jnp.zeros((NDEV, TILE), F32)
        for at, value in enumerate(dots):
            message = jnp.where(lane == at, value, message)
        out_ref[...] = message


def final_kernel(message_ref, *refs):
    states, moved = refs[:3], refs[3:6]
    forces_ref, motion_ref = refs[6:]
    sums = jnp.sum(message_ref[...], axis=0, keepdims=True)
    beta = states[0][4:5, :]
    a = [states[1][6:7, :], states[1][4:5, :]]
    b = [states[2][6:7, :], states[2][7:8, :], states[2][4:5, :]]
    c = [spread(sums, 1 + i) for i in range(3)]
    square = spread(sums, 0) - c[0] * c[0] - c[1] * c[1] - c[2] * c[2]
    c.append(jnp.sqrt(square))
    inner = lambda p, q: sum([x * y for x, y in zip(p, q)][1:], p[0] * q[0])
    n00, n01, n02 = inner(a, a), inner(a, b), inner(a, c)
    n11, n12, n22 = inner(b, b), inner(b, c), inner(c, c)
    l00 = jnp.sqrt(n00)
    l10, l20 = n01 / l00, n02 / l00
    l11 = jnp.sqrt(n11 - l10 * l10)
    l21 = (n12 - l20 * l10) / l11
    l22 = jnp.sqrt(n22 - l20 * l20 - l21 * l21)
    t0 = beta * a[0] / l00
    t1 = (beta * b[0] - l10 * t0) / l11
    t2 = (beta * c[0] - l20 * t0 - l21 * t1) / l22
    y2 = t2 / l22
    y1 = (t1 - l21 * y2) / l11
    y0 = (t0 - l10 * y1 - l20 * y2) / l00
    forces_ref[...] = y0 * moved[0][...] + y1 * moved[1][...] + y2 * moved[2][...]
    for part in range(6):
        half, at = part // 4, (part % 4) * ROWS
        row = slice(2 + half, 3 + half)
        whole = y0 * states[0][row, :] + y1 * states[1][row, :] + y2 * states[2][row, :]
        motion_ref[part : part + 1, :] = whole[:, at : at + ROWS]


def f32(*shape):
    return jax.ShapeDtypeStruct(shape, F32)


def i32(*shape):
    return jax.ShapeDtypeStruct(shape, jnp.int32)


PARAMS = pltpu.CompilerParams(vmem_limit_bytes=24 * 1024 * 1024)


def sums_scratch():
    return [
        pltpu.VMEM((NDEV, TY * TILE), BF16),
        pltpu.VMEM((6 * ROWS, TY * TILE), BF16),
        pltpu.VMEM((6 * ROWS, TY * TILE), BF16),
    ]


def call(body, out, scratch=()):
    return pl.pallas_call(body, out_shape=out, scratch_shapes=list(scratch), compiler_params=PARAMS)


def exchange(message):
    return lax.all_to_all(message, CELL_WIDE, split_axis=0, concat_axis=0, tiled=True)


def local(positions, rhs, blob_owner, blob_row, blob_arm, body_inverse):
    pos = positions.reshape(24, TILE)
    field = rhs.reshape(24, TILE)
    arm = blob_arm.reshape(24, TILE)
    owner = blob_owner.reshape(TY, TILE)
    row = blob_row.reshape(TY, TILE)
    inverse = jnp.transpose(body_inverse, (1, 0, 2)).reshape(6, 6 * ROWS)
    inverse = jnp.pad(inverse, ((0, 2), (0, 64)))
    inverse = jnp.concatenate([inverse[:, :TILE], inverse[:, TILE:]], axis=0)
    message = call(start_kernel, f32(3 * NDEV, TILE), sums_scratch())(pos, field, owner, row, arm)
    fixed = (pos, arm, owner, row)
    states, bases, moveds = [], [], []
    for step in range(ITERS):
        parts = 3 if step == 0 else 2
        back = 6 if step == 0 else 3
        arrived = exchange(message)
        message, state = call(
            lambda *refs, step=step, parts=parts: owner_kernel(step, parts, *refs),
            (f32(back * NDEV, TILE), f32(8, TILE)),
        )(inverse, arrived, *states)
        arrived = exchange(message)
        outs = [
            f32(24 * BLOCKS, TILE),
            f32(24, TILE),
            f32(24, TILE),
            f32(NDEV if step == ITERS - 1 else 2 * NDEV, TILE),
        ]
        if step == 0:
            outs = [
                f32(24 * BLOCKS, TILE),
                f32(24 * BLOCKS, TILE),
                i32(8 * BLOCKS, TILE),
                i32(8 * BLOCKS, TILE),
            ] + outs
        results = call(
            lambda *refs, step=step: local_kernel(step, *refs),
            tuple(outs),
            [pltpu.VMEM((9, 48, TILE), F32)] + sums_scratch(),
        )(arrived, state, field, *fixed, *bases)
        if step == 0:
            fixed = results[:4]
        basis, moved, field, message = results[-4:]
        states.append(state)
        bases.append(basis)
        moveds.append(moved)
    arrived = exchange(message)
    forces, motion = call(final_kernel, (f32(24, TILE), f32(6, ROWS)))(arrived, *states, *moveds)
    return (forces.reshape(rhs.shape), motion)


def solution(mesh):
    split = Mesh(
        mesh.devices.reshape(mesh.shape["cell"], 4, 4, 2), ("cell", "wide_0", "wide_1", "wide_2")
    )
    in_specs = (
        P(None, "cell", WIDE, None),
        P(None, "cell", WIDE, None),
        P("cell", WIDE, None, None),
        P("cell", WIDE, None),
        P(None, "cell", WIDE, None),
        P(None, None, CELL_WIDE),
    )
    out_specs = (P(None, "cell", WIDE, None), P(None, CELL_WIDE))
    return jax.shard_map(local, mesh=split, in_specs=in_specs, out_specs=out_specs, check_vma=False)
```

time: 511 us -> 182 us (0.36); the launches traced: 502 us -> 181 us
  local copies, waits for them, and re-layouts: 126 us -> 4.91 us
  blocking collectives: 193 us -> 91 us
  other arithmetic: 73.4 us -> 0.01 us
  Pallas kernels: 0 us -> 62 us
  starting transfers between devices: 50.5 us -> 11.5 us
  waiting for transfers between devices: 45.2 us -> 11 us
  between operations: 9.96 us -> 0.77 us
    psum x16 -> x0, blocking collectives: 133 us -> none  [over_axes(): return functools.reduce(lax.psum, axes, array)]
    pallas_call x0 -> x8, Pallas kernels: none -> 62 us  [the longest x3 60 us: local(): call(lambda *refs, step=step: local_kernel(step, *refs), tuple(outs), [pl...]
    gather x42 -> x0, local copies, waits for them, and re-layouts: 45.4 us -> none  [the longest x27 15.5 us: local(): jnp.take(outer, starts_of[mobility_code], axis=1)]
    reduce_sum x19 -> x0, other arithmetic: 31.5 us -> none  [the longest x5 12.8 us: pair_sum(): jnp.sum(near[None] * forces[..., None, :] + (inverse * along)[None] * sep...]
    scatter x15 -> x0, local copies, waits for them, and re-layouts: 31 us -> none  [the longest x4 15.4 us: precondition(): buffer = jnp.zeros((6, ndev * capacity), jnp.float32).at[:, slots].set(sent)]
    all_to_all x4 -> x6, blocking collectives: 60.3 us -> 91 us  [exchange(): lax.all_to_all(message, CELL_WIDE, split_axis=0, concat_axis=0, tiled=True)]
    all_to_all x5 -> x1, waiting for transfers between devices: 32.8 us -> 11 us  [exchange(): lax.all_to_all(message, CELL_WIDE, split_axis=0, concat_axis=0, tiled=True)]
    all_to_all x5 -> x1, starting transfers between devices: 33.3 us -> 11.5 us  [exchange(): lax.all_to_all(message, CELL_WIDE, split_axis=0, concat_axis=0, tiled=True)]
  transfers between devices with their start and end apart: 21 -> 1, of which waited for: 13 -> 1; matrix products, arithmetic and copies ran while one was open for 10% -> 0% of each run, Pallas kernels for 0% -> 0%
where the time goes in v1:
time: 182 us; the launch traced here: 181 us
  blocking collectives  91 us (50%)
  Pallas kernels  62 us (34%)
  starting transfers between devices  11.5 us (6%)
  waiting for transfers between devices  11 us (6%)
  local copies, waits for them, and re-layouts  4.91 us (3%)
    all_to_all x6, blocking collectives, exchange(): lax.all_to_all(message, CELL_WIDE, split_axis=0, concat_axis=0, tiled=True)  91 us
    pallas_call x3, Pallas kernels, local(): call(lambda *refs, step=step: local_kernel(step, *refs), tuple(outs), [pl...  60 us
    all_to_all x1, starting transfers between devices, exchange(): lax.all_to_all(message, CELL_WIDE, split_axis=0, concat_axis=0, tiled=True)  11.5 us
    all_to_all x1, waiting for transfers between devices, exchange(): lax.all_to_all(message, CELL_WIDE, split_axis=0, concat_axis=0, tiled=True)  11 us
  transfers between devices with their start and end apart: 1, of which 1 were waited for; matrix products, arithmetic and copies ran while one was open for 0% of the time, Pallas kernels for 0%

profile of v1, /device:TPU:1, one launch (start us, length us, event | category | flops | bytes accessed | tf_op | source)
XLA Modules:
  0.0 181.2 jit_solution(1792570005787697140)
XLA Ops:
  0.6 0.7 copy-done.7
  1.3 0.0 copy-done.6
  1.3 0.7 copy-done
  2.0 0.7 copy-done.2
  2.8 0.7 copy-done.4
  3.5 0.5 shard_map.77
  3.9 0.8 all_to_all.49
  4.7 11.5 %all-to-all-start = ((f32[128,3,128]{2,1,0:T(4,128)}), f32[128,3,128]{2,1,0:T(4,128)S(1)}, u32[]{:S(2)}, u32[]{:S(2)}) async-start(f32[128,3,128]{2,1,0:T(4,128)} %all_to_all.49), calls=%async_computation | async-start | bytes 524288 | tf_op jit(solution)/shard_map/all_to_all | solution.py:397
  16.2 0.1 reshape.39
  16.3 11.0 %all-to-all-done = f32[128,3,128]{2,1,0:T(4,128)S(1)} async-done(((f32[128,3,128]{2,1,0:T(4,128)}), f32[128,3,128]{2,1,0:T(4,128)S(1)}, u32[]{:S(2)}, u32[]{:S(2)}) %all-to-all-start) | async-done | bytes 196640 | tf_op jit(solution)/shard_map/all_to_all | solution.py:397
  27.3 0.1 all_to_all.51.refs_1_
  27.4 0.3 shard_map.78
  27.7 0.1 all_to_all.52
  27.7 18.0 %all_to_all.77 = f32[128,6,128]{2,1,0:T(8,128)S(1)} all-to-all(f32[128,6,128]{2,1,0:T(8,128)S(1)} %all_to_all.52), channel_id=1, replica_groups=mesh['cell'=4,'wide_0'=4,'wide_1'=4,'wide_2'=2] {'cell','wide_0','wide_1..., dimensions={0} | all-to-all | bytes 786432 | tf_op jit(solution)/shard_map/all_to_all | solution.py:397
  45.7 0.7 copy-done.1
  46.4 0.0 copy-done.3
  46.4 0.0 copy-done.5
  46.4 20.0 %shard_map.79 = (f32[144,128]{1,0:T(8,128)S(1)}, f32[144,128]{1,0:T(8,128)S(1)}, s32[48,128]{1,0:T(8,128)S(1)}, s32[48,128]{1,0:T(8,128)S(1)}, f32[144,128]{1,0:...) custom-call(f32[768,128]{1,0:T(8,128)S(1)} %all_to_all.54.refs_0_, ...), custom_call_target="tpu_custom_call" | custom-call | tf_op jit(solution)/shard_map/pallas_call | solution.py:434
  66.5 14.4 %all_to_all.78 = f32[128,2,128]{2,1,0:T(2,128)S(1)} all-to-all(f32[128,2,128]{2,1,0:T(2,128)S(1)} %bitcast.20), channel_id=1, replica_groups=mesh['cell'=4,'wide_0'=4,'wide_1'=4,'wide_2'=2] {'cell','wide_0','wide_1..., dimensions={0} | all-to-all | bytes 262144 | tf_op jit(solution)/shard_map/all_to_all | solution.py:397
  80.9 0.3 shard_map.80
  81.2 0.1 all_to_all.58
  81.3 15.3 %all_to_all.79 = f32[128,3,128]{2,1,0:T(4,128)S(1)} all-to-all(f32[128,3,128]{2,1,0:T(4,128)S(1)} %all_to_all.58), channel_id=1, replica_groups=mesh['cell'=4,'wide_0'=4,'wide_1'=4,'wide_2'=2] {'cell','wide_0','wide_1..., dimensions={0} | all-to-all | bytes 393216 | tf_op jit(solution)/shard_map/all_to_all | solution.py:397
  96.6 0.1 all_to_all.60.refs_0_
  96.7 20.0 %shard_map.81 = (f32[144,128]{1,0:T(8,128)S(1)}, f32[24,128]{1,0:T(8,128)S(1)}, f32[24,128]{1,0:T(8,128)S(1)}, f32[256,128]{1,0:T(8,128)S(1)}) custom-call(f32[384,128]{1,0:T(8,128)S(1)} %all_to_all.60.refs_0_, f32[8,128]{1,0:T(8,128)S(1)} %get-tuple-element.28.refs_1_.refs_3_, f32[24,128]{1,0:T(8,128)S(1)} %get-tuple-element.29.refs_2_, ...), custom_call_target="tpu_custom_call" | custom-call | tf_op jit(solution)/shard_map/pallas_call | solution.py:434
  116.7 14.2 %all_to_all.80 = f32[128,2,128]{2,1,0:T(2,128)S(1)} all-to-all(f32[128,2,128]{2,1,0:T(2,128)S(1)} %bitcast.21), channel_id=1, replica_groups=mesh['cell'=4,'wide_0'=4,'wide_1'=4,'wide_2'=2] {'cell','wide_0','wide_1..., dimensions={0} | all-to-all | bytes 262144 | tf_op jit(solution)/shard_map/all_to_all | solution.py:397
  131.0 0.3 shard_map.82
  131.2 0.1 all_to_all.64
  131.3 15.3 %all_to_all.81 = f32[128,3,128]{2,1,0:T(4,128)S(1)} all-to-all(f32[128,3,128]{2,1,0:T(4,128)S(1)} %all_to_all.64), channel_id=1, replica_groups=mesh['cell'=4,'wide_0'=4,'wide_1'=4,'wide_2'=2] {'cell','wide_0','wide_1..., dimensions={0} | all-to-all | bytes 393216 | tf_op jit(solution)/shard_map/all_to_all | solution.py:397
  146.7 0.1 all_to_all.66.refs_0_
  146.8 20.0 %shard_map.83 = (f32[144,128]{1,0:T(8,128)}, f32[24,128]{1,0:T(8,128)S(1)}, f32[24,128]{1,0:T(8,128)}, f32[128,128]{1,0:T(8,128)S(1)}) custom-call(f32[384,128]{1,0:T(8,128)S(1)} %all_to_all.66.refs_0_, f32[8,128]{1,0:T(8,128)S(1)} %get-tuple-element.37.refs_1_.refs_2_, f32[24,128]{1,0:T(8,128)S(1)} %get-tuple-element.38.refs_2_, ...), custom_call_target="tpu_custom_call" | custom-call | tf_op jit(solution)/shard_map/pallas_call | solution.py:434
  166.7 13.7 %all_to_all.82 = f32[128,1,128]{2,1,0:T(1,128)S(1)} all-to-all(f32[128,1,128]{2,1,0:T(1,128)S(1)} %bitcast.22), channel_id=1, replica_groups=mesh['cell'=4,'wide_0'=4,'wide_1'=4,'wide_2'=2] {'cell','wide_0','wide_1..., dimensions={0} | all-to-all | bytes 131072 | tf_op jit(solution)/shard_map/all_to_all | solution.py:397
  180.4 0.8 shard_map.84
  (14 shorter events, 0.1 us)
Async XLA Ops:
  0.6 0.7 copy-start.7
  0.6 0.7 copy-start.6
  1.3 0.7 copy-start
  2.0 0.7 copy-start.2
  2.7 0.7 copy-start.4
  4.7 11.5 %copy-start.8 = (f32[6,6,32]{2,1,0:T(8,128)S(1)}, f32[6,6,32]{2,1,0:T(8,128)}, u32[]{:S(2)}) copy-start(f32[6,6,32]{2,1,0:T(8,128)} %param.11) | copy-start | bytes 13828
  4.7 22.6 %all-to-all-start = ((f32[128,3,128]{2,1,0:T(4,128)}), f32[128,3,128]{2,1,0:T(4,128)S(1)}, u32[]{:S(2)}, u32[]{:S(2)}) async-start(f32[128,3,128]{2,1,0:T(4,128)} %all_to_all.49), calls=%async_computation | async-start | bytes 524288 | tf_op jit(solution)/shard_map/all_to_all | solution.py:397
  45.7 0.7 copy-start.1
  45.7 0.7 copy-start.3
  45.7 0.7 copy-start.5

commit v2 on v1

--- a/solution.py
+++ b/solution.py
@@ -24,6 +24,7 @@
 ROWS = 32
 HALO_AT = 64
 DOT_AT = 88
+BACK = 4
 BLOCKS = 6
 EDGE_OF = {-1: 3, 0: 4, 1: 5}
 ROW_OF = {-1: 1, 0: 0, 1: 2}
@@ -76,7 +77,7 @@
     return jnp.sum(jnp.sum(x, axis=1, keepdims=True), axis=0, keepdims=True)
 
 
-def forward_message(field, sums, dots, out_ref, parts):
+def forward_message(field, sums, dots, out_ref):
     lane = iota((NDEV, TILE), 1)
     stacked = jnp.concatenate(
         [jnp.zeros((HALO_AT, TILE), F32)]
@@ -88,28 +89,38 @@
     second = second + stacked.T
     for at, dot in enumerate(dots):
         second = jnp.where(lane == DOT_AT + at, dot, second)
-    out_ref[pl.ds(0, NDEV, stride=parts), :] = sums[:, :TILE]
-    out_ref[pl.ds(1, NDEV, stride=parts), :] = second
-
-
-def start_kernel(pos_ref, rhs_ref, owner_ref, row_ref, arm_ref, out_ref, onehot, high, low):
+    out_ref[pl.ds(0, NDEV, stride=2), :] = sums[:, :TILE]
+    out_ref[pl.ds(1, NDEV, stride=2), :] = second
+
+
+def start_kernel(
+    pos_hbm, rhs_hbm, owner_hbm, row_hbm, arm_hbm, out_ref, pack_ref, rhs_ref,
+    owner_ref, row_ref, sems, onehot, high, low,
+):
+    copies = [
+        pltpu.make_async_copy(source, target, sems.at[at])
+        for at, (source, target) in enumerate(
+            (
+                (rhs_hbm, rhs_ref),
+                (arm_hbm, pack_ref.at[24:48, :]),
+                (owner_hbm, owner_ref),
+                (row_hbm, row_ref),
+                (pos_hbm, pack_ref.at[0:24, :]),
+            )
+        )
+    ]
+    for copy in copies:
+        copy.start()
+    for copy in copies:
+        copy.wait()
     field = [rhs_ref[8 * c : 8 * c + 8, :] for c in range(3)]
-    arms = [arm_ref[8 * c : 8 * c + 8, :] for c in range(3)]
+    arms = [pack_ref[24 + 8 * c : 32 + 8 * c, :] for c in range(3)]
     owner, row = owner_ref[...], row_ref[...]
+    pack_ref[48:56, :] = owner.astype(F32)
+    pack_ref[56:64, :] = row.astype(F32)
     sums = body_sums(field, arms, owner, row, onehot, high, low)
     square = total(field[0] * field[0] + field[1] * field[1] + field[2] * field[2])
-    forward_message(field, sums, [square], out_ref, 3)
-    fixed = jnp.concatenate(
-        [
-            pos_ref[...],
-            arm_ref[...],
-            owner.astype(F32),
-            row.astype(F32),
-            jnp.zeros((64, TILE), F32),
-        ],
-        axis=0,
-    )
-    out_ref[pl.ds(2, NDEV, stride=3), :] = fixed.T
+    forward_message(field, sums, [square], out_ref)
 
 
 def turned(x, by):
@@ -139,11 +150,11 @@
     return jnp.broadcast_to(row[:, lane : lane + 1], (1, TILE))
 
 
-def owner_kernel(step, parts, inverse_ref, message_ref, *refs):
+def owner_kernel(step, inverse_ref, message_ref, *refs):
     states = refs[:step]
     out_ref, state_ref = refs[step:]
-    first = rows_of(message_ref, 0, parts)
-    second = rows_of(message_ref, 1, parts)
+    first = rows_of(message_ref, 0, 2)
+    second = rows_of(message_ref, 1, 2)
     sums = [jnp.sum(first, axis=0, keepdims=True), jnp.sum(second, axis=0, keepdims=True)]
     inners = [spread(sums[1], DOT_AT + 1 + i) for i in range(step)]
     square = spread(sums[1], DOT_AT)
@@ -168,19 +179,14 @@
     state_ref[...] = jnp.concatenate(
         sums + motion + [length, scale] + inners + [zero] * (2 - step), axis=0
     )
-    back = 6 if parts == 3 else 3
     for half in range(2):
-        out_ref[pl.ds(half, NDEV, stride=back), :] = jnp.broadcast_to(motion[half], (NDEV, TILE))
+        out_ref[pl.ds(half, NDEV, stride=BACK), :] = jnp.broadcast_to(motion[half], (NDEV, TILE))
     blocks = routed(second, HALO_AT, 24)
     rim = shifted(blocks[0], -HALO_AT)
     for k in range(1, 5):
         rim = rim + shifted(blocks[k], 24 * k - HALO_AT)
-    out_ref[pl.ds(2, NDEV, stride=back), :] = rim
-    if parts == 3:
-        blocks = routed(rows_of(message_ref, 2, parts), 0, 64)
-        out_ref[pl.ds(3, NDEV, stride=back), :] = blocks[0] + shifted(blocks[1], 64)
-        out_ref[pl.ds(4, NDEV, stride=back), :] = blocks[2] + shifted(blocks[3], 64)
-        out_ref[pl.ds(5, NDEV, stride=back), :] = blocks[4]
+    out_ref[pl.ds(2, NDEV, stride=BACK), :] = rim
+    out_ref[pl.ds(3, NDEV, stride=BACK), :] = jnp.zeros((NDEV, TILE), F32)
 
 
 def picked_motion(first, second, owner_ref, row_ref):
@@ -209,96 +215,127 @@
     return results
 
 
-def mobility(pos_ref, moved, source_ref):
+def source_rows(get, rows_ref):
+    for i, dx in enumerate((-1, 0, 1)):
+        for part in range(3):
+            at = 30 * part + 10 * i
+            edge = get(EDGE_OF[dx], part)
+            rows_ref[at : at + 1, :] = edge[7:8]
+            rows_ref[at + 1 : at + 9, :] = get(ROW_OF[dx], part)
+            rows_ref[at + 9 : at + 10, :] = edge[0:1]
+
+
+def sources_of(rows_ref, tile):
+    return [
+        [rows_ref[pl.ds(30 * part + 10 * i + tile + j, 8, stride=0), :] for part in range(3)]
+        for i in range(3)
+        for j in range(3)
+    ]
+
+
+def pair_kernel(
+    pack_ref, before_ref, after_ref, left_ref, right_ref,
+    pair_hbm, arm_ref, owner_ref, row_ref, rows_ref, pair_ref, sems,
+):
     sub = iota((8, TILE), 0)
 
-    def block(get, number, part):
-        return get(number, part)
-
-    def at(number, part):
-        return pos_ref[24 * number + 8 * part : 24 * number + 8 * part + 8, :]
-
-    def moved_at(number, part):
-        return moved[number][part]
-
-    for code in range(9):
-        dx, dy = code // 3 - 1, code % 3 - 1
-        for kind, get in enumerate((at, moved_at)):
-            for part in range(3):
-                x = get(ROW_OF[dx], part)
-                if dy == -1:
-                    x = jnp.where(sub == 7, get(EDGE_OF[dx], part), x)
-                    x = pltpu.roll(x, 1, 0)
-                elif dy == 1:
-                    x = jnp.where(sub == 0, get(EDGE_OF[dx], part), x)
-                    x = pltpu.roll(x, 7, 0)
-                if kind == 0 and part < 2:
-                    x = x + float((dx, dy)[part])
-                place = 24 * kind + 8 * part
-                source_ref[code, place : place + 8, :] = x
-    target = [at(0, part) for part in range(3)]
-    unroll = 8
-
-    def of_code(code, sums):
-        source = [source_ref[code, 8 * k : 8 * k + 8, :] for k in range(6)]
-
-        def of_turn(turn, sums):
-            for k in range(unroll):
-                there = [pltpu.roll(s, turn * unroll + k, 1) for s in source]
-                sep = [target[a] - there[a] for a in range(3)]
+    def get(block, part):
+        if block < 3:
+            ref = (pack_ref, before_ref, after_ref)[block]
+            return ref[8 * part : 8 * part + 8, :]
+        at = 8 * (block - 3) + part
+        left, right = left_ref[at : at + 1, :], right_ref[at : at + 1, :]
+        return jnp.where(sub == 7, left, jnp.where(sub == 0, right, 0.0))
+
+    for block in range(BLOCKS):
+        for part in range(3):
+            place = 24 * block + 8 * part
+            arm_ref[place : place + 8, :] = get(block, 3 + part)
+        owner_ref[8 * block : 8 * block + 8, :] = get(block, 6).astype(jnp.int32)
+        row_ref[8 * block : 8 * block + 8, :] = get(block, 7).astype(jnp.int32)
+    source_rows(get, rows_ref)
+    columns = jnp.concatenate([pack_ref[0:24, :], jnp.zeros((104, TILE), F32)], axis=0).T
+
+    def of_tile(tile, carry):
+        turned_columns = pltpu.roll(columns, TILE - tile, 1)
+        sources = sources_of(rows_ref, tile)
+        for k in range(9):
+            for part, step in ((0, k // 3 - 1), (1, k % 3 - 1)):
+                if step != 0:
+                    sources[k][part] = sources[k][part] + float(step)
+        for group in range(TILE // 8):
+            rows = turned_columns[8 * group : 8 * group + 8]
+            target = [jnp.broadcast_to(rows[:, 8 * a : 8 * a + 1], (8, TILE)) for a in range(3)]
+            for k in range(9):
+                sep = [target[a] - sources[k][a] for a in range(3)]
                 soft = sep[0] * sep[0] + sep[1] * sep[1] + (sep[2] * sep[2] + EPS2)
                 root = lax.rsqrt(soft)
-                inverse = root * root * root
-                near = root + EPS2 * inverse
-                along = sep[0] * there[3] + sep[1] * there[4] + sep[2] * there[5]
-                along = along * inverse
-                sums = tuple(
-                    sums[a] + (near * there[3 + a] + along * sep[a]) for a in range(3)
-                )
-            return sums
-
-        return lax.fori_loop(0, TILE // unroll, of_turn, sums)
-
-    zero = jnp.zeros((8, TILE), F32)
-    return lax.fori_loop(0, 9, of_code, (zero, zero, zero))
+                square = root * root
+                pair_ref[tile, group, k, 0] = root + EPS2 * (square * root)
+                scale = square * lax.rsqrt(root)
+                for a in range(3):
+                    pair_ref[tile, group, k, 1 + a] = sep[a] * scale
+        pltpu.make_async_copy(pair_ref.at[tile], pair_hbm.at[tile], sems.at[tile]).start()
+        return carry
+
+    lax.fori_loop(0, TY, of_tile, 0)
+    for tile in range(TY):
+        pltpu.make_async_copy(pair_ref.at[tile], pair_hbm.at[tile], sems.at[tile]).wait()
+
+
+def mobility(pair_ref, moved, rows_ref, pairs_ref, arrive):
+    source_rows(lambda block, part: moved[block][part], rows_ref)
+
+    def of_tile(tile, carry):
+        arrive(tile)
+        sources = sources_of(rows_ref, tile)
+        sums = [[], [], []]
+        for group in range(TILE // 8):
+            terms = None
+            for k in range(9):
+                near = pair_ref[tile, group, k, 0]
+                sep = [pair_ref[tile, group, k, 1 + a] for a in range(3)]
+                force = sources[k]
+                along = sep[0] * force[0] + sep[1] * force[1] + sep[2] * force[2]
+                term = [near * force[a] + along * sep[a] for a in range(3)]
+                terms = term if terms is None else [terms[a] + term[a] for a in range(3)]
+            for a in range(3):
+                sums[a].append(terms[a])
+        for a in range(3):
+            across = jnp.concatenate(sums[a], axis=0).T
+            pairs_ref[pl.ds(8 * a + tile, 1), :] = jnp.sum(across, axis=0, keepdims=True)
+        return carry
+
+    lax.fori_loop(0, TY, of_tile, 0, unroll=2)
+    return [pairs_ref[8 * a : 8 * a + 8, :] for a in range(3)]
 
 
 def local_kernel(step, *refs):
     refs = list(refs)
     take = lambda n: [refs.pop(0) for _ in range(n)]
     message_ref, state_ref, field_ref = take(3)
-    back = 6 if step == 0 else 3
+    pair_ref, arm_ref, owner_ref, row_ref = take(4)
+    bases = take(step)
+    basis_ref, moved_ref, fresh_ref, out_ref = take(4)
+    rows_ref, pairs_ref, onehot, high, low = take(5)
+    arrive = lambda tile: None
     if step == 0:
-        own_pos, own_arm, own_owner, own_row = take(4)
-    else:
-        pos_ref, arm_ref, owner_ref, row_ref = take(4)
-    bases = take(step)
-    if step == 0:
-        pos_ref, arm_ref, owner_ref, row_ref = take(4)
-    basis_ref, moved_ref, fresh_ref, out_ref = take(4)
-    source_ref, onehot, high, low = take(4)
-    if step == 0:
-        near = rows_of(message_ref, 3, back).T
-        edge = rows_of(message_ref, 4, back).T
-        last = rows_of(message_ref, 5, back).T
-        fixed = [near[:64], near[64:], edge[:64], edge[64:], last[:64]]
-        pos_ref[0:24, :] = own_pos[...]
-        arm_ref[0:24, :] = own_arm[...]
-        owner_ref[0:8, :] = own_owner[...]
-        row_ref[0:8, :] = own_row[...]
-        for k in range(5):
-            pos_ref[24 * (k + 1) : 24 * (k + 2), :] = fixed[k][0:24]
-            arm_ref[24 * (k + 1) : 24 * (k + 2), :] = fixed[k][24:48]
-            owner_ref[8 * (k + 1) : 8 * (k + 2), :] = fixed[k][48:56].astype(jnp.int32)
-            row_ref[8 * (k + 1) : 8 * (k + 2), :] = fixed[k][56:64].astype(jnp.int32)
-    rim = rows_of(message_ref, 2, back).T
+        pair_hbm = pair_ref
+        pair_ref, sems = take(2)
+        fetch = lambda tile: pltpu.make_async_copy(
+            pair_hbm.at[tile], pair_ref.at[tile], sems.at[tile]
+        )
+        for tile in range(TY):
+            fetch(tile).start()
+        arrive = lambda tile: fetch(tile).wait()
+    rim = rows_of(message_ref, 2, BACK).T
     basis = jnp.concatenate([field_ref[...], rim[:120]], axis=0)
     for i in range(step):
         basis = basis - state_ref[6 + i : 7 + i, :] * bases[i][...]
     basis = basis * state_ref[5:6, :]
     basis_ref[...] = basis
     motions = picked_motion(
-        rows_of(message_ref, 0, back), rows_of(message_ref, 1, back), owner_ref, row_ref
+        rows_of(message_ref, 0, BACK), rows_of(message_ref, 1, BACK), owner_ref, row_ref
     )
     moved = []
     for block in range(BLOCKS):
@@ -311,7 +348,7 @@
                 for a in range(3)
             ]
         )
-    pairs = mobility(pos_ref, moved, source_ref)
+    pairs = mobility(pair_ref, moved, rows_ref, pairs_ref, arrive)
     fresh = [moved[0][a] + FACTOR * pairs[a] for a in range(3)]
     for a in range(3):
         moved_ref[8 * a : 8 * a + 8, :] = moved[0][a]
@@ -329,7 +366,7 @@
         sums = body_sums(
             fresh, arms, owner_ref[0:8, :], row_ref[0:8, :], onehot, high, low
         )
-        forward_message(fresh, sums, dots, out_ref, 2)
+        forward_message(fresh, sums, dots, out_ref)
     else:
         lane = iota((NDEV, TILE), 1)
         message = jnp.zeros((NDEV, TILE), F32)
@@ -370,6 +407,10 @@
         motion_ref[part : part + 1, :] = whole[:, at : at + ROWS]
 
 
+HBM = pl.BlockSpec(memory_space=pltpu.HBM)
+VMEM = pl.BlockSpec(memory_space=pltpu.VMEM)
+
+
 def f32(*shape):
     return jax.ShapeDtypeStruct(shape, F32)
 
@@ -378,7 +419,7 @@
     return jax.ShapeDtypeStruct(shape, jnp.int32)
 
 
-PARAMS = pltpu.CompilerParams(vmem_limit_bytes=24 * 1024 * 1024)
+PAIRS = (TY, TILE // 8, 9, 4, 8, TILE)
 
 
 def sums_scratch():
@@ -389,12 +430,31 @@
     ]
 
 
-def call(body, out, scratch=()):
-    return pl.pallas_call(body, out_shape=out, scratch_shapes=list(scratch), compiler_params=PARAMS)
+def call(body, out, scratch=(), mib=16, **options):
+    return pl.pallas_call(
+        body,
+        out_shape=out,
+        scratch_shapes=list(scratch),
+        compiler_params=pltpu.CompilerParams(vmem_limit_bytes=mib * 1024 * 1024),
+        **options,
+    )
 
 
 def exchange(message):
     return lax.all_to_all(message, CELL_WIDE, split_axis=0, concat_axis=0, tiled=True)
+
+
+def ring(array, axes, step):
+    count = lax.axis_size(axes)
+    return lax.ppermute(array, axes, [(i, (i + step) % count) for i in range(count)])
+
+
+def rims(pack):
+    before, after = ring(pack, "cell", 1), ring(pack, "cell", -1)
+    rows = [x.reshape(8, TY, TILE) for x in (before, pack, after)]
+    last = jnp.concatenate([x[:, TY - 1] for x in rows], axis=0)
+    first = jnp.concatenate([x[:, 0] for x in rows], axis=0)
+    return before, after, ring(last, WIDE, 1), ring(first, WIDE, -1)
 
 
 def local(positions, rhs, blob_owner, blob_row, blob_arm, body_inverse):
@@ -406,39 +466,60 @@
     inverse = jnp.transpose(body_inverse, (1, 0, 2)).reshape(6, 6 * ROWS)
     inverse = jnp.pad(inverse, ((0, 2), (0, 64)))
     inverse = jnp.concatenate([inverse[:, :TILE], inverse[:, TILE:]], axis=0)
-    message = call(start_kernel, f32(3 * NDEV, TILE), sums_scratch())(pos, field, owner, row, arm)
-    fixed = (pos, arm, owner, row)
+    message, pack, field = call(
+        start_kernel,
+        (f32(2 * NDEV, TILE), f32(64, TILE), f32(24, TILE)),
+        [
+            pltpu.VMEM((TY, TILE), jnp.int32),
+            pltpu.VMEM((TY, TILE), jnp.int32),
+            pltpu.SemaphoreType.DMA((5,)),
+        ]
+        + sums_scratch(),
+        in_specs=[HBM] * 5,
+    )(*[pltpu.with_memory_space_constraint(x, pltpu.HBM) for x in (pos, field, owner, row, arm)])
+    before, after, left, right = rims(pack)
+    arrived, left, right = lax.optimization_barrier((exchange(message), left, right))
+    pair_count = 9 * TY * TILE * TILE
+    pairs, *fixed = call(
+        pair_kernel,
+        (
+            f32(*PAIRS),
+            f32(24 * BLOCKS, TILE),
+            i32(8 * BLOCKS, TILE),
+            i32(8 * BLOCKS, TILE),
+        ),
+        [pltpu.VMEM((96, TILE), F32), pltpu.VMEM(PAIRS, F32), pltpu.SemaphoreType.DMA((TY,))],
+        mib=40,
+        out_specs=(HBM, VMEM, VMEM, VMEM),
+        cost_estimate=pl.CostEstimate(
+            flops=20 * pair_count, transcendentals=2 * pair_count, bytes_accessed=16 * pair_count
+        ),
+    )(pack, before, after, left, right)
     states, bases, moveds = [], [], []
     for step in range(ITERS):
-        parts = 3 if step == 0 else 2
-        back = 6 if step == 0 else 3
-        arrived = exchange(message)
+        if step > 0:
+            arrived = exchange(message)
         message, state = call(
-            lambda *refs, step=step, parts=parts: owner_kernel(step, parts, *refs),
-            (f32(back * NDEV, TILE), f32(8, TILE)),
+            lambda *refs, step=step: owner_kernel(step, *refs),
+            (f32(BACK * NDEV, TILE), f32(8, TILE)),
         )(inverse, arrived, *states)
         arrived = exchange(message)
-        outs = [
-            f32(24 * BLOCKS, TILE),
-            f32(24, TILE),
-            f32(24, TILE),
-            f32(NDEV if step == ITERS - 1 else 2 * NDEV, TILE),
-        ]
+        basis, moved, field, message = call(
+            lambda *refs, step=step: local_kernel(step, *refs),
+            (
+                f32(24 * BLOCKS, TILE),
+                f32(24, TILE),
+                f32(24, TILE),
+                f32(NDEV if step == ITERS - 1 else 2 * NDEV, TILE),
+            ),
+            [pltpu.VMEM((96, TILE), F32), pltpu.VMEM((24, TILE), F32)]
+            + sums_scratch()
+            + ([pltpu.VMEM(PAIRS, F32), pltpu.SemaphoreType.DMA((TY,))] if step == 0 else []),
+            mib=40 if step == 0 else 16,
+            in_specs=[VMEM] * 3 + [HBM if step == 0 else VMEM] + [VMEM] * (3 + step),
+        )(arrived, state, field, pairs, *fixed, *bases)
         if step == 0:
-            outs = [
-                f32(24 * BLOCKS, TILE),
-                f32(24 * BLOCKS, TILE),
-                i32(8 * BLOCKS, TILE),
-                i32(8 * BLOCKS, TILE),
-            ] + outs
-        results = call(
-            lambda *refs, step=step: local_kernel(step, *refs),
-            tuple(outs),
-            [pltpu.VMEM((9, 48, TILE), F32)] + sums_scratch(),
-        )(arrived, state, field, *fixed, *bases)
-        if step == 0:
-            fixed = results[:4]
-        basis, moved, field, message = results[-4:]
+            pairs = pltpu.with_memory_space_constraint(pairs, pltpu.VMEM)
         states.append(state)
         bases.append(basis)
         moveds.append(moved)

time: 182 us -> 141 us (0.77)
  Pallas kernels: 62 us -> 30.4 us
  blocking collectives: 91 us -> 74.5 us
  starting transfers between devices: 11.5 us -> 23.2 us
  local copies, waits for them, and re-layouts: 4.91 us -> 0.85 us
    pallas_call x7 -> x8, Pallas kernels: 61.3 us -> 29.6 us  [the longest x3 19 us: local(): call(lambda *refs, step=step: local_kernel(step, *refs), (f32(24 * BLOCKS...]
    all_to_all x6 -> x5, blocking collectives: 91 us -> 74.5 us  [exchange(): lax.all_to_all(message, CELL_WIDE, split_axis=0, concat_axis=0, tiled=True)]
    ppermute x0 -> x4, starting transfers between devices: none -> 6.37 us  [ring(): lax.ppermute(array, axes, [(i, (i + step) % count) for i in range(count)])]
    all_to_all x1 -> x2, starting transfers between devices: 11.5 us -> 16.8 us  [exchange(): lax.all_to_all(message, CELL_WIDE, split_axis=0, concat_axis=0, tiled=True)]
    unnamed x18 -> x2, local copies, waits for them, and re-layouts: 3.5 us -> 0.01 us
    ppermute x0 -> x4, waiting for transfers between devices: none -> 3.41 us  [ring(): lax.ppermute(array, axes, [(i, (i + step) % count) for i in range(count)])]
    all_to_all x1 -> x2, waiting for transfers between devices: 11 us -> 7.89 us  [exchange(): lax.all_to_all(message, CELL_WIDE, split_axis=0, concat_axis=0, tiled=True)]
  transfers between devices with their start and end apart: 1 -> 6, of which waited for: 1 -> 4; matrix products, arithmetic and copies ran while one was open for 0% -> 1% of each run, Pallas kernels for 0% -> 5%
where the time goes in v2:
time: 141 us
  blocking collectives  74.5 us (53%)
  Pallas kernels  30.4 us (22%)
  starting transfers between devices  23.2 us (16%)
  waiting for transfers between devices  11.3 us (8%)
    all_to_all x5, blocking collectives, exchange(): lax.all_to_all(message, CELL_WIDE, split_axis=0, concat_axis=0, tiled=True)  74.5 us
    pallas_call x3, Pallas kernels, local(): call(lambda *refs, step=step: local_kernel(step, *refs), (f32(24 * BLOCKS...  19 us
    all_to_all x2, starting transfers between devices, exchange(): lax.all_to_all(message, CELL_WIDE, split_axis=0, concat_axis=0, tiled=True)  16.8 us
    all_to_all x2, waiting for transfers between devices, exchange(): lax.all_to_all(message, CELL_WIDE, split_axis=0, concat_axis=0, tiled=True)  7.89 us
    pallas_call x1, Pallas kernels, local(): call(pair_kernel, (f32(*PAIRS), f32(24 * BLOCKS, TILE), i32(8 * BLOCKS, T...  7.19 us
    ppermute x4, starting transfers between devices, ring(): lax.ppermute(array, axes, [(i, (i + step) % count) for i in range(count)])  6.37 us
    ppermute x4, waiting for transfers between devices, ring(): lax.ppermute(array, axes, [(i, (i + step) % count) for i in range(count)])  3.41 us
  transfers between devices with their start and end apart: 6, of which 4 were waited for; matrix products, arithmetic and copies ran while one was open for 1% of the time, Pallas kernels for 5%

profile of v2, /device:TPU:1, one launch (start us, length us, event | category | flops | bytes accessed | tf_op | source)
XLA Modules:
  0.0 141.0 jit_solution(12248840399261177142)
XLA Ops:
  0.6 1.9 %shard_map.77 = (f32[256,128]{1,0:T(8,128)}, f32[64,128]{1,0:T(8,128)S(1)}, f32[24,128]{1,0:T(8,128)S(1)}) custom-call(f32[24,128]{1,0:T(8,128)} %bitcast.68, f32[24,128]{1,0:T(8,128)} %bitcast.69, s32[8,128]{1,0:T(8,128)} %bitcast.71, s32[8,128]{1,0:T(8,128)} %bitcast.72, f32[24,128]{1,0:T(8,128)} %bitcast.70), custom_call_target="tpu_custom_call" | custom-call | tf_op jit(solution)/shard_map/pallas_call | solution.py:469
  2.6 4.7 %collective-permute-start.1 = (f32[64,128]{1,0:T(8,128)S(1)}, f32[64,128]{1,0:T(8,128)S(1)}, u32[]{:S(2)}, u32[]{:S(2)}) collective-permute-start(f32[64,128]{1,0:T(8,128)S(1)} %get-tuple-element.31.pack_ref), channel_id=1, source_target_pairs={{0,96},{32,0},{64,32},{96,64},{1,97},{33,1},{65,33},{97,65},{2,98}... | collective-permute-start | bytes 98312 | tf_op jit(solution)/shard_map/ppermute | solution.py:449
  7.2 0.0 collective-permute-start
  7.2 10.1 %all-to-all-start = ((f32[128,2,128]{2,1,0:T(2,128)}), f32[128,2,128]{2,1,0:T(2,128)S(1)}, u32[]{:S(2)}, u32[]{:S(2)}) async-start(f32[128,2,128]{2,1,0:T(2,128)} %bitcast.6), calls=%async_computation | async-start | bytes 262144 | tf_op jit(solution)/shard_map/all_to_all | solution.py:444
  17.4 0.7 copy.18
  18.1 0.1 reshape.48
  18.2 0.0 collective-permute-done.1.after_ref
  18.2 0.0 collective-permute-done.before_ref
  18.3 1.7 %collective-permute-start.2 = (f32[24,128]{1,0:T(8,128)S(1)}, f32[24,128]{1,0:T(8,128)S(1)}, u32[]{:S(2)}, u32[]{:S(2)}) collective-permute-start(f32[24,128]{1,0:T(8,128)S(1)} %pad_maximum_fusion), channel_id=1, source_target_pairs={{0,1},{1,2},{2,3},{3,4},{4,5},{5,6},{6,7},{7,8},{8,9},{9,10},{10,1... | collective-permute-start | bytes 36872 | tf_op jit(solution)/shard_map/ppermute | solution.py:449
  20.0 0.0 collective-permute-start.3
  20.0 0.8 collective-permute-done.2.left_ref
  20.8 2.6 %collective-permute-done.3.right_ref = f32[24,128]{1,0:T(8,128)S(1)} collective-permute-done((f32[24,128]{1,0:T(8,128)S(1)}, f32[24,128]{1,0:T(8,128)S(1)}, u32[]{:S(2)}, u32[]{:S(2)}) %collective-permute-start.3) | collective-permute-done | bytes 12320 | tf_op jit(solution)/shard_map/ppermute | solution.py:449
  23.4 4.0 %all-to-all-done = f32[128,2,128]{2,1,0:T(2,128)S(1)} async-done(((f32[128,2,128]{2,1,0:T(2,128)}), f32[128,2,128]{2,1,0:T(2,128)S(1)}, u32[]{:S(2)}, u32[]{:S(2)}) %all-to-all-start) | async-done | bytes 131104 | tf_op jit(solution)/shard_map/all_to_all | solution.py:444
  27.4 1.0 shard_map.78
  28.4 6.7 %all-to-all-start.1 = ((f32[128,4,128]{2,1,0:T(4,128)}), f32[128,4,128]{2,1,0:T(4,128)S(1)}, u32[]{:S(2)}, u32[]{:S(2)}) async-start(f32[128,4,128]{2,1,0:T(4,128)} %bitcast.17), calls=%async_computation.1 | async-start | bytes 524288 | tf_op jit(solution)/shard_map/all_to_all | solution.py:444
  35.1 7.2 %shard_map.79 = (f32[8,16,9,4,8,128]{5,4,3,2,1,0:T(8,128)}, f32[144,128]{1,0:T(8,128)S(1)}, s32[48,128]{1,0:T(8,128)S(1)}, s32[48,128]{1,0:T(8,128)S(1)}) custom-call(f32[64,128]{1,0:T(8,128)S(1)} %get-tuple-element.31.pack_ref, f32[64,128]{1,0:T(8,128)S(1)} %collective-permute-done.before_ref, f32[64,128]{1,0:T(8,128)S(1)} %collective-permute-done.1.after_ref, ...), custom_call_target="tpu_custom_call" | custom-call | flops 23592960 | bytes 18874368 | tf_op jit(solution)/shard_map/pallas_call | solution.py:483
  42.3 3.9 %all-to-all-done.1 = f32[128,4,128]{2,1,0:T(4,128)S(1)} async-done(((f32[128,4,128]{2,1,0:T(4,128)}), f32[128,4,128]{2,1,0:T(4,128)S(1)}, u32[]{:S(2)}, u32[]{:S(2)}) %all-to-all-start.1) | async-done | bytes 262176 | tf_op jit(solution)/shard_map/all_to_all | solution.py:444
  46.2 0.0 copy-start
  46.2 8.6 %shard_map.80 = (f32[144,128]{1,0:T(8,128)S(1)}, f32[24,128]{1,0:T(8,128)S(1)}, f32[24,128]{1,0:T(8,128)S(1)}, f32[256,128]{1,0:T(8,128)S(1)}) custom-call(f32[512,128]{1,0:T(8,128)S(1)} %bitcast.46, f32[8,128]{1,0:T(8,128)S(1)} %get-tuple-element.34.refs_1_.refs_2_.refs_0_, f32[24,128]{1,0:T(8,128)S(1)} %get-tuple-element.35.refs_2_, ...), custom_call_target="tpu_custom_call" | custom-call | tf_op jit(solution)/shard_map/pallas_call | solution.py:507
  54.7 15.8 %all_to_all.78 = f32[128,2,128]{2,1,0:T(2,128)S(1)} all-to-all(f32[128,2,128]{2,1,0:T(2,128)S(1)} %bitcast.55), channel_id=1, replica_groups=mesh['cell'=4,'wide_0'=4,'wide_1'=4,'wide_2'=2] {'cell','wide_0','wide_1..., dimensions={0} | all-to-all | bytes 262144 | tf_op jit(solution)/shard_map/all_to_all | solution.py:444
  70.6 0.3 shard_map.81
  70.8 15.3 %all_to_all.79 = f32[128,4,128]{2,1,0:T(4,128)S(1)} all-to-all(f32[128,4,128]{2,1,0:T(4,128)S(1)} %bitcast.54), channel_id=1, replica_groups=mesh['cell'=4,'wide_0'=4,'wide_1'=4,'wide_2'=2] {'cell','wide_0','wide_1..., dimensions={0} | all-to-all | bytes 524288 | tf_op jit(solution)/shard_map/all_to_all | solution.py:444
  86.2 0.0 copy-done
  86.2 5.3 %shard_map.82 = (f32[144,128]{1,0:T(8,128)S(1)}, f32[24,128]{1,0:T(8,128)S(1)}, f32[24,128]{1,0:T(8,128)S(1)}, f32[256,128]{1,0:T(8,128)S(1)}) custom-call(f32[512,128]{1,0:T(8,128)S(1)} %bitcast.48, f32[8,128]{1,0:T(8,128)S(1)} %get-tuple-element.44.refs_1_.refs_3_, f32[24,128]{1,0:T(8,128)S(1)} %get-tuple-element.45.refs_2_, ...), custom_call_target="tpu_custom_call" | custom-call | tf_op jit(solution)/shard_map/pallas_call | solution.py:507
  91.4 14.3 %all_to_all.80 = f32[128,2,128]{2,1,0:T(2,128)S(1)} all-to-all(f32[128,2,128]{2,1,0:T(2,128)S(1)} %bitcast.56), channel_id=1, replica_groups=mesh['cell'=4,'wide_0'=4,'wide_1'=4,'wide_2'=2] {'cell','wide_0','wide_1..., dimensions={0} | all-to-all | bytes 262144 | tf_op jit(solution)/shard_map/all_to_all | solution.py:444
  105.7 0.3 shard_map.83
  106.0 15.2 %all_to_all.81 = f32[128,4,128]{2,1,0:T(4,128)S(1)} all-to-all(f32[128,4,128]{2,1,0:T(4,128)S(1)} %bitcast.53), channel_id=1, replica_groups=mesh['cell'=4,'wide_0'=4,'wide_1'=4,'wide_2'=2] {'cell','wide_0','wide_1..., dimensions={0} | all-to-all | bytes 524288 | tf_op jit(solution)/shard_map/all_to_all | solution.py:444
  121.1 5.2 %shard_map.84 = (f32[144,128]{1,0:T(8,128)}, f32[24,128]{1,0:T(8,128)S(1)}, f32[24,128]{1,0:T(8,128)}, f32[128,128]{1,0:T(8,128)S(1)}) custom-call(f32[512,128]{1,0:T(8,128)S(1)} %bitcast.47, f32[8,128]{1,0:T(8,128)S(1)} %get-tuple-element.49.refs_1_.refs_2_, f32[24,128]{1,0:T(8,128)S(1)} %get-tuple-element.50.refs_2_, ...), custom_call_target="tpu_custom_call" | custom-call | tf_op jit(solution)/shard_map/pallas_call | solution.py:507
  126.3 13.9 %all_to_all.82 = f32[128,1,128]{2,1,0:T(1,128)S(1)} all-to-all(f32[128,1,128]{2,1,0:T(1,128)S(1)} %bitcast.57), channel_id=1, replica_groups=mesh['cell'=4,'wide_0'=4,'wide_1'=4,'wide_2'=2] {'cell','wide_0','wide_1..., dimensions={0} | all-to-all | bytes 131072 | tf_op jit(solution)/shard_map/all_to_all | solution.py:444
  140.2 0.8 shard_map.85
  (7 shorter events, 0.0 us)
Async XLA Ops:
  2.6 15.7 %collective-permute-start.1 = (f32[64,128]{1,0:T(8,128)S(1)}, f32[64,128]{1,0:T(8,128)S(1)}, u32[]{:S(2)}, u32[]{:S(2)}) collective-permute-start(f32[64,128]{1,0:T(8,128)S(1)} %get-tuple-element.31.pack_ref), channel_id=1, source_target_pairs={{0,96},{32,0},{64,32},{96,64},{1,97},{33,1},{65,33},{97,65},{2,98}... | collective-permute-start | bytes 98312 | tf_op jit(solution)/shard_map/ppermute | solution.py:449
  7.2 11.0 %collective-permute-start = (f32[64,128]{1,0:T(8,128)S(1)}, f32[64,128]{1,0:T(8,128)S(1)}, u32[]{:S(2)}, u32[]{:S(2)}) collective-permute-start(f32[64,128]{1,0:T(8,128)S(1)} %get-tuple-element.31.pack_ref), channel_id=1, source_target_pairs={{0,32},{32,64},{64,96},{96,0},{1,33},{33,65},{65,97},{97,1},{2,34}... | collective-permute-start | bytes 98312 | tf_op jit(solution)/shard_map/ppermute | solution.py:449
  7.2 20.2 %all-to-all-start = ((f32[128,2,128]{2,1,0:T(2,128)}), f32[128,2,128]{2,1,0:T(2,128)S(1)}, u32[]{:S(2)}, u32[]{:S(2)}) async-start(f32[128,2,128]{2,1,0:T(2,128)} %bitcast.6), calls=%async_computation | async-start | bytes 262144 | tf_op jit(solution)/shard_map/all_to_all | solution.py:444
  18.3 2.5 %collective-permute-start.2 = (f32[24,128]{1,0:T(8,128)S(1)}, f32[24,128]{1,0:T(8,128)S(1)}, u32[]{:S(2)}, u32[]{:S(2)}) collective-permute-start(f32[24,128]{1,0:T(8,128)S(1)} %pad_maximum_fusion), channel_id=1, source_target_pairs={{0,1},{1,2},{2,3},{3,4},{4,5},{5,6},{6,7},{7,8},{8,9},{9,10},{10,1... | collective-permute-start | bytes 36872 | tf_op jit(solution)/shard_map/ppermute | solution.py:449
  20.0 3.4 %collective-permute-start.3 = (f32[24,128]{1,0:T(8,128)S(1)}, f32[24,128]{1,0:T(8,128)S(1)}, u32[]{:S(2)}, u32[]{:S(2)}) collective-permute-start(f32[24,128]{1,0:T(8,128)S(1)} %pad_maximum_fusion.1), channel_id=1, source_target_pairs={{0,31},{1,0},{2,1},{3,2},{4,3},{5,4},{6,5},{7,6},{8,7},{9,8},{10,9... | collective-permute-start | bytes 36872 | tf_op jit(solution)/shard_map/ppermute | solution.py:449
  28.4 17.8 %all-to-all-start.1 = ((f32[128,4,128]{2,1,0:T(4,128)}), f32[128,4,128]{2,1,0:T(4,128)S(1)}, u32[]{:S(2)}, u32[]{:S(2)}) async-start(f32[128,4,128]{2,1,0:T(4,128)} %bitcast.17), calls=%async_computation.1 | async-start | bytes 524288 | tf_op jit(solution)/shard_map/all_to_all | solution.py:444
  46.2 40.0 %copy-start = (f32[8,16,9,4,8,128]{5,4,3,2,1,0:T(8,128)S(1)}, f32[8,16,9,4,8,128]{5,4,3,2,1,0:T(8,128)}, u32[]{:S(2)}) copy-start(f32[8,16,9,4,8,128]{5,4,3,2,1,0:T(8,128)} %get-tuple-element.38.refs_3_) | copy-start | bytes 56623108

commit v3 on v2

--- a/solution.py
+++ b/solution.py
@@ -24,10 +24,14 @@
 ROWS = 32
 HALO_AT = 64
 DOT_AT = 88
+FIRST = 4
 BACK = 4
+FIXED = 56
 BLOCKS = 6
 EDGE_OF = {-1: 3, 0: 4, 1: 5}
 ROW_OF = {-1: 1, 0: 0, 1: 2}
+EDGES_AT = 64
+EDGE_STEP = (1, 0, 2)
 
 
 def iota(shape, axis):
@@ -77,7 +81,7 @@
     return jnp.sum(jnp.sum(x, axis=1, keepdims=True), axis=0, keepdims=True)
 
 
-def forward_message(field, sums, dots, out_ref):
+def forward_message(field, sums, dots, out_ref, parts):
     lane = iota((NDEV, TILE), 1)
     stacked = jnp.concatenate(
         [jnp.zeros((HALO_AT, TILE), F32)]
@@ -89,8 +93,8 @@
     second = second + stacked.T
     for at, dot in enumerate(dots):
         second = jnp.where(lane == DOT_AT + at, dot, second)
-    out_ref[pl.ds(0, NDEV, stride=2), :] = sums[:, :TILE]
-    out_ref[pl.ds(1, NDEV, stride=2), :] = second
+    out_ref[pl.ds(0, NDEV, stride=parts), :] = sums[:, :TILE]
+    out_ref[pl.ds(1, NDEV, stride=parts), :] = second
 
 
 def start_kernel(
@@ -116,11 +120,13 @@
     field = [rhs_ref[8 * c : 8 * c + 8, :] for c in range(3)]
     arms = [pack_ref[24 + 8 * c : 32 + 8 * c, :] for c in range(3)]
     owner, row = owner_ref[...], row_ref[...]
-    pack_ref[48:56, :] = owner.astype(F32)
-    pack_ref[56:64, :] = row.astype(F32)
+    pack_ref[48:56, :] = (owner * ROWS + row).astype(F32)
+    pack_ref[56:128, :] = jnp.zeros((72, TILE), F32)
     sums = body_sums(field, arms, owner, row, onehot, high, low)
     square = total(field[0] * field[0] + field[1] * field[1] + field[2] * field[2])
-    forward_message(field, sums, [square], out_ref)
+    forward_message(field, sums, [square], out_ref, FIRST)
+    out_ref[pl.ds(2, NDEV, stride=FIRST), :] = pack_ref[...].T
+    out_ref[pl.ds(3, NDEV, stride=FIRST), :] = jnp.zeros((NDEV, TILE), F32)
 
 
 def turned(x, by):
@@ -153,8 +159,9 @@
 def owner_kernel(step, inverse_ref, message_ref, *refs):
     states = refs[:step]
     out_ref, state_ref = refs[step:]
-    first = rows_of(message_ref, 0, 2)
-    second = rows_of(message_ref, 1, 2)
+    parts = FIRST if step == 0 else 2
+    first = rows_of(message_ref, 0, parts)
+    second = rows_of(message_ref, 1, parts)
     sums = [jnp.sum(first, axis=0, keepdims=True), jnp.sum(second, axis=0, keepdims=True)]
     inners = [spread(sums[1], DOT_AT + 1 + i) for i in range(step)]
     square = spread(sums[1], DOT_AT)
@@ -179,14 +186,21 @@
     state_ref[...] = jnp.concatenate(
         sums + motion + [length, scale] + inners + [zero] * (2 - step), axis=0
     )
-    for half in range(2):
-        out_ref[pl.ds(half, NDEV, stride=BACK), :] = jnp.broadcast_to(motion[half], (NDEV, TILE))
+    sent = [jnp.broadcast_to(m, (NDEV, TILE)) for m in motion]
     blocks = routed(second, HALO_AT, 24)
     rim = shifted(blocks[0], -HALO_AT)
     for k in range(1, 5):
         rim = rim + shifted(blocks[k], 24 * k - HALO_AT)
-    out_ref[pl.ds(2, NDEV, stride=BACK), :] = rim
-    out_ref[pl.ds(3, NDEV, stride=BACK), :] = jnp.zeros((NDEV, TILE), F32)
+    sent.append(rim)
+    if step == 0:
+        blocks = routed(rows_of(message_ref, 2, parts), 0, FIXED)
+        for k in range(3):
+            sent[1] = sent[1] + shifted(blocks[2 + k], EDGES_AT + 2 * EDGE_STEP[k])
+        sent.append(blocks[0] + shifted(blocks[1], 64))
+    else:
+        sent.append(jnp.zeros((NDEV, TILE), F32))
+    for part in range(BACK):
+        out_ref[pl.ds(part, NDEV, stride=BACK), :] = sent[part]
 
 
 def picked_motion(first, second, owner_ref, row_ref):
@@ -233,68 +247,17 @@
     ]
 
 
-def pair_kernel(
-    pack_ref, before_ref, after_ref, left_ref, right_ref,
-    pair_hbm, arm_ref, owner_ref, row_ref, rows_ref, pair_ref, sems,
-):
-    sub = iota((8, TILE), 0)
-
-    def get(block, part):
-        if block < 3:
-            ref = (pack_ref, before_ref, after_ref)[block]
-            return ref[8 * part : 8 * part + 8, :]
-        at = 8 * (block - 3) + part
-        left, right = left_ref[at : at + 1, :], right_ref[at : at + 1, :]
-        return jnp.where(sub == 7, left, jnp.where(sub == 0, right, 0.0))
-
-    for block in range(BLOCKS):
-        for part in range(3):
-            place = 24 * block + 8 * part
-            arm_ref[place : place + 8, :] = get(block, 3 + part)
-        owner_ref[8 * block : 8 * block + 8, :] = get(block, 6).astype(jnp.int32)
-        row_ref[8 * block : 8 * block + 8, :] = get(block, 7).astype(jnp.int32)
-    source_rows(get, rows_ref)
-    columns = jnp.concatenate([pack_ref[0:24, :], jnp.zeros((104, TILE), F32)], axis=0).T
+def mobility(moved, rows_ref, pairs_ref, pair_at):
+    source_rows(lambda block, part: moved[block][part], rows_ref)
 
     def of_tile(tile, carry):
-        turned_columns = pltpu.roll(columns, TILE - tile, 1)
-        sources = sources_of(rows_ref, tile)
-        for k in range(9):
-            for part, step in ((0, k // 3 - 1), (1, k % 3 - 1)):
-                if step != 0:
-                    sources[k][part] = sources[k][part] + float(step)
-        for group in range(TILE // 8):
-            rows = turned_columns[8 * group : 8 * group + 8]
-            target = [jnp.broadcast_to(rows[:, 8 * a : 8 * a + 1], (8, TILE)) for a in range(3)]
-            for k in range(9):
-                sep = [target[a] - sources[k][a] for a in range(3)]
-                soft = sep[0] * sep[0] + sep[1] * sep[1] + (sep[2] * sep[2] + EPS2)
-                root = lax.rsqrt(soft)
-                square = root * root
-                pair_ref[tile, group, k, 0] = root + EPS2 * (square * root)
-                scale = square * lax.rsqrt(root)
-                for a in range(3):
-                    pair_ref[tile, group, k, 1 + a] = sep[a] * scale
-        pltpu.make_async_copy(pair_ref.at[tile], pair_hbm.at[tile], sems.at[tile]).start()
-        return carry
-
-    lax.fori_loop(0, TY, of_tile, 0)
-    for tile in range(TY):
-        pltpu.make_async_copy(pair_ref.at[tile], pair_hbm.at[tile], sems.at[tile]).wait()
-
-
-def mobility(pair_ref, moved, rows_ref, pairs_ref, arrive):
-    source_rows(lambda block, part: moved[block][part], rows_ref)
-
-    def of_tile(tile, carry):
-        arrive(tile)
         sources = sources_of(rows_ref, tile)
         sums = [[], [], []]
+        pair = pair_at(tile)
         for group in range(TILE // 8):
             terms = None
             for k in range(9):
-                near = pair_ref[tile, group, k, 0]
-                sep = [pair_ref[tile, group, k, 1 + a] for a in range(3)]
+                near, *sep = pair(group, k)
                 force = sources[k]
                 along = sep[0] * force[0] + sep[1] * force[1] + sep[2] * force[2]
                 term = [near * force[a] + along * sep[a] for a in range(3)]
@@ -310,24 +273,74 @@
     return [pairs_ref[8 * a : 8 * a + 8, :] for a in range(3)]
 
 
+def stored_pairs(pair_ref):
+    def pair_at(tile):
+        return lambda group, k: [pair_ref[tile, group, k, part] for part in range(4)]
+
+    return pair_at
+
+
+def new_pairs(pair_ref, own_position, rows_ref):
+    columns = jnp.concatenate([own_position, jnp.zeros((104, TILE), F32)], axis=0).T
+
+    def pair_at(tile):
+        turned_columns = pltpu.roll(columns, TILE - tile, 1)
+        sources = sources_of(rows_ref, tile)
+        targets = {}
+
+        def pair(group, k):
+            if group not in targets:
+                rows = turned_columns[8 * group : 8 * group + 8]
+                targets[group] = [
+                    jnp.broadcast_to(rows[:, 8 * a : 8 * a + 1], (8, TILE)) for a in range(3)
+                ]
+            target = targets[group]
+            shift = (float(k // 3 - 1), float(k % 3 - 1), 0.0)
+            sep = [target[a] - (sources[k][a] + shift[a]) for a in range(3)]
+            soft = sep[0] * sep[0] + sep[1] * sep[1] + (sep[2] * sep[2] + EPS2)
+            root = lax.rsqrt(soft)
+            square = root * root
+            scale = square * lax.rsqrt(root)
+            found = [root + EPS2 * (square * root)] + [sep[a] * scale for a in range(3)]
+            for part in range(4):
+                pair_ref[tile, group, k, part] = found[part]
+            return found
+
+        return pair
+
+    return pair_at
+
+
 def local_kernel(step, *refs):
     refs = list(refs)
     take = lambda n: [refs.pop(0) for _ in range(n)]
     message_ref, state_ref, field_ref = take(3)
-    pair_ref, arm_ref, owner_ref, row_ref = take(4)
+    if step == 0:
+        (pack_ref,) = take(1)
+    else:
+        pair_ref, arm_ref, owner_ref, row_ref = take(4)
     bases = take(step)
+    if step == 0:
+        pair_ref, arm_ref, owner_ref, row_ref = take(4)
     basis_ref, moved_ref, fresh_ref, out_ref = take(4)
     rows_ref, pairs_ref, onehot, high, low = take(5)
-    arrive = lambda tile: None
     if step == 0:
-        pair_hbm = pair_ref
-        pair_ref, sems = take(2)
-        fetch = lambda tile: pltpu.make_async_copy(
-            pair_hbm.at[tile], pair_ref.at[tile], sems.at[tile]
-        )
-        for tile in range(TY):
-            fetch(tile).start()
-        arrive = lambda tile: fetch(tile).wait()
+        (places_ref,) = take(1)
+        rows = rows_of(message_ref, 3, BACK).T
+        edges = rows_of(message_ref, 1, BACK).T
+        fixed = [pack_ref[0:FIXED, :], rows[:FIXED], rows[64 : 64 + FIXED]]
+        for k in range(3):
+            at = EDGES_AT + 2 * EDGE_STEP[k]
+            fixed.append(edges[at : at + FIXED])
+        for block in range(BLOCKS):
+            arm_ref[24 * block : 24 * block + 24, :] = fixed[block][24:48]
+            code = fixed[block][48:56].astype(jnp.int32)
+            owner_ref[8 * block : 8 * block + 8, :] = lax.shift_right_logical(code, 5)
+            row_ref[8 * block : 8 * block + 8, :] = code & (ROWS - 1)
+        source_rows(lambda block, part: fixed[block][8 * part : 8 * part + 8], places_ref)
+        pair_at = new_pairs(pair_ref, fixed[0][0:24], places_ref)
+    else:
+        pair_at = stored_pairs(pair_ref)
     rim = rows_of(message_ref, 2, BACK).T
     basis = jnp.concatenate([field_ref[...], rim[:120]], axis=0)
     for i in range(step):
@@ -348,7 +361,7 @@
                 for a in range(3)
             ]
         )
-    pairs = mobility(pair_ref, moved, rows_ref, pairs_ref, arrive)
+    pairs = mobility(moved, rows_ref, pairs_ref, pair_at)
     fresh = [moved[0][a] + FACTOR * pairs[a] for a in range(3)]
     for a in range(3):
         moved_ref[8 * a : 8 * a + 8, :] = moved[0][a]
@@ -366,7 +379,7 @@
         sums = body_sums(
             fresh, arms, owner_ref[0:8, :], row_ref[0:8, :], onehot, high, low
         )
-        forward_message(fresh, sums, dots, out_ref)
+        forward_message(fresh, sums, dots, out_ref, 2)
     else:
         lane = iota((NDEV, TILE), 1)
         message = jnp.zeros((NDEV, TILE), F32)
@@ -444,19 +457,6 @@
     return lax.all_to_all(message, CELL_WIDE, split_axis=0, concat_axis=0, tiled=True)
 
 
-def ring(array, axes, step):
-    count = lax.axis_size(axes)
-    return lax.ppermute(array, axes, [(i, (i + step) % count) for i in range(count)])
-
-
-def rims(pack):
-    before, after = ring(pack, "cell", 1), ring(pack, "cell", -1)
-    rows = [x.reshape(8, TY, TILE) for x in (before, pack, after)]
-    last = jnp.concatenate([x[:, TY - 1] for x in rows], axis=0)
-    first = jnp.concatenate([x[:, 0] for x in rows], axis=0)
-    return before, after, ring(last, WIDE, 1), ring(first, WIDE, -1)
-
-
 def local(positions, rhs, blob_owner, blob_row, blob_arm, body_inverse):
     pos = positions.reshape(24, TILE)
     field = rhs.reshape(24, TILE)
@@ -468,7 +468,7 @@
     inverse = jnp.concatenate([inverse[:, :TILE], inverse[:, TILE:]], axis=0)
     message, pack, field = call(
         start_kernel,
-        (f32(2 * NDEV, TILE), f32(64, TILE), f32(24, TILE)),
+        (f32(FIRST * NDEV, TILE), f32(TILE, TILE), f32(24, TILE)),
         [
             pltpu.VMEM((TY, TILE), jnp.int32),
             pltpu.VMEM((TY, TILE), jnp.int32),
@@ -477,49 +477,36 @@
         + sums_scratch(),
         in_specs=[HBM] * 5,
     )(*[pltpu.with_memory_space_constraint(x, pltpu.HBM) for x in (pos, field, owner, row, arm)])
-    before, after, left, right = rims(pack)
-    arrived, left, right = lax.optimization_barrier((exchange(message), left, right))
-    pair_count = 9 * TY * TILE * TILE
-    pairs, *fixed = call(
-        pair_kernel,
-        (
-            f32(*PAIRS),
-            f32(24 * BLOCKS, TILE),
-            i32(8 * BLOCKS, TILE),
-            i32(8 * BLOCKS, TILE),
-        ),
-        [pltpu.VMEM((96, TILE), F32), pltpu.VMEM(PAIRS, F32), pltpu.SemaphoreType.DMA((TY,))],
-        mib=40,
-        out_specs=(HBM, VMEM, VMEM, VMEM),
-        cost_estimate=pl.CostEstimate(
-            flops=20 * pair_count, transcendentals=2 * pair_count, bytes_accessed=16 * pair_count
-        ),
-    )(pack, before, after, left, right)
     states, bases, moveds = [], [], []
     for step in range(ITERS):
-        if step > 0:
-            arrived = exchange(message)
+        arrived = exchange(message)
         message, state = call(
             lambda *refs, step=step: owner_kernel(step, *refs),
             (f32(BACK * NDEV, TILE), f32(8, TILE)),
         )(inverse, arrived, *states)
         arrived = exchange(message)
-        basis, moved, field, message = call(
-            lambda *refs, step=step: local_kernel(step, *refs),
-            (
+        outs = [
+            f32(24 * BLOCKS, TILE),
+            f32(24, TILE),
+            f32(24, TILE),
+            f32(NDEV if step == ITERS - 1 else 2 * NDEV, TILE),
+        ]
+        scratch = [pltpu.VMEM((96, TILE), F32), pltpu.VMEM((24, TILE), F32)] + sums_scratch()
+        if step == 0:
+            outs = [
+                pltpu.VMEM(PAIRS, F32),
                 f32(24 * BLOCKS, TILE),
-                f32(24, TILE),
-                f32(24, TILE),
-                f32(NDEV if step == ITERS - 1 else 2 * NDEV, TILE),
-            ),
-            [pltpu.VMEM((96, TILE), F32), pltpu.VMEM((24, TILE), F32)]
-            + sums_scratch()
-            + ([pltpu.VMEM(PAIRS, F32), pltpu.SemaphoreType.DMA((TY,))] if step == 0 else []),
-            mib=40 if step == 0 else 16,
-            in_specs=[VMEM] * 3 + [HBM if step == 0 else VMEM] + [VMEM] * (3 + step),
-        )(arrived, state, field, pairs, *fixed, *bases)
+                i32(8 * BLOCKS, TILE),
+                i32(8 * BLOCKS, TILE),
+            ] + outs
+            scratch.append(pltpu.VMEM((96, TILE), F32))
+        results = call(
+            lambda *refs, step=step: local_kernel(step, *refs), tuple(outs), scratch
+        )(arrived, state, field, *(fixed if step else (pack,)), *bases)
         if step == 0:
-            pairs = pltpu.with_memory_space_constraint(pairs, pltpu.VMEM)
+            pairs = pltpu.with_memory_space_constraint(results[0], pltpu.VMEM)
+            fixed = (pairs, *results[1:4])
+        basis, moved, field, message = results[-4:]
         states.append(state)
         bases.append(basis)
         moveds.append(moved)

time: 141 us -> 136 us (0.965)
  blocking collectives: 74.5 us -> 88.3 us
  starting transfers between devices: 23.2 us -> 11.5 us
  Pallas kernels: 30.4 us -> 23.7 us
    all_to_all x5 -> x6, blocking collectives: 74.5 us -> 88.3 us  [exchange(): lax.all_to_all(message, CELL_WIDE, split_axis=0, concat_axis=0, tiled=True)]
    ppermute x4 -> x0, starting transfers between devices: 6.37 us -> none  [ring(): lax.ppermute(array, axes, [(i, (i + step) % count) for i in range(count)])]
    pallas_call x5 -> x4, Pallas kernels: 28.1 us -> 22.1 us  [the longest x3 20.1 us: local(): call(lambda *refs, step=step: local_kernel(step, *refs), tuple(outs), scr...]
    all_to_all x2 -> x1, starting transfers between devices: 16.8 us -> 11.5 us  [exchange(): lax.all_to_all(message, CELL_WIDE, split_axis=0, concat_axis=0, tiled=True)]
    ppermute x4 -> x0, waiting for transfers between devices: 3.41 us -> none  [ring(): lax.ppermute(array, axes, [(i, (i + step) % count) for i in range(count)])]
    all_to_all x2 -> x1, waiting for transfers between devices: 7.89 us -> 10.3 us  [exchange(): lax.all_to_all(message, CELL_WIDE, split_axis=0, concat_axis=0, tiled=True)]
  transfers between devices with their start and end apart: 6 -> 1, of which waited for: 4 -> 1; matrix products, arithmetic and copies ran while one was open for 1% -> 1% of each run, Pallas kernels for 5% -> 0%
where the time goes in v3:
time: 136 us; the launch traced here: 135 us
  blocking collectives  88.3 us (65%)
  Pallas kernels  23.7 us (17%)
  starting transfers between devices  11.5 us (8%)
  waiting for transfers between devices  10.3 us (8%)
    all_to_all x6, blocking collectives, exchange(): lax.all_to_all(message, CELL_WIDE, split_axis=0, concat_axis=0, tiled=True)  88.3 us
    pallas_call x3, Pallas kernels, local(): call(lambda *refs, step=step: local_kernel(step, *refs), tuple(outs), scr...  20.1 us
    all_to_all x1, starting transfers between devices, exchange(): lax.all_to_all(message, CELL_WIDE, split_axis=0, concat_axis=0, tiled=True)  11.5 us
    all_to_all x1, waiting for transfers between devices, exchange(): lax.all_to_all(message, CELL_WIDE, split_axis=0, concat_axis=0, tiled=True)  10.3 us
  transfers between devices with their start and end apart: 1, of which 1 were waited for; matrix products, arithmetic and copies ran while one was open for 1% of the time, Pallas kernels for 0%

profile of v3, /device:TPU:1, one launch (start us, length us, event | category | flops | bytes accessed | tf_op | source)
XLA Modules:
  0.0 135.3 jit_solution(14904719833234071361)
XLA Ops:
  0.6 2.0 %shard_map.77 = (f32[512,128]{1,0:T(8,128)}, f32[128,128]{1,0:T(8,128)S(1)}, f32[24,128]{1,0:T(8,128)S(1)}) custom-call(f32[24,128]{1,0:T(8,128)} %bitcast.39, f32[24,128]{1,0:T(8,128)} %bitcast.40, s32[8,128]{1,0:T(8,128)} %bitcast.42, s32[8,128]{1,0:T(8,128)} %bitcast.43, f32[24,128]{1,0:T(8,128)} %bitcast.41), custom_call_target="tpu_custom_call" | custom-call | tf_op jit(solution)/shard_map/pallas_call | solution.py:469
  2.6 11.5 %all-to-all-start = ((f32[128,4,128]{2,1,0:T(4,128)}), f32[128,4,128]{2,1,0:T(4,128)S(1)}, u32[]{:S(2)}, u32[]{:S(2)}) async-start(f32[128,4,128]{2,1,0:T(4,128)} %bitcast.6), calls=%async_computation | async-start | bytes 524288 | tf_op jit(solution)/shard_map/all_to_all | solution.py:457
  14.1 0.7 copy.10
  14.9 0.1 reshape.39
  15.0 10.3 %all-to-all-done = f32[128,4,128]{2,1,0:T(4,128)S(1)} async-done(((f32[128,4,128]{2,1,0:T(4,128)}), f32[128,4,128]{2,1,0:T(4,128)S(1)}, u32[]{:S(2)}, u32[]{:S(2)}) %all-to-all-start) | async-done | bytes 262176 | tf_op jit(solution)/shard_map/all_to_all | solution.py:457
  25.2 0.3 shard_map.78
  25.5 15.4 %all_to_all.77 = f32[128,4,128]{2,1,0:T(4,128)S(1)} all-to-all(f32[128,4,128]{2,1,0:T(4,128)S(1)} %bitcast.33), channel_id=1, replica_groups=mesh['cell'=4,'wide_0'=4,'wide_1'=4,'wide_2'=2] {'cell','wide_0','wide_1..., dimensions={0} | all-to-all | bytes 524288 | tf_op jit(solution)/shard_map/all_to_all | solution.py:457
  40.9 9.7 %shard_map.79 = (f32[8,16,9,4,8,128]{5,4,3,2,1,0:T(8,128)S(1)}, f32[144,128]{1,0:T(8,128)S(1)}, s32[48,128]{1,0:T(8,128)S(1)}, s32[48,128]{1,0:T(8,128)S(1)}, f3...) custom-call(f32[512,128]{1,0:T(8,128)S(1)} %bitcast.28, ...), custom_call_target="tpu_custom_call" | custom-call | tf_op jit(solution)/shard_map/pallas_call | solution.py:503
  50.6 14.3 %all_to_all.78 = f32[128,2,128]{2,1,0:T(2,128)S(1)} all-to-all(f32[128,2,128]{2,1,0:T(2,128)S(1)} %bitcast.35), channel_id=1, replica_groups=mesh['cell'=4,'wide_0'=4,'wide_1'=4,'wide_2'=2] {'cell','wide_0','wide_1..., dimensions={0} | all-to-all | bytes 262144 | tf_op jit(solution)/shard_map/all_to_all | solution.py:457
  64.9 0.3 shard_map.80
  65.1 15.3 %all_to_all.79 = f32[128,4,128]{2,1,0:T(4,128)S(1)} all-to-all(f32[128,4,128]{2,1,0:T(4,128)S(1)} %bitcast.34), channel_id=1, replica_groups=mesh['cell'=4,'wide_0'=4,'wide_1'=4,'wide_2'=2] {'cell','wide_0','wide_1..., dimensions={0} | all-to-all | bytes 524288 | tf_op jit(solution)/shard_map/all_to_all | solution.py:457
  80.5 5.3 %shard_map.81 = (f32[144,128]{1,0:T(8,128)S(1)}, f32[24,128]{1,0:T(8,128)S(1)}, f32[24,128]{1,0:T(8,128)S(1)}, f32[256,128]{1,0:T(8,128)S(1)}) custom-call(f32[512,128]{1,0:T(8,128)S(1)} %bitcast.26, f32[8,128]{1,0:T(8,128)S(1)} %get-tuple-element.34.refs_1_.refs_3_, f32[24,128]{1,0:T(8,128)S(1)} %get-tuple-element.35.refs_2_, ...), custom_call_target="tpu_custom_call" | custom-call | tf_op jit(solution)/shard_map/pallas_call | solution.py:503
  85.8 14.3 %all_to_all.80 = f32[128,2,128]{2,1,0:T(2,128)S(1)} all-to-all(f32[128,2,128]{2,1,0:T(2,128)S(1)} %bitcast.36), channel_id=1, replica_groups=mesh['cell'=4,'wide_0'=4,'wide_1'=4,'wide_2'=2] {'cell','wide_0','wide_1..., dimensions={0} | all-to-all | bytes 262144 | tf_op jit(solution)/shard_map/all_to_all | solution.py:457
  100.0 0.3 shard_map.82
  100.3 15.2 %all_to_all.81 = f32[128,4,128]{2,1,0:T(4,128)S(1)} all-to-all(f32[128,4,128]{2,1,0:T(4,128)S(1)} %bitcast.32), channel_id=1, replica_groups=mesh['cell'=4,'wide_0'=4,'wide_1'=4,'wide_2'=2] {'cell','wide_0','wide_1..., dimensions={0} | all-to-all | bytes 524288 | tf_op jit(solution)/shard_map/all_to_all | solution.py:457
  115.5 5.2 %shard_map.83 = (f32[144,128]{1,0:T(8,128)}, f32[24,128]{1,0:T(8,128)S(1)}, f32[24,128]{1,0:T(8,128)}, f32[128,128]{1,0:T(8,128)S(1)}) custom-call(f32[512,128]{1,0:T(8,128)S(1)} %bitcast.25, f32[8,128]{1,0:T(8,128)S(1)} %get-tuple-element.43.refs_1_.refs_2_, f32[24,128]{1,0:T(8,128)S(1)} %get-tuple-element.44.refs_2_, ...), custom_call_target="tpu_custom_call" | custom-call | tf_op jit(solution)/shard_map/pallas_call | solution.py:503
  120.6 13.9 %all_to_all.82 = f32[128,1,128]{2,1,0:T(1,128)S(1)} all-to-all(f32[128,1,128]{2,1,0:T(1,128)S(1)} %bitcast.37), channel_id=1, replica_groups=mesh['cell'=4,'wide_0'=4,'wide_1'=4,'wide_2'=2] {'cell','wide_0','wide_1..., dimensions={0} | all-to-all | bytes 131072 | tf_op jit(solution)/shard_map/all_to_all | solution.py:457
  134.5 0.8 shard_map.84
  (2 shorter events, 0.0 us)
Async XLA Ops:
  2.6 22.6 %all-to-all-start = ((f32[128,4,128]{2,1,0:T(4,128)}), f32[128,4,128]{2,1,0:T(4,128)S(1)}, u32[]{:S(2)}, u32[]{:S(2)}) async-start(f32[128,4,128]{2,1,0:T(4,128)} %bitcast.6), calls=%async_computation | async-start | bytes 524288 | tf_op jit(solution)/shard_map/all_to_all | solution.py:457

commit v4 on v3

--- a/solution.py
+++ b/solution.py
@@ -98,7 +98,8 @@
 
 
 def start_kernel(
-    pos_hbm, rhs_hbm, owner_hbm, row_hbm, arm_hbm, out_ref, pack_ref, rhs_ref,
+    rhs_hbm, owner_hbm, row_hbm, arm_hbm, pos_hbm, inverse_hbm,
+    out_ref, pack_ref, rhs_ref, inverse_ref,
     owner_ref, row_ref, sems, onehot, high, low,
 ):
     copies = [
@@ -106,16 +107,17 @@
         for at, (source, target) in enumerate(
             (
                 (rhs_hbm, rhs_ref),
-                (arm_hbm, pack_ref.at[24:48, :]),
                 (owner_hbm, owner_ref),
                 (row_hbm, row_ref),
+                (arm_hbm, pack_ref.at[24:48, :]),
                 (pos_hbm, pack_ref.at[0:24, :]),
+                (inverse_hbm, inverse_ref),
             )
         )
     ]
     for copy in copies:
         copy.start()
-    for copy in copies:
+    for copy in copies[:4]:
         copy.wait()
     field = [rhs_ref[8 * c : 8 * c + 8, :] for c in range(3)]
     arms = [pack_ref[24 + 8 * c : 32 + 8 * c, :] for c in range(3)]
@@ -125,6 +127,8 @@
     sums = body_sums(field, arms, owner, row, onehot, high, low)
     square = total(field[0] * field[0] + field[1] * field[1] + field[2] * field[2])
     forward_message(field, sums, [square], out_ref, FIRST)
+    for copy in copies[4:]:
+        copy.wait()
     out_ref[pl.ds(2, NDEV, stride=FIRST), :] = pack_ref[...].T
     out_ref[pl.ds(3, NDEV, stride=FIRST), :] = jnp.zeros((NDEV, TILE), F32)
 
@@ -178,11 +182,13 @@
     tiled = jnp.where((lane // ROWS == sub % 4) & (sub < 6), tiled, 0.0)
     tiled = tiled + pltpu.roll(tiled, 32, 1)
     tiled = tiled + pltpu.roll(tiled, 64, 1)
-    motion = [
-        jnp.sum(inverse_ref[8 * half : 8 * half + 8, :] * tiled, axis=0, keepdims=True)
-        for half in range(2)
-    ]
     zero = jnp.zeros((1, TILE), F32)
+    by_row = [inverse_ref[a] for a in range(6)]
+    by_row += [jnp.zeros((6, ROWS), F32)] * 2
+    motion = []
+    for half in range(2):
+        inverse = jnp.concatenate(by_row[4 * half : 4 * half + 4], axis=1)
+        motion.append(jnp.sum(inverse * tiled[0:6], axis=0, keepdims=True))
     state_ref[...] = jnp.concatenate(
         sums + motion + [length, scale] + inners + [zero] * (2 - step), axis=0
     )
@@ -215,16 +221,23 @@
         owner = owner_ref[8 * block : 8 * block + 8, :]
         row = row_ref[8 * block : 8 * block + 8, :]
         values = [jnp.zeros((8, TILE), F32) for _ in range(6)]
-        for tile in range(TY) if block < 3 else (0, 7):
-            pick = slice(tile, tile + 1)
-            onehot = jnp.where(owner_ids == owner[pick], 1.0, 0.0).astype(BF16)
+        for pair in ((0, 1), (2, 3), (4, 5), (6, 7)) if block < 3 else ((0, 7),):
+            onehot = jnp.concatenate(
+                [
+                    jnp.where(owner_ids == owner[tile : tile + 1], 1.0, 0.0).astype(BF16)
+                    for tile in pair
+                ],
+                axis=1,
+            )
             onehot = jnp.concatenate([onehot, onehot], axis=0)
             found = jnp.dot(table, onehot, preferred_element_type=F32)
-            mine = row_ids == row[pick]
-            for part in range(6):
-                chosen = jnp.where(mine, found[part * ROWS : (part + 1) * ROWS], 0.0)
-                value = jnp.sum(chosen, axis=0, keepdims=True)
-                values[part] = jnp.where(sub == tile, value, values[part])
+            for at, tile in enumerate(pair):
+                mine = row_ids == row[tile : tile + 1]
+                lanes = slice(at * TILE, (at + 1) * TILE)
+                for part in range(6):
+                    chosen = jnp.where(mine, found[part * ROWS : (part + 1) * ROWS, lanes], 0.0)
+                    value = jnp.sum(chosen, axis=0, keepdims=True)
+                    values[part] = jnp.where(sub == tile, value, values[part])
         results.append(values)
     return results
 
@@ -269,7 +282,7 @@
             pairs_ref[pl.ds(8 * a + tile, 1), :] = jnp.sum(across, axis=0, keepdims=True)
         return carry
 
-    lax.fori_loop(0, TY, of_tile, 0, unroll=2)
+    lax.fori_loop(0, TY, of_tile, 0, unroll=4)
     return [pairs_ref[8 * a : 8 * a + 8, :] for a in range(3)]
 
 
@@ -322,7 +335,9 @@
     bases = take(step)
     if step == 0:
         pair_ref, arm_ref, owner_ref, row_ref = take(4)
-    basis_ref, moved_ref, fresh_ref, out_ref = take(4)
+    if step < ITERS - 1:
+        basis_ref, fresh_ref = take(2)
+    moved_ref, out_ref = take(2)
     rows_ref, pairs_ref, onehot, high, low = take(5)
     if step == 0:
         (places_ref,) = take(1)
@@ -346,7 +361,6 @@
     for i in range(step):
         basis = basis - state_ref[6 + i : 7 + i, :] * bases[i][...]
     basis = basis * state_ref[5:6, :]
-    basis_ref[...] = basis
     motions = picked_motion(
         rows_of(message_ref, 0, BACK), rows_of(message_ref, 1, BACK), owner_ref, row_ref
     )
@@ -365,7 +379,6 @@
     fresh = [moved[0][a] + FACTOR * pairs[a] for a in range(3)]
     for a in range(3):
         moved_ref[8 * a : 8 * a + 8, :] = moved[0][a]
-        fresh_ref[8 * a : 8 * a + 8, :] = fresh[a]
 
     def dot(get):
         return total(fresh[0] * get(0) + fresh[1] * get(1) + fresh[2] * get(2))
@@ -375,6 +388,9 @@
         dots.append(dot(lambda a: bases[i][8 * a : 8 * a + 8, :]))
     dots.append(dot(lambda a: basis[8 * a : 8 * a + 8]))
     if step < ITERS - 1:
+        basis_ref[...] = basis
+        for a in range(3):
+            fresh_ref[8 * a : 8 * a + 8, :] = fresh[a]
         arms = [arm_ref[8 * a : 8 * a + 8, :] for a in range(3)]
         sums = body_sums(
             fresh, arms, owner_ref[0:8, :], row_ref[0:8, :], onehot, high, low
@@ -463,20 +479,18 @@
     arm = blob_arm.reshape(24, TILE)
     owner = blob_owner.reshape(TY, TILE)
     row = blob_row.reshape(TY, TILE)
-    inverse = jnp.transpose(body_inverse, (1, 0, 2)).reshape(6, 6 * ROWS)
-    inverse = jnp.pad(inverse, ((0, 2), (0, 64)))
-    inverse = jnp.concatenate([inverse[:, :TILE], inverse[:, TILE:]], axis=0)
-    message, pack, field = call(
+    held = (field, owner, row, arm, pos, body_inverse)
+    message, pack, field, inverse = call(
         start_kernel,
-        (f32(FIRST * NDEV, TILE), f32(TILE, TILE), f32(24, TILE)),
+        (f32(FIRST * NDEV, TILE), f32(TILE, TILE), f32(24, TILE), f32(6, 6, ROWS)),
         [
             pltpu.VMEM((TY, TILE), jnp.int32),
             pltpu.VMEM((TY, TILE), jnp.int32),
-            pltpu.SemaphoreType.DMA((5,)),
+            pltpu.SemaphoreType.DMA((6,)),
         ]
         + sums_scratch(),
-        in_specs=[HBM] * 5,
-    )(*[pltpu.with_memory_space_constraint(x, pltpu.HBM) for x in (pos, field, owner, row, arm)])
+        in_specs=[HBM] * 6,
+    )(*[pltpu.with_memory_space_constraint(x, pltpu.HBM) for x in held])
     states, bases, moveds = [], [], []
     for step in range(ITERS):
         arrived = exchange(message)
@@ -485,12 +499,10 @@
             (f32(BACK * NDEV, TILE), f32(8, TILE)),
         )(inverse, arrived, *states)
         arrived = exchange(message)
-        outs = [
-            f32(24 * BLOCKS, TILE),
-            f32(24, TILE),
-            f32(24, TILE),
-            f32(NDEV if step == ITERS - 1 else 2 * NDEV, TILE),
-        ]
+        last = step == ITERS - 1
+        outs = [f32(24, TILE), f32(NDEV if last else 2 * NDEV, TILE)]
+        if not last:
+            outs = [f32(24 * BLOCKS, TILE), f32(24, TILE)] + outs
         scratch = [pltpu.VMEM((96, TILE), F32), pltpu.VMEM((24, TILE), F32)] + sums_scratch()
         if step == 0:
             outs = [
@@ -506,10 +518,12 @@
         if step == 0:
             pairs = pltpu.with_memory_space_constraint(results[0], pltpu.VMEM)
             fixed = (pairs, *results[1:4])
-        basis, moved, field, message = results[-4:]
+        moved, message = results[-2:]
         states.append(state)
-        bases.append(basis)
         moveds.append(moved)
+        if not last:
+            bases.append(results[-4])
+            field = results[-3]
     arrived = exchange(message)
     forces, motion = call(final_kernel, (f32(24, TILE), f32(6, ROWS)))(arrived, *states, *moveds)
     return (forces.reshape(rhs.shape), motion)

time: 136 us -> 132 us (0.971)
  blocking collectives: 88.3 us -> 111 us
  starting transfers between devices: 11.5 us -> 0 us
  waiting for transfers between devices: 10.3 us -> 0 us
  Pallas kernels: 23.7 us -> 19.8 us
    all_to_all x6 -> x7, blocking collectives: 88.3 us -> 111 us  [exchange(): lax.all_to_all(message, CELL_WIDE, split_axis=0, concat_axis=0, tiled=True)]
    all_to_all x1 -> x0, starting transfers between devices: 11.5 us -> none  [exchange(): lax.all_to_all(message, CELL_WIDE, split_axis=0, concat_axis=0, tiled=True)]
    all_to_all x1 -> x0, waiting for transfers between devices: 10.3 us -> none  [exchange(): lax.all_to_all(message, CELL_WIDE, split_axis=0, concat_axis=0, tiled=True)]
    pallas_call x3, Pallas kernels: 20.1 us -> 16.8 us  [local(): call(lambda *refs, step=step: local_kernel(step, *refs), tuple(outs), scr...]
  transfers between devices with their start and end apart: 1 -> 0, of which waited for: 1 -> 0; matrix products, arithmetic and copies ran while one was open for 1% -> 0% of each run, Pallas kernels for 0% -> 0%
where the time goes in v4:
time: 132 us; the launch traced here: 131 us
  blocking collectives  111 us (84%)
  Pallas kernels  19.8 us (15%)
    all_to_all x7, blocking collectives, exchange(): lax.all_to_all(message, CELL_WIDE, split_axis=0, concat_axis=0, tiled=True)  111 us
    pallas_call x3, Pallas kernels, local(): call(lambda *refs, step=step: local_kernel(step, *refs), tuple(outs), scr...  16.8 us

profile of v4, /device:TPU:1, one launch (start us, length us, event | category | flops | bytes accessed | tf_op | source)
XLA Modules:
  0.0 131.2 jit_solution(10216743816342702807)
XLA Ops:
  0.6 1.4 %shard_map.77 = (f32[512,128]{1,0:T(8,128)S(1)}, f32[128,128]{1,0:T(8,128)S(1)}, f32[24,128]{1,0:T(8,128)S(1)}, f32[6,6,32]{2,1,0:T(8,128)S(1)}) custom-call(f32[24,128]{1,0:T(8,128)} %bitcast.38, s32[8,128]{1,0:T(8,128)} %bitcast.41, s32[8,128]{1,0:T(8,128)} %bitcast.42, f32[24,128]{1,0:T(8,128)} %bitcast.39, f32[24,128]{1,0:T(8,128)} %bitcast.40, ...), custom_call_target="tpu_custom_call" | custom-call | tf_op jit(solution)/shard_map/pallas_call | solution.py:483
  2.0 22.5 %all_to_all.77 = f32[128,4,128]{2,1,0:T(4,128)S(1)} all-to-all(f32[128,4,128]{2,1,0:T(4,128)S(1)} %bitcast.31), channel_id=1, replica_groups=mesh['cell'=4,'wide_0'=4,'wide_1'=4,'wide_2'=2] {'cell','wide_0','wide_1..., dimensions={0} | all-to-all | bytes 524288 | tf_op jit(solution)/shard_map/all_to_all | solution.py:473
  24.5 0.3 shard_map.78
  24.8 15.3 %all_to_all.78 = f32[128,4,128]{2,1,0:T(4,128)S(1)} all-to-all(f32[128,4,128]{2,1,0:T(4,128)S(1)} %bitcast.33), channel_id=1, replica_groups=mesh['cell'=4,'wide_0'=4,'wide_1'=4,'wide_2'=2] {'cell','wide_0','wide_1..., dimensions={0} | all-to-all | bytes 524288 | tf_op jit(solution)/shard_map/all_to_all | solution.py:473
  40.1 8.6 %shard_map.79 = (f32[8,16,9,4,8,128]{5,4,3,2,1,0:T(8,128)S(1)}, f32[144,128]{1,0:T(8,128)S(1)}, s32[48,128]{1,0:T(8,128)S(1)}, s32[48,128]{1,0:T(8,128)S(1)}, f3...) custom-call(f32[512,128]{1,0:T(8,128)S(1)} %bitcast.26, ...), custom_call_target="tpu_custom_call" | custom-call | tf_op jit(solution)/shard_map/pallas_call | solution.py:515
  48.8 14.2 %all_to_all.79 = f32[128,2,128]{2,1,0:T(2,128)S(1)} all-to-all(f32[128,2,128]{2,1,0:T(2,128)S(1)} %bitcast.35), channel_id=1, replica_groups=mesh['cell'=4,'wide_0'=4,'wide_1'=4,'wide_2'=2] {'cell','wide_0','wide_1..., dimensions={0} | all-to-all | bytes 262144 | tf_op jit(solution)/shard_map/all_to_all | solution.py:473
  63.0 0.3 shard_map.80
  63.3 15.3 %all_to_all.80 = f32[128,4,128]{2,1,0:T(4,128)S(1)} all-to-all(f32[128,4,128]{2,1,0:T(4,128)S(1)} %bitcast.34), channel_id=1, replica_groups=mesh['cell'=4,'wide_0'=4,'wide_1'=4,'wide_2'=2] {'cell','wide_0','wide_1..., dimensions={0} | all-to-all | bytes 524288 | tf_op jit(solution)/shard_map/all_to_all | solution.py:473
  78.6 4.4 %shard_map.81 = (f32[144,128]{1,0:T(8,128)S(1)}, f32[24,128]{1,0:T(8,128)S(1)}, f32[24,128]{1,0:T(8,128)S(1)}, f32[256,128]{1,0:T(8,128)S(1)}) custom-call(f32[512,128]{1,0:T(8,128)S(1)} %bitcast.25, f32[8,128]{1,0:T(8,128)S(1)} %get-tuple-element.36.refs_1_.refs_3_, f32[24,128]{1,0:T(8,128)S(1)} %get-tuple-element.37.refs_2_, ...), custom_call_target="tpu_custom_call" | custom-call | tf_op jit(solution)/shard_map/pallas_call | solution.py:515
  83.0 14.3 %all_to_all.81 = f32[128,2,128]{2,1,0:T(2,128)S(1)} all-to-all(f32[128,2,128]{2,1,0:T(2,128)S(1)} %bitcast.36), channel_id=1, replica_groups=mesh['cell'=4,'wide_0'=4,'wide_1'=4,'wide_2'=2] {'cell','wide_0','wide_1..., dimensions={0} | all-to-all | bytes 262144 | tf_op jit(solution)/shard_map/all_to_all | solution.py:473
  97.3 0.3 shard_map.82
  97.5 15.3 %all_to_all.82 = f32[128,4,128]{2,1,0:T(4,128)S(1)} all-to-all(f32[128,4,128]{2,1,0:T(4,128)S(1)} %bitcast.32), channel_id=1, replica_groups=mesh['cell'=4,'wide_0'=4,'wide_1'=4,'wide_2'=2] {'cell','wide_0','wide_1..., dimensions={0} | all-to-all | bytes 524288 | tf_op jit(solution)/shard_map/all_to_all | solution.py:473
  112.9 3.8 %shard_map.83 = (f32[24,128]{1,0:T(8,128)S(1)}, f32[128,128]{1,0:T(8,128)S(1)}) custom-call(f32[512,128]{1,0:T(8,128)S(1)} %bitcast.24, f32[8,128]{1,0:T(8,128)S(1)} %get-tuple-element.45.refs_1_.refs_2_, f32[24,128]{1,0:T(8,128)S(1)} %get-tuple-element.46.refs_2_, f32[8,16,9,4,8,128]{5,4,3,2,1,0:T(8,128)S(1)} %get-tuple-element.38.refs_3_, ...), custom_call_target="tpu_custom_call" | custom-call | tf_op jit(solution)/shard_map/pallas_call | solution.py:515
  116.7 13.7 %all_to_all.83 = f32[128,1,128]{2,1,0:T(1,128)S(1)} all-to-all(f32[128,1,128]{2,1,0:T(1,128)S(1)} %bitcast.37), channel_id=1, replica_groups=mesh['cell'=4,'wide_0'=4,'wide_1'=4,'wide_2'=2] {'cell','wide_0','wide_1..., dimensions={0} | all-to-all | bytes 131072 | tf_op jit(solution)/shard_map/all_to_all | solution.py:473
  130.4 0.8 shard_map.84

commit v5 on v4

--- a/solution.py
+++ b/solution.py
@@ -24,8 +24,8 @@
 ROWS = 32
 HALO_AT = 64
 DOT_AT = 88
-FIRST = 4
-BACK = 4
+FIRST = 3
+BACK = (4, 3, 3)
 FIXED = 56
 BLOCKS = 6
 EDGE_OF = {-1: 3, 0: 4, 1: 5}
@@ -130,7 +130,6 @@
     for copy in copies[4:]:
         copy.wait()
     out_ref[pl.ds(2, NDEV, stride=FIRST), :] = pack_ref[...].T
-    out_ref[pl.ds(3, NDEV, stride=FIRST), :] = jnp.zeros((NDEV, TILE), F32)
 
 
 def turned(x, by):
@@ -203,10 +202,8 @@
         for k in range(3):
             sent[1] = sent[1] + shifted(blocks[2 + k], EDGES_AT + 2 * EDGE_STEP[k])
         sent.append(blocks[0] + shifted(blocks[1], 64))
-    else:
-        sent.append(jnp.zeros((NDEV, TILE), F32))
-    for part in range(BACK):
-        out_ref[pl.ds(part, NDEV, stride=BACK), :] = sent[part]
+    for part in range(BACK[step]):
+        out_ref[pl.ds(part, NDEV, stride=BACK[step]), :] = sent[part]
 
 
 def picked_motion(first, second, owner_ref, row_ref):
@@ -326,6 +323,7 @@
 
 def local_kernel(step, *refs):
     refs = list(refs)
+    back = BACK[step]
     take = lambda n: [refs.pop(0) for _ in range(n)]
     message_ref, state_ref, field_ref = take(3)
     if step == 0:
@@ -341,8 +339,8 @@
     rows_ref, pairs_ref, onehot, high, low = take(5)
     if step == 0:
         (places_ref,) = take(1)
-        rows = rows_of(message_ref, 3, BACK).T
-        edges = rows_of(message_ref, 1, BACK).T
+        rows = rows_of(message_ref, 3, back).T
+        edges = rows_of(message_ref, 1, back).T
         fixed = [pack_ref[0:FIXED, :], rows[:FIXED], rows[64 : 64 + FIXED]]
         for k in range(3):
             at = EDGES_AT + 2 * EDGE_STEP[k]
@@ -356,13 +354,13 @@
         pair_at = new_pairs(pair_ref, fixed[0][0:24], places_ref)
     else:
         pair_at = stored_pairs(pair_ref)
-    rim = rows_of(message_ref, 2, BACK).T
+    rim = rows_of(message_ref, 2, back).T
     basis = jnp.concatenate([field_ref[...], rim[:120]], axis=0)
     for i in range(step):
         basis = basis - state_ref[6 + i : 7 + i, :] * bases[i][...]
     basis = basis * state_ref[5:6, :]
     motions = picked_motion(
-        rows_of(message_ref, 0, BACK), rows_of(message_ref, 1, BACK), owner_ref, row_ref
+        rows_of(message_ref, 0, back), rows_of(message_ref, 1, back), owner_ref, row_ref
     )
     moved = []
     for block in range(BLOCKS):
@@ -470,7 +468,10 @@
 
 
 def exchange(message):
-    return lax.all_to_all(message, CELL_WIDE, split_axis=0, concat_axis=0, tiled=True)
+    rows = message.shape[0]
+    moved = message.reshape(NDEV, 1, rows * TILE // NDEV)
+    moved = lax.all_to_all(moved, CELL_WIDE, split_axis=0, concat_axis=0, tiled=True)
+    return moved.reshape(rows, TILE)
 
 
 def local(positions, rhs, blob_owner, blob_row, blob_arm, body_inverse):
@@ -496,7 +497,7 @@
         arrived = exchange(message)
         message, state = call(
             lambda *refs, step=step: owner_kernel(step, *refs),
-            (f32(BACK * NDEV, TILE), f32(8, TILE)),
+            (f32(BACK[step] * NDEV, TILE), f32(8, TILE)),
         )(inverse, arrived, *states)
         arrived = exchange(message)
         last = step == ITERS - 1

time: 132 us -> 131 us (level)
  blocking collectives: 111 us -> 109 us
  Pallas kernels: 19.8 us -> 21.7 us
    all_to_all x7, blocking collectives: 111 us -> 109 us  [exchange(): lax.all_to_all(moved, CELL_WIDE, split_axis=0, concat_axis=0, tiled=True)]
    pallas_call x3, Pallas kernels: 16.8 us -> 18.7 us  [local(): call(lambda *refs, step=step: local_kernel(step, *refs), tuple(outs), scr...]
where the time goes in v5:
time: 131 us
  blocking collectives  109 us (83%)
  Pallas kernels  21.7 us (17%)
    all_to_all x7, blocking collectives, exchange(): lax.all_to_all(moved, CELL_WIDE, split_axis=0, concat_axis=0, tiled=True)  109 us
    pallas_call x3, Pallas kernels, local(): call(lambda *refs, step=step: local_kernel(step, *refs), tuple(outs), scr...  18.7 us

profile of v5, /device:TPU:1, one launch (start us, length us, event | category | flops | bytes accessed | tf_op | source)
XLA Modules:
  0.0 131.1 jit_solution(15087158822481598239)
XLA Ops:
  0.6 1.4 %shard_map.77 = (f32[384,128]{1,0:T(8,128)S(1)}, f32[128,128]{1,0:T(8,128)S(1)}, f32[24,128]{1,0:T(8,128)S(1)}, f32[6,6,32]{2,1,0:T(8,128)S(1)}) custom-call(f32[24,128]{1,0:T(8,128)} %bitcast.38, s32[8,128]{1,0:T(8,128)} %bitcast.41, s32[8,128]{1,0:T(8,128)} %bitcast.42, f32[24,128]{1,0:T(8,128)} %bitcast.39, f32[24,128]{1,0:T(8,128)} %bitcast.40, ...), custom_call_target="tpu_custom_call" | custom-call | tf_op jit(solution)/shard_map/pallas_call | solution.py:484
  2.0 21.8 %all_to_all.35 = f32[128,1,384]{2,1,0:T(1,128)S(1)} all-to-all(f32[128,1,384]{2,1,0:T(1,128)S(1)} %bitcast.32), channel_id=1, replica_groups=mesh['cell'=4,'wide_0'=4,'wide_1'=4,'wide_2'=2] {'cell','wide_0','wide_1..., dimensions={0} | all-to-all | bytes 393216 | tf_op jit(solution)/shard_map/all_to_all | solution.py:473
  23.9 0.3 shard_map.78
  24.1 15.3 %all_to_all.36 = f32[128,1,512]{2,1,0:T(1,128)S(1)} all-to-all(f32[128,1,512]{2,1,0:T(1,128)S(1)} %bitcast.31), channel_id=1, replica_groups=mesh['cell'=4,'wide_0'=4,'wide_1'=4,'wide_2'=2] {'cell','wide_0','wide_1..., dimensions={0} | all-to-all | bytes 524288 | tf_op jit(solution)/shard_map/all_to_all | solution.py:473
  39.5 9.3 %shard_map.79 = (f32[8,16,9,4,8,128]{5,4,3,2,1,0:T(8,128)S(1)}, f32[144,128]{1,0:T(8,128)S(1)}, s32[48,128]{1,0:T(8,128)S(1)}, s32[48,128]{1,0:T(8,128)S(1)}, f3...) custom-call(f32[512,128]{1,0:T(8,128)S(1)} %bitcast.24, ...), custom_call_target="tpu_custom_call" | custom-call | tf_op jit(solution)/shard_map/pallas_call | solution.py:516
  48.7 14.3 %all_to_all.37 = f32[128,1,256]{2,1,0:T(1,128)S(1)} all-to-all(f32[128,1,256]{2,1,0:T(1,128)S(1)} %bitcast.35), channel_id=1, replica_groups=mesh['cell'=4,'wide_0'=4,'wide_1'=4,'wide_2'=2] {'cell','wide_0','wide_1..., dimensions={0} | all-to-all | bytes 262144 | tf_op jit(solution)/shard_map/all_to_all | solution.py:473
  63.0 0.3 shard_map.80
  63.3 14.7 %all_to_all.38 = f32[128,1,384]{2,1,0:T(1,128)S(1)} all-to-all(f32[128,1,384]{2,1,0:T(1,128)S(1)} %bitcast.34), channel_id=1, replica_groups=mesh['cell'=4,'wide_0'=4,'wide_1'=4,'wide_2'=2] {'cell','wide_0','wide_1..., dimensions={0} | all-to-all | bytes 393216 | tf_op jit(solution)/shard_map/all_to_all | solution.py:473
  77.9 5.0 %shard_map.81 = (f32[144,128]{1,0:T(8,128)S(1)}, f32[24,128]{1,0:T(8,128)S(1)}, f32[24,128]{1,0:T(8,128)S(1)}, f32[256,128]{1,0:T(8,128)S(1)}) custom-call(f32[384,128]{1,0:T(8,128)S(1)} %bitcast.26, f32[8,128]{1,0:T(8,128)S(1)} %get-tuple-element.36.refs_1_.refs_3_, f32[24,128]{1,0:T(8,128)S(1)} %get-tuple-element.37.refs_2_, ...), custom_call_target="tpu_custom_call" | custom-call | tf_op jit(solution)/shard_map/pallas_call | solution.py:516
  82.9 14.3 %all_to_all.39 = f32[128,1,256]{2,1,0:T(1,128)S(1)} all-to-all(f32[128,1,256]{2,1,0:T(1,128)S(1)} %bitcast.36), channel_id=1, replica_groups=mesh['cell'=4,'wide_0'=4,'wide_1'=4,'wide_2'=2] {'cell','wide_0','wide_1..., dimensions={0} | all-to-all | bytes 262144 | tf_op jit(solution)/shard_map/all_to_all | solution.py:473
  97.2 0.3 shard_map.82
  97.5 14.7 %all_to_all.40 = f32[128,1,384]{2,1,0:T(1,128)S(1)} all-to-all(f32[128,1,384]{2,1,0:T(1,128)S(1)} %bitcast.33), channel_id=1, replica_groups=mesh['cell'=4,'wide_0'=4,'wide_1'=4,'wide_2'=2] {'cell','wide_0','wide_1..., dimensions={0} | all-to-all | bytes 393216 | tf_op jit(solution)/shard_map/all_to_all | solution.py:473
  112.1 4.4 %shard_map.83 = (f32[24,128]{1,0:T(8,128)S(1)}, f32[128,128]{1,0:T(8,128)S(1)}) custom-call(f32[384,128]{1,0:T(8,128)S(1)} %bitcast.25, f32[8,128]{1,0:T(8,128)S(1)} %get-tuple-element.45.refs_1_.refs_2_, f32[24,128]{1,0:T(8,128)S(1)} %get-tuple-element.46.refs_2_, f32[8,16,9,4,8,128]{5,4,3,2,1,0:T(8,128)S(1)} %get-tuple-element.38.refs_3_, ...), custom_call_target="tpu_custom_call" | custom-call | tf_op jit(solution)/shard_map/pallas_call | solution.py:516
  116.6 13.7 %all_to_all.41 = f32[128,1,128]{2,1,0:T(1,128)S(1)} all-to-all(f32[128,1,128]{2,1,0:T(1,128)S(1)} %bitcast.37), channel_id=1, replica_groups=mesh['cell'=4,'wide_0'=4,'wide_1'=4,'wide_2'=2] {'cell','wide_0','wide_1..., dimensions={0} | all-to-all | bytes 131072 | tf_op jit(solution)/shard_map/all_to_all | solution.py:473
  130.3 0.8 shard_map.84

commit v6 on v5

--- a/solution.py
+++ b/solution.py
@@ -25,7 +25,7 @@
 HALO_AT = 64
 DOT_AT = 88
 FIRST = 3
-BACK = (4, 3, 3)
+BACK = (4, 4, 3)
 FIXED = 56
 BLOCKS = 6
 EDGE_OF = {-1: 3, 0: 4, 1: 5}
@@ -202,6 +202,7 @@
         for k in range(3):
             sent[1] = sent[1] + shifted(blocks[2 + k], EDGES_AT + 2 * EDGE_STEP[k])
         sent.append(blocks[0] + shifted(blocks[1], 64))
+    sent = sent + [jnp.zeros((NDEV, TILE), F32)] * (BACK[step] - len(sent))
     for part in range(BACK[step]):
         out_ref[pl.ds(part, NDEV, stride=BACK[step]), :] = sent[part]
 
@@ -257,7 +258,7 @@
     ]
 
 
-def mobility(moved, rows_ref, pairs_ref, pair_at):
+def mobility(moved, rows_ref, pairs_ref, pair_at, across_ref):
     source_rows(lambda block, part: moved[block][part], rows_ref)
 
     def of_tile(tile, carry):
@@ -275,11 +276,20 @@
             for a in range(3):
                 sums[a].append(terms[a])
         for a in range(3):
-            across = jnp.concatenate(sums[a], axis=0).T
-            pairs_ref[pl.ds(8 * a + tile, 1), :] = jnp.sum(across, axis=0, keepdims=True)
+            across = jnp.concatenate(sums[a], axis=0)
+            if across_ref is None:
+                pairs_ref[pl.ds(8 * a + tile, 1), :] = jnp.sum(across.T, axis=0, keepdims=True)
+            else:
+                across_ref[a, tile] = across
         return carry
 
-    lax.fori_loop(0, TY, of_tile, 0, unroll=4)
+    lax.fori_loop(0, TY, of_tile, 0, unroll=4 if across_ref is None else 4)
+    if across_ref is not None:
+        for a in range(3):
+            for tile in range(TY):
+                pairs_ref[8 * a + tile : 8 * a + tile + 1, :] = jnp.sum(
+                    across_ref[a, tile].T, axis=0, keepdims=True
+                )
     return [pairs_ref[8 * a : 8 * a + 8, :] for a in range(3)]
 
 
@@ -337,6 +347,7 @@
         basis_ref, fresh_ref = take(2)
     moved_ref, out_ref = take(2)
     rows_ref, pairs_ref, onehot, high, low = take(5)
+    across_ref = take(1)[0] if step in DEFERRED else None
     if step == 0:
         (places_ref,) = take(1)
         rows = rows_of(message_ref, 3, back).T
@@ -373,7 +384,7 @@
                 for a in range(3)
             ]
         )
-    pairs = mobility(moved, rows_ref, pairs_ref, pair_at)
+    pairs = mobility(moved, rows_ref, pairs_ref, pair_at, across_ref)
     fresh = [moved[0][a] + FACTOR * pairs[a] for a in range(3)]
     for a in range(3):
         moved_ref[8 * a : 8 * a + 8, :] = moved[0][a]
@@ -410,22 +421,21 @@
     a = [states[1][6:7, :], states[1][4:5, :]]
     b = [states[2][6:7, :], states[2][7:8, :], states[2][4:5, :]]
     c = [spread(sums, 1 + i) for i in range(3)]
-    square = spread(sums, 0) - c[0] * c[0] - c[1] * c[1] - c[2] * c[2]
-    c.append(jnp.sqrt(square))
     inner = lambda p, q: sum([x * y for x, y in zip(p, q)][1:], p[0] * q[0])
     n00, n01, n02 = inner(a, a), inner(a, b), inner(a, c)
-    n11, n12, n22 = inner(b, b), inner(b, c), inner(c, c)
-    l00 = jnp.sqrt(n00)
-    l10, l20 = n01 / l00, n02 / l00
-    l11 = jnp.sqrt(n11 - l10 * l10)
-    l21 = (n12 - l20 * l10) / l11
-    l22 = jnp.sqrt(n22 - l20 * l20 - l21 * l21)
-    t0 = beta * a[0] / l00
-    t1 = (beta * b[0] - l10 * t0) / l11
-    t2 = (beta * c[0] - l20 * t0 - l21 * t1) / l22
-    y2 = t2 / l22
-    y1 = (t1 - l21 * y2) / l11
-    y0 = (t0 - l10 * y1 - l20 * y2) / l00
+    n11, n12 = inner(b, b), inner(b, c)
+    n22 = spread(sums, 0)
+    i00 = lax.rsqrt(n00)
+    l10, l20 = n01 * i00, n02 * i00
+    i11 = lax.rsqrt(n11 - l10 * l10)
+    l21 = (n12 - l20 * l10) * i11
+    i22 = lax.rsqrt(n22 - l20 * l20 - l21 * l21)
+    t0 = beta * a[0] * i00
+    t1 = (beta * b[0] - l10 * t0) * i11
+    t2 = (beta * c[0] - l20 * t0 - l21 * t1) * i22
+    y2 = t2 * i22
+    y1 = (t1 - l21 * y2) * i11
+    y0 = (t0 - l10 * y1 - l20 * y2) * i00
     forces_ref[...] = y0 * moved[0][...] + y1 * moved[1][...] + y2 * moved[2][...]
     for part in range(6):
         half, at = part // 4, (part % 4) * ROWS
@@ -446,6 +456,7 @@
     return jax.ShapeDtypeStruct(shape, jnp.int32)
 
 
+DEFERRED = (0,)
 PAIRS = (TY, TILE // 8, 9, 4, 8, TILE)
 
 
@@ -469,6 +480,8 @@
 
 def exchange(message):
     rows = message.shape[0]
+    if rows != 3 * NDEV:
+        return lax.all_to_all(message, CELL_WIDE, split_axis=0, concat_axis=0, tiled=True)
     moved = message.reshape(NDEV, 1, rows * TILE // NDEV)
     moved = lax.all_to_all(moved, CELL_WIDE, split_axis=0, concat_axis=0, tiled=True)
     return moved.reshape(rows, TILE)
@@ -505,6 +518,8 @@
         if not last:
             outs = [f32(24 * BLOCKS, TILE), f32(24, TILE)] + outs
         scratch = [pltpu.VMEM((96, TILE), F32), pltpu.VMEM((24, TILE), F32)] + sums_scratch()
+        if step in DEFERRED:
+            scratch.append(pltpu.VMEM((3, TY, TILE, TILE), F32))
         if step == 0:
             outs = [
                 pltpu.VMEM(PAIRS, F32),

time: 131 us -> 130 us (level)
  Pallas kernels: 21.7 us -> 19.3 us
    all_to_all x0 -> x5, blocking collectives: none -> 72.9 us  [exchange(): lax.all_to_all(message, CELL_WIDE, split_axis=0, concat_axis=0, tiled=True)]
    all_to_all x7 -> x2, blocking collectives: 109 us -> 36.5 us  [exchange(): lax.all_to_all(moved, CELL_WIDE, split_axis=0, concat_axis=0, tiled=True)]
    pallas_call x3, Pallas kernels: 18.7 us -> 16.4 us  [local(): call(lambda *refs, step=step: local_kernel(step, *refs), tuple(outs), scr...]
where the time goes in v6:
time: 130 us; the launch traced here: 129 us
  blocking collectives  109 us (84%)
  Pallas kernels  19.3 us (15%)
    all_to_all x5, blocking collectives, exchange(): lax.all_to_all(message, CELL_WIDE, split_axis=0, concat_axis=0, tiled=True)  72.9 us
    all_to_all x2, blocking collectives, exchange(): lax.all_to_all(moved, CELL_WIDE, split_axis=0, concat_axis=0, tiled=True)  36.5 us
    pallas_call x3, Pallas kernels, local(): call(lambda *refs, step=step: local_kernel(step, *refs), tuple(outs), scr...  16.4 us

profile of v6, /device:TPU:1, one launch (start us, length us, event | category | flops | bytes accessed | tf_op | source)
XLA Modules:
  0.0 129.4 jit_solution(4099007396439627936)
XLA Ops:
  0.6 1.4 %shard_map.77 = (f32[384,128]{1,0:T(8,128)S(1)}, f32[128,128]{1,0:T(8,128)S(1)}, f32[24,128]{1,0:T(8,128)S(1)}, f32[6,6,32]{2,1,0:T(8,128)S(1)}) custom-call(f32[24,128]{1,0:T(8,128)} %bitcast.38, s32[8,128]{1,0:T(8,128)} %bitcast.41, s32[8,128]{1,0:T(8,128)} %bitcast.42, f32[24,128]{1,0:T(8,128)} %bitcast.39, f32[24,128]{1,0:T(8,128)} %bitcast.40, ...), custom_call_target="tpu_custom_call" | custom-call | tf_op jit(solution)/shard_map/pallas_call | solution.py:497
  2.0 21.8 %all_to_all.65 = f32[128,1,384]{2,1,0:T(1,128)S(1)} all-to-all(f32[128,1,384]{2,1,0:T(1,128)S(1)} %bitcast.33), channel_id=1, replica_groups=mesh['cell'=4,'wide_0'=4,'wide_1'=4,'wide_2'=2] {'cell','wide_0','wide_1..., dimensions={0} | all-to-all | bytes 393216 | tf_op jit(solution)/shard_map/all_to_all | solution.py:486
  23.9 0.3 shard_map.78
  24.1 15.3 %all_to_all.66 = f32[128,4,128]{2,1,0:T(4,128)S(1)} all-to-all(f32[128,4,128]{2,1,0:T(4,128)S(1)} %bitcast.31), channel_id=1, replica_groups=mesh['cell'=4,'wide_0'=4,'wide_1'=4,'wide_2'=2] {'cell','wide_0','wide_1..., dimensions={0} | all-to-all | bytes 524288 | tf_op jit(solution)/shard_map/all_to_all | solution.py:484
  39.5 8.1 %shard_map.79 = (f32[8,16,9,4,8,128]{5,4,3,2,1,0:T(8,128)S(1)}, f32[144,128]{1,0:T(8,128)S(1)}, s32[48,128]{1,0:T(8,128)S(1)}, s32[48,128]{1,0:T(8,128)S(1)}, f3...) custom-call(f32[512,128]{1,0:T(8,128)S(1)} %bitcast.25, ...), custom_call_target="tpu_custom_call" | custom-call | tf_op jit(solution)/shard_map/pallas_call | solution.py:531
  47.6 14.2 %all_to_all.67 = f32[128,2,128]{2,1,0:T(2,128)S(1)} all-to-all(f32[128,2,128]{2,1,0:T(2,128)S(1)} %bitcast.35), channel_id=1, replica_groups=mesh['cell'=4,'wide_0'=4,'wide_1'=4,'wide_2'=2] {'cell','wide_0','wide_1..., dimensions={0} | all-to-all | bytes 262144 | tf_op jit(solution)/shard_map/all_to_all | solution.py:484
  61.9 0.3 shard_map.80
  62.1 15.3 %all_to_all.68 = f32[128,4,128]{2,1,0:T(4,128)S(1)} all-to-all(f32[128,4,128]{2,1,0:T(4,128)S(1)} %bitcast.32), channel_id=1, replica_groups=mesh['cell'=4,'wide_0'=4,'wide_1'=4,'wide_2'=2] {'cell','wide_0','wide_1..., dimensions={0} | all-to-all | bytes 524288 | tf_op jit(solution)/shard_map/all_to_all | solution.py:484
  77.5 4.4 %shard_map.81 = (f32[144,128]{1,0:T(8,128)S(1)}, f32[24,128]{1,0:T(8,128)S(1)}, f32[24,128]{1,0:T(8,128)S(1)}, f32[256,128]{1,0:T(8,128)S(1)}) custom-call(f32[512,128]{1,0:T(8,128)S(1)} %bitcast.24, f32[8,128]{1,0:T(8,128)S(1)} %get-tuple-element.36.refs_1_.refs_3_, f32[24,128]{1,0:T(8,128)S(1)} %get-tuple-element.37.refs_2_, ...), custom_call_target="tpu_custom_call" | custom-call | tf_op jit(solution)/shard_map/pallas_call | solution.py:531
  81.9 14.3 %all_to_all.69 = f32[128,2,128]{2,1,0:T(2,128)S(1)} all-to-all(f32[128,2,128]{2,1,0:T(2,128)S(1)} %bitcast.36), channel_id=1, replica_groups=mesh['cell'=4,'wide_0'=4,'wide_1'=4,'wide_2'=2] {'cell','wide_0','wide_1..., dimensions={0} | all-to-all | bytes 262144 | tf_op jit(solution)/shard_map/all_to_all | solution.py:484
  96.1 0.3 shard_map.82
  96.4 14.7 %all_to_all.70 = f32[128,1,384]{2,1,0:T(1,128)S(1)} all-to-all(f32[128,1,384]{2,1,0:T(1,128)S(1)} %bitcast.34), channel_id=1, replica_groups=mesh['cell'=4,'wide_0'=4,'wide_1'=4,'wide_2'=2] {'cell','wide_0','wide_1..., dimensions={0} | all-to-all | bytes 393216 | tf_op jit(solution)/shard_map/all_to_all | solution.py:486
  111.1 3.8 %shard_map.83 = (f32[24,128]{1,0:T(8,128)S(1)}, f32[128,128]{1,0:T(8,128)S(1)}) custom-call(f32[384,128]{1,0:T(8,128)S(1)} %bitcast.26, f32[8,128]{1,0:T(8,128)S(1)} %get-tuple-element.45.refs_1_.refs_2_, f32[24,128]{1,0:T(8,128)S(1)} %get-tuple-element.46.refs_2_, f32[8,16,9,4,8,128]{5,4,3,2,1,0:T(8,128)S(1)} %get-tuple-element.38.refs_3_, ...), custom_call_target="tpu_custom_call" | custom-call | tf_op jit(solution)/shard_map/pallas_call | solution.py:531
  114.9 13.7 %all_to_all.71 = f32[128,1,128]{2,1,0:T(1,128)S(1)} all-to-all(f32[128,1,128]{2,1,0:T(1,128)S(1)} %bitcast.37), channel_id=1, replica_groups=mesh['cell'=4,'wide_0'=4,'wide_1'=4,'wide_2'=2] {'cell','wide_0','wide_1..., dimensions={0} | all-to-all | bytes 131072 | tf_op jit(solution)/shard_map/all_to_all | solution.py:484
  128.6 0.8 shard_map.84

commit v7 on v6

--- a/solution.py
+++ b/solution.py
@@ -258,8 +258,19 @@
     ]
 
 
-def mobility(moved, rows_ref, pairs_ref, pair_at, across_ref):
+def field_blocks(rows_ref, block_ref):
+    block_ref[...] = jnp.zeros_like(block_ref)
+    for part in range(3):
+        high, low = split2(rows_ref[30 * part : 30 * part + 30, :])
+        for tile in range(30):
+            block_ref[tile, part : part + 1, :] = high[tile : tile + 1]
+            block_ref[tile, 3 + part : 4 + part, :] = low[tile : tile + 1]
+
+
+def mobility(moved, rows_ref, block_ref, near_ref, pairs_ref, pair_at):
     source_rows(lambda block, part: moved[block][part], rows_ref)
+    field_blocks(rows_ref, block_ref)
+    contract = (((1,), (1,)), ((), ()))
 
     def of_tile(tile, carry):
         sources = sources_of(rows_ref, tile)
@@ -268,45 +279,46 @@
         for group in range(TILE // 8):
             terms = None
             for k in range(9):
-                near, *sep = pair(group, k)
+                sep = pair(group, k)
                 force = sources[k]
                 along = sep[0] * force[0] + sep[1] * force[1] + sep[2] * force[2]
-                term = [near * force[a] + along * sep[a] for a in range(3)]
+                term = [along * sep[a] for a in range(3)]
                 terms = term if terms is None else [terms[a] + term[a] for a in range(3)]
             for a in range(3):
                 sums[a].append(terms[a])
+        blocks = [block_ref[10 * (k // 3) + k % 3 + tile].astype(BF16) for k in range(9)]
+        blocks = jnp.concatenate(blocks, axis=1)
+        near = [
+            lax.dot_general(blocks, near_ref[i, tile], contract, preferred_element_type=F32)
+            for i in range(2)
+        ]
+        near = near[0][0:3] + near[0][3:6] + near[1][0:3]
         for a in range(3):
-            across = jnp.concatenate(sums[a], axis=0)
-            if across_ref is None:
-                pairs_ref[pl.ds(8 * a + tile, 1), :] = jnp.sum(across.T, axis=0, keepdims=True)
-            else:
-                across_ref[a, tile] = across
+            across = jnp.concatenate(sums[a], axis=0).T
+            pairs_ref[pl.ds(8 * a + tile, 1), :] = (
+                jnp.sum(across, axis=0, keepdims=True) + near[a : a + 1]
+            )
         return carry
 
-    lax.fori_loop(0, TY, of_tile, 0, unroll=4 if across_ref is None else 4)
-    if across_ref is not None:
-        for a in range(3):
-            for tile in range(TY):
-                pairs_ref[8 * a + tile : 8 * a + tile + 1, :] = jnp.sum(
-                    across_ref[a, tile].T, axis=0, keepdims=True
-                )
+    lax.fori_loop(0, TY, of_tile, 0, unroll=4)
     return [pairs_ref[8 * a : 8 * a + 8, :] for a in range(3)]
 
 
 def stored_pairs(pair_ref):
     def pair_at(tile):
-        return lambda group, k: [pair_ref[tile, group, k, part] for part in range(4)]
+        return lambda group, k: [pair_ref[tile, group, k, part] for part in range(3)]
 
     return pair_at
 
 
-def new_pairs(pair_ref, own_position, rows_ref):
+def new_pairs(pair_ref, near_ref, own_position, rows_ref):
     columns = jnp.concatenate([own_position, jnp.zeros((104, TILE), F32)], axis=0).T
 
     def pair_at(tile):
         turned_columns = pltpu.roll(columns, TILE - tile, 1)
         sources = sources_of(rows_ref, tile)
         targets = {}
+        nears = {}
 
         def pair(group, k):
             if group not in targets:
@@ -321,8 +333,16 @@
             root = lax.rsqrt(soft)
             square = root * root
             scale = square * lax.rsqrt(root)
-            found = [root + EPS2 * (square * root)] + [sep[a] * scale for a in range(3)]
-            for part in range(4):
+            nears[group, k] = root + EPS2 * (square * root)
+            if group % 2 == 1:
+                both = jnp.concatenate([nears[group - 1, k], nears[group, k]], axis=0)
+                high, low = split2(both)
+                place = slice(8 * group - 8, 8 * group + 8)
+                lanes = slice(k * TILE, (k + 1) * TILE)
+                near_ref[0, tile, place, lanes] = high.astype(BF16)
+                near_ref[1, tile, place, lanes] = low.astype(BF16)
+            found = [sep[a] * scale for a in range(3)]
+            for part in range(3):
                 pair_ref[tile, group, k, part] = found[part]
             return found
 
@@ -339,15 +359,14 @@
     if step == 0:
         (pack_ref,) = take(1)
     else:
-        pair_ref, arm_ref, owner_ref, row_ref = take(4)
+        pair_ref, near_ref, arm_ref, owner_ref, row_ref = take(5)
     bases = take(step)
     if step == 0:
-        pair_ref, arm_ref, owner_ref, row_ref = take(4)
+        pair_ref, near_ref, arm_ref, owner_ref, row_ref = take(5)
     if step < ITERS - 1:
         basis_ref, fresh_ref = take(2)
     moved_ref, out_ref = take(2)
-    rows_ref, pairs_ref, onehot, high, low = take(5)
-    across_ref = take(1)[0] if step in DEFERRED else None
+    rows_ref, block_ref, pairs_ref, onehot, high, low = take(6)
     if step == 0:
         (places_ref,) = take(1)
         rows = rows_of(message_ref, 3, back).T
@@ -362,7 +381,7 @@
             owner_ref[8 * block : 8 * block + 8, :] = lax.shift_right_logical(code, 5)
             row_ref[8 * block : 8 * block + 8, :] = code & (ROWS - 1)
         source_rows(lambda block, part: fixed[block][8 * part : 8 * part + 8], places_ref)
-        pair_at = new_pairs(pair_ref, fixed[0][0:24], places_ref)
+        pair_at = new_pairs(pair_ref, near_ref, fixed[0][0:24], places_ref)
     else:
         pair_at = stored_pairs(pair_ref)
     rim = rows_of(message_ref, 2, back).T
@@ -384,7 +403,7 @@
                 for a in range(3)
             ]
         )
-    pairs = mobility(moved, rows_ref, pairs_ref, pair_at, across_ref)
+    pairs = mobility(moved, rows_ref, block_ref, near_ref, pairs_ref, pair_at)
     fresh = [moved[0][a] + FACTOR * pairs[a] for a in range(3)]
     for a in range(3):
         moved_ref[8 * a : 8 * a + 8, :] = moved[0][a]
@@ -456,8 +475,8 @@
     return jax.ShapeDtypeStruct(shape, jnp.int32)
 
 
-DEFERRED = (0,)
-PAIRS = (TY, TILE // 8, 9, 4, 8, TILE)
+PAIRS = (TY, TILE // 8, 9, 3, 8, TILE)
+NEAR = (2, TY, TILE, 9 * TILE)
 
 
 def sums_scratch():
@@ -517,12 +536,15 @@
         outs = [f32(24, TILE), f32(NDEV if last else 2 * NDEV, TILE)]
         if not last:
             outs = [f32(24 * BLOCKS, TILE), f32(24, TILE)] + outs
-        scratch = [pltpu.VMEM((96, TILE), F32), pltpu.VMEM((24, TILE), F32)] + sums_scratch()
-        if step in DEFERRED:
-            scratch.append(pltpu.VMEM((3, TY, TILE, TILE), F32))
+        scratch = [
+            pltpu.VMEM((96, TILE), F32),
+            pltpu.VMEM((30, 16, TILE), F32),
+            pltpu.VMEM((24, TILE), F32),
+        ] + sums_scratch()
         if step == 0:
             outs = [
                 pltpu.VMEM(PAIRS, F32),
+                pltpu.VMEM(NEAR, BF16),
                 f32(24 * BLOCKS, TILE),
                 i32(8 * BLOCKS, TILE),
                 i32(8 * BLOCKS, TILE),
@@ -532,8 +554,8 @@
             lambda *refs, step=step: local_kernel(step, *refs), tuple(outs), scratch
         )(arrived, state, field, *(fixed if step else (pack,)), *bases)
         if step == 0:
-            pairs = pltpu.with_memory_space_constraint(results[0], pltpu.VMEM)
-            fixed = (pairs, *results[1:4])
+            held = [pltpu.with_memory_space_constraint(x, pltpu.VMEM) for x in results[:2]]
+            fixed = (*held, *results[2:5])
         moved, message = results[-2:]
         states.append(state)
         moveds.append(moved)

time: 130 us -> 129 us (level)
  no operation moved by 1% of the time
where the time goes in v7:
time: 129 us
  blocking collectives  109 us (84%)
  Pallas kernels  18.6 us (14%)
    all_to_all x5, blocking collectives, exchange(): lax.all_to_all(message, CELL_WIDE, split_axis=0, concat_axis=0, tiled=True)  72.9 us
    all_to_all x2, blocking collectives, exchange(): lax.all_to_all(moved, CELL_WIDE, split_axis=0, concat_axis=0, tiled=True)  36.5 us
    pallas_call x3, Pallas kernels, local(): call(lambda *refs, step=step: local_kernel(step, *refs), tuple(outs), scr...  15.7 us

profile of v7, /device:TPU:1, one launch (start us, length us, event | category | flops | bytes accessed | tf_op | source)
XLA Modules:
  0.0 128.8 jit_solution(14539147564677735217)
XLA Ops:
  0.6 1.4 %shard_map.77 = (f32[384,128]{1,0:T(8,128)S(1)}, f32[128,128]{1,0:T(8,128)S(1)}, f32[24,128]{1,0:T(8,128)S(1)}, f32[6,6,32]{2,1,0:T(8,128)S(1)}) custom-call(f32[24,128]{1,0:T(8,128)} %bitcast.38, s32[8,128]{1,0:T(8,128)} %bitcast.41, s32[8,128]{1,0:T(8,128)} %bitcast.42, f32[24,128]{1,0:T(8,128)} %bitcast.39, f32[24,128]{1,0:T(8,128)} %bitcast.40, ...), custom_call_target="tpu_custom_call" | custom-call | tf_op jit(solution)/shard_map/pallas_call | solution.py:516
  2.0 21.8 %all_to_all.65 = f32[128,1,384]{2,1,0:T(1,128)S(1)} all-to-all(f32[128,1,384]{2,1,0:T(1,128)S(1)} %bitcast.33), channel_id=1, replica_groups=mesh['cell'=4,'wide_0'=4,'wide_1'=4,'wide_2'=2] {'cell','wide_0','wide_1..., dimensions={0} | all-to-all | bytes 393216 | tf_op jit(solution)/shard_map/all_to_all | solution.py:505
  23.9 0.3 shard_map.78
  24.1 15.3 %all_to_all.66 = f32[128,4,128]{2,1,0:T(4,128)S(1)} all-to-all(f32[128,4,128]{2,1,0:T(4,128)S(1)} %bitcast.31), channel_id=1, replica_groups=mesh['cell'=4,'wide_0'=4,'wide_1'=4,'wide_2'=2] {'cell','wide_0','wide_1..., dimensions={0} | all-to-all | bytes 524288 | tf_op jit(solution)/shard_map/all_to_all | solution.py:503
  39.5 8.8 %shard_map.79 = (f32[8,16,9,3,8,128]{5,4,3,2,1,0:T(8,128)S(1)}, bf16[2,8,128,1152]{3,2,1,0:T(8,128)(2,1)S(1)}, f32[144,128]{1,0:T(8,128)S(1)}, s32[48,128]{1,0:T...) custom-call(f32[512,128]{1,0:T(8,128)S(1)} %bitcast.25, ...), custom_call_target="tpu_custom_call" | custom-call | tf_op jit(solution)/shard_map/pallas_call | solution.py:553
  48.2 14.3 %all_to_all.67 = f32[128,2,128]{2,1,0:T(2,128)S(1)} all-to-all(f32[128,2,128]{2,1,0:T(2,128)S(1)} %bitcast.35), channel_id=1, replica_groups=mesh['cell'=4,'wide_0'=4,'wide_1'=4,'wide_2'=2] {'cell','wide_0','wide_1..., dimensions={0} | all-to-all | bytes 262144 | tf_op jit(solution)/shard_map/all_to_all | solution.py:503
  62.5 0.3 shard_map.80
  62.8 15.3 %all_to_all.68 = f32[128,4,128]{2,1,0:T(4,128)S(1)} all-to-all(f32[128,4,128]{2,1,0:T(4,128)S(1)} %bitcast.32), channel_id=1, replica_groups=mesh['cell'=4,'wide_0'=4,'wide_1'=4,'wide_2'=2] {'cell','wide_0','wide_1..., dimensions={0} | all-to-all | bytes 524288 | tf_op jit(solution)/shard_map/all_to_all | solution.py:503
  78.1 3.7 %shard_map.81 = (f32[144,128]{1,0:T(8,128)S(1)}, f32[24,128]{1,0:T(8,128)S(1)}, f32[24,128]{1,0:T(8,128)S(1)}, f32[256,128]{1,0:T(8,128)S(1)}) custom-call(f32[512,128]{1,0:T(8,128)S(1)} %bitcast.24, f32[8,128]{1,0:T(8,128)S(1)} %get-tuple-element.37.refs_1_.refs_3_, f32[24,128]{1,0:T(8,128)S(1)} %get-tuple-element.38.refs_2_, ...), custom_call_target="tpu_custom_call" | custom-call | tf_op jit(solution)/shard_map/pallas_call | solution.py:553
  81.8 14.3 %all_to_all.69 = f32[128,2,128]{2,1,0:T(2,128)S(1)} all-to-all(f32[128,2,128]{2,1,0:T(2,128)S(1)} %bitcast.36), channel_id=1, replica_groups=mesh['cell'=4,'wide_0'=4,'wide_1'=4,'wide_2'=2] {'cell','wide_0','wide_1..., dimensions={0} | all-to-all | bytes 262144 | tf_op jit(solution)/shard_map/all_to_all | solution.py:503
  96.0 0.3 shard_map.82
  96.3 14.7 %all_to_all.70 = f32[128,1,384]{2,1,0:T(1,128)S(1)} all-to-all(f32[128,1,384]{2,1,0:T(1,128)S(1)} %bitcast.34), channel_id=1, replica_groups=mesh['cell'=4,'wide_0'=4,'wide_1'=4,'wide_2'=2] {'cell','wide_0','wide_1..., dimensions={0} | all-to-all | bytes 393216 | tf_op jit(solution)/shard_map/all_to_all | solution.py:505
  111.0 3.3 %shard_map.83 = (f32[24,128]{1,0:T(8,128)S(1)}, f32[128,128]{1,0:T(8,128)S(1)}) custom-call(f32[384,128]{1,0:T(8,128)S(1)} %bitcast.26, f32[8,128]{1,0:T(8,128)S(1)} %get-tuple-element.47.refs_1_.refs_2_, f32[24,128]{1,0:T(8,128)S(1)} %get-tuple-element.48.refs_2_, f32[8,16,9,3,8,128]{5,4,3,2,1,0:T(8,128)S(1)} %get-tuple-element.39.refs_3_, ...), custom_call_target="tpu_custom_call" | custom-call | tf_op jit(solution)/shard_map/pallas_call | solution.py:553
  114.2 13.7 %all_to_all.71 = f32[128,1,128]{2,1,0:T(1,128)S(1)} all-to-all(f32[128,1,128]{2,1,0:T(1,128)S(1)} %bitcast.37), channel_id=1, replica_groups=mesh['cell'=4,'wide_0'=4,'wide_1'=4,'wide_2'=2] {'cell','wide_0','wide_1..., dimensions={0} | all-to-all | bytes 131072 | tf_op jit(solution)/shard_map/all_to_all | solution.py:503
  128.0 0.8 shard_map.84

commit v8 on v7

--- a/solution.py
+++ b/solution.py
@@ -71,10 +71,9 @@
             high_ref[place, lanes] = jnp.where(mine, high[pick], 0.0).astype(BF16)
             low_ref[place, lanes] = jnp.where(mine, low[pick], 0.0).astype(BF16)
     contract = (((1,), (1,)), ((), ()))
-    onehot = onehot_ref[...]
-    return lax.dot_general(
-        onehot, high_ref[...], contract, preferred_element_type=F32
-    ) + lax.dot_general(onehot, low_ref[...], contract, preferred_element_type=F32)
+    onehot = jnp.concatenate([onehot_ref[...]] * 2, axis=1)
+    values = jnp.concatenate([high_ref[...], low_ref[...]], axis=1)
+    return lax.dot_general(onehot, values, contract, preferred_element_type=F32)
 
 
 def total(x):

time: 129 us -> 129 us (level)
  no operation moved by 1% of the time
where the time goes in v8:
time: 129 us
  blocking collectives  109 us (84%)
  Pallas kernels  18.6 us (14%)
    all_to_all x5, blocking collectives, exchange(): lax.all_to_all(message, CELL_WIDE, split_axis=0, concat_axis=0, tiled=True)  72.9 us
    all_to_all x2, blocking collectives, exchange(): lax.all_to_all(moved, CELL_WIDE, split_axis=0, concat_axis=0, tiled=True)  36.5 us
    pallas_call x3, Pallas kernels, local(): call(lambda *refs, step=step: local_kernel(step, *refs), tuple(outs), scr...  15.7 us

profile of v8, /device:TPU:1, one launch (start us, length us, event | category | flops | bytes accessed | tf_op | source)
XLA Modules:
  0.0 128.8 jit_solution(7842812577449843267)
XLA Ops:
  0.6 1.4 %shard_map.77 = (f32[384,128]{1,0:T(8,128)S(1)}, f32[128,128]{1,0:T(8,128)S(1)}, f32[24,128]{1,0:T(8,128)S(1)}, f32[6,6,32]{2,1,0:T(8,128)S(1)}) custom-call(f32[24,128]{1,0:T(8,128)} %bitcast.38, s32[8,128]{1,0:T(8,128)} %bitcast.41, s32[8,128]{1,0:T(8,128)} %bitcast.42, f32[24,128]{1,0:T(8,128)} %bitcast.39, f32[24,128]{1,0:T(8,128)} %bitcast.40, ...), custom_call_target="tpu_custom_call" | custom-call | tf_op jit(solution)/shard_map/pallas_call | solution.py:515
  2.0 21.8 %all_to_all.65 = f32[128,1,384]{2,1,0:T(1,128)S(1)} all-to-all(f32[128,1,384]{2,1,0:T(1,128)S(1)} %bitcast.33), channel_id=1, replica_groups=mesh['cell'=4,'wide_0'=4,'wide_1'=4,'wide_2'=2] {'cell','wide_0','wide_1..., dimensions={0} | all-to-all | bytes 393216 | tf_op jit(solution)/shard_map/all_to_all | solution.py:504
  23.9 0.3 shard_map.78
  24.1 15.3 %all_to_all.66 = f32[128,4,128]{2,1,0:T(4,128)S(1)} all-to-all(f32[128,4,128]{2,1,0:T(4,128)S(1)} %bitcast.31), channel_id=1, replica_groups=mesh['cell'=4,'wide_0'=4,'wide_1'=4,'wide_2'=2] {'cell','wide_0','wide_1..., dimensions={0} | all-to-all | bytes 524288 | tf_op jit(solution)/shard_map/all_to_all | solution.py:502
  39.5 8.8 %shard_map.79 = (f32[8,16,9,3,8,128]{5,4,3,2,1,0:T(8,128)S(1)}, bf16[2,8,128,1152]{3,2,1,0:T(8,128)(2,1)S(1)}, f32[144,128]{1,0:T(8,128)S(1)}, s32[48,128]{1,0:T...) custom-call(f32[512,128]{1,0:T(8,128)S(1)} %bitcast.25, ...), custom_call_target="tpu_custom_call" | custom-call | tf_op jit(solution)/shard_map/pallas_call | solution.py:552
  48.2 14.3 %all_to_all.67 = f32[128,2,128]{2,1,0:T(2,128)S(1)} all-to-all(f32[128,2,128]{2,1,0:T(2,128)S(1)} %bitcast.35), channel_id=1, replica_groups=mesh['cell'=4,'wide_0'=4,'wide_1'=4,'wide_2'=2] {'cell','wide_0','wide_1..., dimensions={0} | all-to-all | bytes 262144 | tf_op jit(solution)/shard_map/all_to_all | solution.py:502
  62.5 0.3 shard_map.80
  62.8 15.3 %all_to_all.68 = f32[128,4,128]{2,1,0:T(4,128)S(1)} all-to-all(f32[128,4,128]{2,1,0:T(4,128)S(1)} %bitcast.32), channel_id=1, replica_groups=mesh['cell'=4,'wide_0'=4,'wide_1'=4,'wide_2'=2] {'cell','wide_0','wide_1..., dimensions={0} | all-to-all | bytes 524288 | tf_op jit(solution)/shard_map/all_to_all | solution.py:502
  78.1 3.7 %shard_map.81 = (f32[144,128]{1,0:T(8,128)S(1)}, f32[24,128]{1,0:T(8,128)S(1)}, f32[24,128]{1,0:T(8,128)S(1)}, f32[256,128]{1,0:T(8,128)S(1)}) custom-call(f32[512,128]{1,0:T(8,128)S(1)} %bitcast.24, f32[8,128]{1,0:T(8,128)S(1)} %get-tuple-element.37.refs_1_.refs_3_, f32[24,128]{1,0:T(8,128)S(1)} %get-tuple-element.38.refs_2_, ...), custom_call_target="tpu_custom_call" | custom-call | tf_op jit(solution)/shard_map/pallas_call | solution.py:552
  81.8 14.2 %all_to_all.69 = f32[128,2,128]{2,1,0:T(2,128)S(1)} all-to-all(f32[128,2,128]{2,1,0:T(2,128)S(1)} %bitcast.36), channel_id=1, replica_groups=mesh['cell'=4,'wide_0'=4,'wide_1'=4,'wide_2'=2] {'cell','wide_0','wide_1..., dimensions={0} | all-to-all | bytes 262144 | tf_op jit(solution)/shard_map/all_to_all | solution.py:502
  96.0 0.3 shard_map.82
  96.3 14.7 %all_to_all.70 = f32[128,1,384]{2,1,0:T(1,128)S(1)} all-to-all(f32[128,1,384]{2,1,0:T(1,128)S(1)} %bitcast.34), channel_id=1, replica_groups=mesh['cell'=4,'wide_0'=4,'wide_1'=4,'wide_2'=2] {'cell','wide_0','wide_1..., dimensions={0} | all-to-all | bytes 393216 | tf_op jit(solution)/shard_map/all_to_all | solution.py:504
  111.0 3.3 %shard_map.83 = (f32[24,128]{1,0:T(8,128)S(1)}, f32[128,128]{1,0:T(8,128)S(1)}) custom-call(f32[384,128]{1,0:T(8,128)S(1)} %bitcast.26, f32[8,128]{1,0:T(8,128)S(1)} %get-tuple-element.47.refs_1_.refs_2_, f32[24,128]{1,0:T(8,128)S(1)} %get-tuple-element.48.refs_2_, f32[8,16,9,3,8,128]{5,4,3,2,1,0:T(8,128)S(1)} %get-tuple-element.39.refs_3_, ...), custom_call_target="tpu_custom_call" | custom-call | tf_op jit(solution)/shard_map/pallas_call | solution.py:552
  114.2 13.7 %all_to_all.71 = f32[128,1,128]{2,1,0:T(1,128)S(1)} all-to-all(f32[128,1,128]{2,1,0:T(1,128)S(1)} %bitcast.37), channel_id=1, replica_groups=mesh['cell'=4,'wide_0'=4,'wide_1'=4,'wide_2'=2] {'cell','wide_0','wide_1..., dimensions={0} | all-to-all | bytes 131072 | tf_op jit(solution)/shard_map/all_to_all | solution.py:502
  128.0 0.8 shard_map.84

commit v9 on v7

--- a/solution.py
+++ b/solution.py
@@ -267,7 +267,7 @@
             block_ref[tile, 3 + part : 4 + part, :] = low[tile : tile + 1]
 
 
-def mobility(moved, rows_ref, block_ref, near_ref, pairs_ref, pair_at):
+def mobility(moved, rows_ref, block_ref, near_ref, pairs_ref, pair_at, across_ref):
     source_rows(lambda block, part: moved[block][part], rows_ref)
     field_blocks(rows_ref, block_ref)
     contract = (((1,), (1,)), ((), ()))
@@ -294,13 +294,22 @@
         ]
         near = near[0][0:3] + near[0][3:6] + near[1][0:3]
         for a in range(3):
-            across = jnp.concatenate(sums[a], axis=0).T
-            pairs_ref[pl.ds(8 * a + tile, 1), :] = (
-                jnp.sum(across, axis=0, keepdims=True) + near[a : a + 1]
-            )
+            across = jnp.concatenate(sums[a], axis=0)
+            found = near[a : a + 1]
+            if across_ref is None:
+                found = found + jnp.sum(across.T, axis=0, keepdims=True)
+            else:
+                across_ref[a, tile] = across
+            pairs_ref[pl.ds(8 * a + tile, 1), :] = found
         return carry
 
     lax.fori_loop(0, TY, of_tile, 0, unroll=4)
+    if across_ref is not None:
+        for a in range(3):
+            for tile in range(TY):
+                place = slice(8 * a + tile, 8 * a + tile + 1)
+                across = jnp.sum(across_ref[a, tile].T, axis=0, keepdims=True)
+                pairs_ref[place, :] = pairs_ref[place, :] + across
     return [pairs_ref[8 * a : 8 * a + 8, :] for a in range(3)]
 
 
@@ -367,6 +376,7 @@
         basis_ref, fresh_ref = take(2)
     moved_ref, out_ref = take(2)
     rows_ref, block_ref, pairs_ref, onehot, high, low = take(6)
+    across_ref = take(1)[0] if step in DEFERRED else None
     if step == 0:
         (places_ref,) = take(1)
         rows = rows_of(message_ref, 3, back).T
@@ -403,7 +413,7 @@
                 for a in range(3)
             ]
         )
-    pairs = mobility(moved, rows_ref, block_ref, near_ref, pairs_ref, pair_at)
+    pairs = mobility(moved, rows_ref, block_ref, near_ref, pairs_ref, pair_at, across_ref)
     fresh = [moved[0][a] + FACTOR * pairs[a] for a in range(3)]
     for a in range(3):
         moved_ref[8 * a : 8 * a + 8, :] = moved[0][a]
@@ -475,6 +485,7 @@
     return jax.ShapeDtypeStruct(shape, jnp.int32)
 
 
+DEFERRED = (0,)
 PAIRS = (TY, TILE // 8, 9, 3, 8, TILE)
 NEAR = (2, TY, TILE, 9 * TILE)
 
@@ -541,6 +552,8 @@
             pltpu.VMEM((30, 16, TILE), F32),
             pltpu.VMEM((24, TILE), F32),
         ] + sums_scratch()
+        if step in DEFERRED:
+            scratch.append(pltpu.VMEM((3, TY, TILE, TILE), F32))
         if step == 0:
             outs = [
                 pltpu.VMEM(PAIRS, F32),

time: 129 us -> 129 us (level)
  no operation moved by 1% of the time
where the time goes in v9:
time: 129 us
  blocking collectives  109 us (84%)
  Pallas kernels  18.6 us (14%)
    all_to_all x5, blocking collectives, exchange(): lax.all_to_all(message, CELL_WIDE, split_axis=0, concat_axis=0, tiled=True)  72.9 us
    all_to_all x2, blocking collectives, exchange(): lax.all_to_all(moved, CELL_WIDE, split_axis=0, concat_axis=0, tiled=True)  36.5 us
    pallas_call x3, Pallas kernels, local(): call(lambda *refs, step=step: local_kernel(step, *refs), tuple(outs), scr...  15.6 us

profile of v9, /device:TPU:1, one launch (start us, length us, event | category | flops | bytes accessed | tf_op | source)
XLA Modules:
  0.0 128.7 jit_solution(7886197456516658460)
XLA Ops:
  0.6 1.4 %shard_map.77 = (f32[384,128]{1,0:T(8,128)S(1)}, f32[128,128]{1,0:T(8,128)S(1)}, f32[24,128]{1,0:T(8,128)S(1)}, f32[6,6,32]{2,1,0:T(8,128)S(1)}) custom-call(f32[24,128]{1,0:T(8,128)} %bitcast.38, s32[8,128]{1,0:T(8,128)} %bitcast.41, s32[8,128]{1,0:T(8,128)} %bitcast.42, f32[24,128]{1,0:T(8,128)} %bitcast.39, f32[24,128]{1,0:T(8,128)} %bitcast.40, ...), custom_call_target="tpu_custom_call" | custom-call | tf_op jit(solution)/shard_map/pallas_call | solution.py:527
  2.0 21.8 %all_to_all.65 = f32[128,1,384]{2,1,0:T(1,128)S(1)} all-to-all(f32[128,1,384]{2,1,0:T(1,128)S(1)} %bitcast.33), channel_id=1, replica_groups=mesh['cell'=4,'wide_0'=4,'wide_1'=4,'wide_2'=2] {'cell','wide_0','wide_1..., dimensions={0} | all-to-all | bytes 393216 | tf_op jit(solution)/shard_map/all_to_all | solution.py:516
  23.9 0.3 shard_map.78
  24.1 15.3 %all_to_all.66 = f32[128,4,128]{2,1,0:T(4,128)S(1)} all-to-all(f32[128,4,128]{2,1,0:T(4,128)S(1)} %bitcast.31), channel_id=1, replica_groups=mesh['cell'=4,'wide_0'=4,'wide_1'=4,'wide_2'=2] {'cell','wide_0','wide_1..., dimensions={0} | all-to-all | bytes 524288 | tf_op jit(solution)/shard_map/all_to_all | solution.py:514
  39.5 8.7 %shard_map.79 = (f32[8,16,9,3,8,128]{5,4,3,2,1,0:T(8,128)S(1)}, bf16[2,8,128,1152]{3,2,1,0:T(8,128)(2,1)S(1)}, f32[144,128]{1,0:T(8,128)S(1)}, s32[48,128]{1,0:T...) custom-call(f32[512,128]{1,0:T(8,128)S(1)} %bitcast.25, ...), custom_call_target="tpu_custom_call" | custom-call | tf_op jit(solution)/shard_map/pallas_call | solution.py:566
  48.2 14.3 %all_to_all.67 = f32[128,2,128]{2,1,0:T(2,128)S(1)} all-to-all(f32[128,2,128]{2,1,0:T(2,128)S(1)} %bitcast.35), channel_id=1, replica_groups=mesh['cell'=4,'wide_0'=4,'wide_1'=4,'wide_2'=2] {'cell','wide_0','wide_1..., dimensions={0} | all-to-all | bytes 262144 | tf_op jit(solution)/shard_map/all_to_all | solution.py:514
  62.4 0.3 shard_map.80
  62.7 15.3 %all_to_all.68 = f32[128,4,128]{2,1,0:T(4,128)S(1)} all-to-all(f32[128,4,128]{2,1,0:T(4,128)S(1)} %bitcast.32), channel_id=1, replica_groups=mesh['cell'=4,'wide_0'=4,'wide_1'=4,'wide_2'=2] {'cell','wide_0','wide_1..., dimensions={0} | all-to-all | bytes 524288 | tf_op jit(solution)/shard_map/all_to_all | solution.py:514
  78.0 3.7 %shard_map.81 = (f32[144,128]{1,0:T(8,128)S(1)}, f32[24,128]{1,0:T(8,128)S(1)}, f32[24,128]{1,0:T(8,128)S(1)}, f32[256,128]{1,0:T(8,128)S(1)}) custom-call(f32[512,128]{1,0:T(8,128)S(1)} %bitcast.24, f32[8,128]{1,0:T(8,128)S(1)} %get-tuple-element.37.refs_1_.refs_3_, f32[24,128]{1,0:T(8,128)S(1)} %get-tuple-element.38.refs_2_, ...), custom_call_target="tpu_custom_call" | custom-call | tf_op jit(solution)/shard_map/pallas_call | solution.py:566
  81.7 14.3 %all_to_all.69 = f32[128,2,128]{2,1,0:T(2,128)S(1)} all-to-all(f32[128,2,128]{2,1,0:T(2,128)S(1)} %bitcast.36), channel_id=1, replica_groups=mesh['cell'=4,'wide_0'=4,'wide_1'=4,'wide_2'=2] {'cell','wide_0','wide_1..., dimensions={0} | all-to-all | bytes 262144 | tf_op jit(solution)/shard_map/all_to_all | solution.py:514
  95.9 0.3 shard_map.82
  96.2 14.7 %all_to_all.70 = f32[128,1,384]{2,1,0:T(1,128)S(1)} all-to-all(f32[128,1,384]{2,1,0:T(1,128)S(1)} %bitcast.34), channel_id=1, replica_groups=mesh['cell'=4,'wide_0'=4,'wide_1'=4,'wide_2'=2] {'cell','wide_0','wide_1..., dimensions={0} | all-to-all | bytes 393216 | tf_op jit(solution)/shard_map/all_to_all | solution.py:516
  110.9 3.3 %shard_map.83 = (f32[24,128]{1,0:T(8,128)S(1)}, f32[128,128]{1,0:T(8,128)S(1)}) custom-call(f32[384,128]{1,0:T(8,128)S(1)} %bitcast.26, f32[8,128]{1,0:T(8,128)S(1)} %get-tuple-element.47.refs_1_.refs_2_, f32[24,128]{1,0:T(8,128)S(1)} %get-tuple-element.48.refs_2_, f32[8,16,9,3,8,128]{5,4,3,2,1,0:T(8,128)S(1)} %get-tuple-element.39.refs_3_, ...), custom_call_target="tpu_custom_call" | custom-call | tf_op jit(solution)/shard_map/pallas_call | solution.py:566
  114.2 13.7 %all_to_all.71 = f32[128,1,128]{2,1,0:T(1,128)S(1)} all-to-all(f32[128,1,128]{2,1,0:T(1,128)S(1)} %bitcast.37), channel_id=1, replica_groups=mesh['cell'=4,'wide_0'=4,'wide_1'=4,'wide_2'=2] {'cell','wide_0','wide_1..., dimensions={0} | all-to-all | bytes 131072 | tf_op jit(solution)/shard_map/all_to_all | solution.py:514
  127.9 0.8 shard_map.84
